TPU v7x, 32 devices: a whole 2x2x4 slice. The times are simulated.
32 devices in a mesh: fsdp: 8 (over y, x, core), sp: 4 (over z).
Axes of the slice: x: 2, y: 2, z: 4, core: 2. Of those that a mesh axis runs over, the one named last changes fastest.
Arguments:
- hidden_in: bfloat16 [8, 1024, 2048], P('fsdp', 'sp'), may hold values from -6 to 6
- segments: int32 [8, 1024], P('fsdp'), may hold values from 0 to 3, never falling along the last dimension, each value on 1 to 640 neighbouring positions
- ln1_gain: float32 [2048], replicated, may hold values from 0.5 to 1.5
- ln1_bias: float32 [2048], replicated, may hold values from -1 to 1
- ln2_gain: float32 [2048], replicated, may hold values from 0.5 to 1.5
- ln2_bias: float32 [2048], replicated, may hold values from -1 to 1
- w_qkv: bfloat16 [6144, 2048], P('fsdp'), may hold values from -0.125 to 0.125
- b_qkv: float32 [6144], replicated, may hold values from -1 to 1
- w_dense: bfloat16 [2048, 2048], P('fsdp'), may hold values from -0.75 to 0.75
- b_dense: float32 [2048], replicated, may hold values from -1 to 1
- w_up: bfloat16 [8192, 2048], P('fsdp'), may hold values from -0.125 to 0.125
- b_up: float32 [8192], replicated, may hold values from -1 to 1
- w_down: bfloat16 [8192, 2048], P('fsdp'), may hold values from -0.0625 to 0.0625
- b_down: float32 [2048], replicated, may hold values from -1 to 1
- cotangent: bfloat16 [8, 1024, 2048], P('fsdp', 'sp'), may hold values from -6 to 6
Outputs:
- output: bfloat16 [8, 1024, 2048], P('fsdp', 'sp')
- input_grad: bfloat16 [8, 1024, 2048], P('fsdp', 'sp')
- grad_ln1_gain: float32 [2048], P('fsdp')
- grad_ln1_bias: float32 [2048], P('fsdp')
- grad_ln2_gain: float32 [2048], P('fsdp')
- grad_ln2_bias: float32 [2048], P('fsdp')
- grad_w_qkv: float32 [6144, 2048], P('fsdp')
- grad_b_qkv: float32 [6144], P('fsdp')
- grad_w_dense: float32 [2048, 2048], P('fsdp')
- grad_b_dense: float32 [2048], P('fsdp')
- grad_w_up: float32 [8192, 2048], P('fsdp')
- grad_b_up: float32 [8192], P('fsdp')
- grad_w_down: float32 [8192, 2048], P('fsdp')
- grad_b_down: float32 [2048], P('fsdp')
Inputs may be any that keep to these rules, and one draw needn't show every extreme that they name: `segments`: along each sequence the segment numbers never fall; each document is one run of 1 to 640 positions, and some document has exactly 640.
All inputs are finite; a program needn't handle non-finite values.
Results may differ from a plain program's by a relative error of at most 0.011.
Values may be sent and summed in bfloat16 or wider, within the bound.
A program may use at most 704 MiB of HBM per device.

v0:
```python
import math

import jax
import jax.numpy as jnp
from jax import lax
from jax.sharding import PartitionSpec as P

HEADS = 8
HEAD_DIM = 256
ROT = 64


EPSILON = 1e-05
NEGATIVE = -1e30
ROOT_HALF = 0.7071067811865476
ROOT_TWO_PI = 2.5066282746310002


def contract_rows(former, latter):
    return lax.dot_general(
        former, latter, (((0,), (0,)), ((), ())), preferred_element_type=jnp.float32
    )


def times_transposed(former, latter):
    return lax.dot_general(
        former, latter, (((1,), (1,)), ((), ())), preferred_element_type=jnp.float32
    )


def norm_forward(inputs, norm_gain, norm_shift):
    average = jnp.mean(inputs, axis=-1, keepdims=True)
    centred = inputs - average
    variance = jnp.mean(centred * centred, axis=-1, keepdims=True)
    inverse = lax.rsqrt(variance + EPSILON)
    scaled = centred * inverse
    return (scaled * norm_gain + norm_shift, scaled, inverse)


def norm_backward(upstream, scaled, inverse, norm_gain):
    weighted = upstream * norm_gain
    first_mean = jnp.mean(weighted, axis=-1, keepdims=True)
    second_mean = jnp.mean(weighted * scaled, axis=-1, keepdims=True)
    input_part = inverse * (weighted - first_mean - scaled * second_mean)
    return (input_part, jnp.sum(upstream * scaled, axis=0), jnp.sum(upstream, axis=0))


def gelu_pair(hidden):
    cumulative = 0.5 * (1.0 + jax.scipy.special.erf(hidden * ROOT_HALF))
    return (
        hidden * cumulative,
        cumulative + hidden * jnp.exp(-0.5 * hidden * hidden) / ROOT_TWO_PI,
    )


def rotary_tables(segment_rows):
    length = segment_rows.shape[-1]
    places = jnp.arange(length, dtype=jnp.int32)
    changes = jnp.concatenate(
        [
            jnp.ones_like(segment_rows[..., :1]),
            (segment_rows[..., 1:] != segment_rows[..., :-1]).astype(jnp.int32),
        ],
        axis=-1,
    )
    first_place = lax.cummax(changes * places, axis=segment_rows.ndim - 1)
    position = (places - first_place).astype(jnp.float32)
    exponent = jnp.arange(0, ROT, 2).astype(jnp.float32) / ROT
    frequency = 1.0 / jnp.power(10000.0, exponent)
    angles = position[..., None] * frequency
    angles = jnp.concatenate([angles, angles], axis=-1)
    return (jnp.cos(angles), jnp.sin(angles))


def rotate(heads_part, cos_table, sin_table):
    half_rot = ROT // 2
    turned = heads_part[..., :ROT]
    swapped = jnp.concatenate([-turned[..., half_rot:], turned[..., :half_rot]], axis=-1)
    turned = turned * cos_table[..., None, :] + swapped * sin_table[..., None, :]
    return jnp.concatenate([turned, heads_part[..., ROT:]], axis=-1)


def unrotate(grads_part, cos_table, sin_table):
    half_rot = ROT // 2
    turned = grads_part[..., :ROT]
    along_sin = turned * sin_table[..., None, :]
    back_turn = jnp.concatenate([along_sin[..., half_rot:], -along_sin[..., :half_rot]], axis=-1)
    turned = turned * cos_table[..., None, :] + back_turn
    return jnp.concatenate([turned, grads_part[..., ROT:]], axis=-1)


def build_mask(segment_row):
    places = jnp.arange(segment_row.shape[0], dtype=jnp.int32)
    return (segment_row[:, None] == segment_row[None, :]) & (places[None, :] <= places[:, None])


def attend_forward(scanned):
    queries, keys_rot, values, segment_row = scanned
    scores = jnp.einsum("qhd,khd->hqk", queries, keys_rot, preferred_element_type=jnp.float32) * (
        1.0 / math.sqrt(HEAD_DIM)
    )
    scores = jnp.where(build_mask(segment_row)[None], scores, NEGATIVE)
    row_top = jnp.max(scores, axis=-1, keepdims=True)
    exponent = jnp.exp(scores - row_top)
    row_total = jnp.sum(exponent, axis=-1, keepdims=True)
    attention = (exponent / row_total).astype(jnp.bfloat16)
    context = jnp.einsum("hqk,khd->qhd", attention, values, preferred_element_type=jnp.float32)
    return (context.astype(jnp.bfloat16), row_top + jnp.log(row_total))


def attend_backward(scanned):
    queries, keys_rot, values, segment_row, log_total, context_grad = scanned
    scale_factor = 1.0 / math.sqrt(HEAD_DIM)
    scores = (
        jnp.einsum("qhd,khd->hqk", queries, keys_rot, preferred_element_type=jnp.float32)
        * scale_factor
    )
    attention = jnp.where(build_mask(segment_row)[None], jnp.exp(scores - log_total), 0.0)
    value_grad = jnp.einsum(
        "hqk,qhd->khd",
        attention.astype(jnp.bfloat16),
        context_grad,
        preferred_element_type=jnp.float32,
    )
    attention_grad = jnp.einsum(
        "qhd,khd->hqk", context_grad, values, preferred_element_type=jnp.float32
    )
    row_centre = jnp.sum(attention * attention_grad, axis=-1, keepdims=True)
    score_grad = (attention * (attention_grad - row_centre)).astype(jnp.bfloat16)
    query_grad = (
        jnp.einsum("hqk,khd->qhd", score_grad, keys_rot, preferred_element_type=jnp.float32)
        * scale_factor
    )
    key_grad = (
        jnp.einsum("hqk,qhd->khd", score_grad, queries, preferred_element_type=jnp.float32)
        * scale_factor
    )
    return (query_grad, key_grad, value_grad)


def per_device(
    hidden_in,
    segments,
    ln1_gain,
    ln1_bias,
    ln2_gain,
    ln2_bias,
    w_qkv,
    b_qkv,
    w_dense,
    b_dense,
    w_up,
    b_up,
    w_down,
    b_down,
    cotangent,
):
    seq_count, shard_len, width = hidden_in.shape
    tok_rows = seq_count * shard_len
    inputs = hidden_in.reshape(tok_rows, width).astype(jnp.float32)
    upstream = cotangent.reshape(tok_rows, width)
    upstream_f32 = upstream.astype(jnp.float32)
    full_qkv, full_dense = (
        lax.all_gather(w_qkv, "fsdp", axis=0, tiled=True),
        lax.all_gather(w_dense, "fsdp", axis=0, tiled=True),
    )
    normed, scaled_attn, inverse_attn = norm_forward(inputs, ln1_gain, ln1_bias)
    normed = normed.astype(jnp.bfloat16)
    packed = (times_transposed(normed, full_qkv) + b_qkv).astype(jnp.bfloat16)
    packed = packed.reshape(seq_count, shard_len, HEADS, 3 * HEAD_DIM)
    by_head = lax.all_to_all(packed, "sp", split_axis=2, concat_axis=1, tiled=True)
    cos_table, sin_table = rotary_tables(segments)
    queries = rotate(by_head[..., :HEAD_DIM].astype(jnp.float32), cos_table, sin_table).astype(
        jnp.bfloat16
    )
    keys_rot = rotate(
        by_head[..., HEAD_DIM : 2 * HEAD_DIM].astype(jnp.float32), cos_table, sin_table
    ).astype(jnp.bfloat16)
    values = by_head[..., 2 * HEAD_DIM :]
    context, log_total = lax.map(attend_forward, (queries, keys_rot, values, segments))
    merged = lax.all_to_all(context, "sp", split_axis=1, concat_axis=2, tiled=True).reshape(
        tok_rows, width
    )
    attended = times_transposed(merged, full_dense) + b_dense
    normed_mlp, scaled_mlp, inverse_mlp = norm_forward(inputs, ln2_gain, ln2_bias)
    normed_mlp = normed_mlp.astype(jnp.bfloat16)
    full_up, full_down = (
        lax.all_gather(w_up, "fsdp", axis=0, tiled=True),
        lax.all_gather(w_down, "fsdp", axis=0, tiled=True),
    )
    hidden = times_transposed(normed_mlp, full_up) + b_up
    activated, slope = gelu_pair(hidden)
    activated = activated.astype(jnp.bfloat16)
    mlp_out = jnp.dot(activated, full_down, preferred_element_type=jnp.float32) + b_down
    hidden_grad = (times_transposed(upstream, full_down) * slope).astype(jnp.bfloat16)
    mlp_in_grad = jnp.dot(hidden_grad, full_up, preferred_element_type=jnp.float32)
    grad_cols = hidden_grad
    mlp_shard = lax.psum_scatter(
        jnp.concatenate(
            [contract_rows(grad_cols, normed_mlp), contract_rows(activated, upstream)], axis=1
        ),
        "fsdp",
        scatter_dimension=0,
        tiled=True,
    )
    up_grad = mlp_shard[:, :width]
    down_grad = mlp_shard[:, width:]
    bias_up = jnp.sum(hidden_grad.astype(jnp.float32), axis=0)
    output = (inputs + attended + mlp_out).astype(jnp.bfloat16).reshape(seq_count, shard_len, width)
    dense_in_grad = jnp.dot(upstream, full_dense, preferred_element_type=jnp.float32).astype(
        jnp.bfloat16
    )
    context_grad = lax.all_to_all(
        dense_in_grad.reshape(seq_count, shard_len, HEADS, HEAD_DIM),
        "sp",
        split_axis=2,
        concat_axis=1,
        tiled=True,
    )
    query_grad, key_grad, value_grad = lax.map(
        attend_backward, (queries, keys_rot, values, segments, log_total, context_grad)
    )
    packed_grad = jnp.concatenate(
        [
            unrotate(query_grad, cos_table, sin_table),
            unrotate(key_grad, cos_table, sin_table),
            value_grad,
        ],
        axis=-1,
    ).astype(jnp.bfloat16)
    packed_grad = lax.all_to_all(
        packed_grad, "sp", split_axis=1, concat_axis=2, tiled=True
    ).reshape(tok_rows, 3 * width)
    normed_grad = jnp.dot(packed_grad, full_qkv, preferred_element_type=jnp.float32)
    qkv_part = w_qkv.shape[0]
    dense_part = w_dense.shape[0]
    block_size = qkv_part + dense_part
    block_total = lax.axis_size("fsdp") * block_size // block_size
    grad_cols = packed_grad
    qkv_term = contract_rows(grad_cols, normed).reshape(block_total, qkv_part, width)
    dense_term = contract_rows(upstream, merged).reshape(block_total, dense_part, width)
    attn_shard = lax.psum_scatter(
        jnp.concatenate([qkv_term, dense_term], axis=1).reshape(
            lax.axis_size("fsdp") * block_size, width
        ),
        "fsdp",
        scatter_dimension=0,
        tiled=True,
    )
    qkv_local = attn_shard[:qkv_part]
    dense_local = attn_shard[qkv_part:]
    grad_qkv_w, grad_dense_w, grad_up_w, grad_down_w = lax.psum(
        (qkv_local, dense_local, up_grad, down_grad), "sp"
    )
    attn_input, gain_one, shift_one = norm_backward(
        normed_grad, scaled_attn, inverse_attn, ln1_gain
    )
    mlp_input, gain_two, shift_two = norm_backward(mlp_in_grad, scaled_mlp, inverse_mlp, ln2_gain)
    input_grad = (
        (upstream_f32 + attn_input + mlp_input)
        .astype(jnp.bfloat16)
        .reshape(seq_count, shard_len, width)
    )
    bias_out = jnp.sum(upstream_f32, axis=0)
    bias_qkv = jnp.sum(packed_grad.astype(jnp.float32), axis=0)
    summed = lax.psum(
        (gain_one, shift_one, gain_two, shift_two, bias_qkv, bias_out, bias_up), ("fsdp", "sp")
    )
    fsdp_index = lax.axis_index("fsdp")
    fsdp_count = lax.axis_size("fsdp")

    def own_part(vector):
        piece_len = vector.shape[0] // fsdp_count
        return lax.dynamic_slice_in_dim(vector, fsdp_index * piece_len, piece_len, 0)

    bias_out_part = own_part(summed[5])
    return (
        output,
        input_grad,
        own_part(summed[0]),
        own_part(summed[1]),
        own_part(summed[2]),
        own_part(summed[3]),
        grad_qkv_w,
        own_part(summed[4]),
        grad_dense_w,
        bias_out_part,
        grad_up_w,
        own_part(summed[6]),
        grad_down_w,
        bias_out_part,
    )


def solution(mesh):
    return jax.shard_map(
        per_device,
        mesh=mesh,
        in_specs=(
            P("fsdp", "sp", None),
            P("fsdp", None),
            P(),
            P(),
            P(),
            P(),
            P("fsdp", None),
            P(),
            P("fsdp", None),
            P(),
            P("fsdp", None),
            P(),
            P("fsdp", None),
            P(),
            P("fsdp", "sp", None),
        ),
        out_specs=(
            P("fsdp", "sp", None),
            P("fsdp", "sp", None),
            P("fsdp"),
            P("fsdp"),
            P("fsdp"),
            P("fsdp"),
            P("fsdp", None),
            P("fsdp"),
            P("fsdp", None),
            P("fsdp"),
            P("fsdp", None),
            P("fsdp"),
            P("fsdp", None),
            P("fsdp"),
        ),
        check_vma=False,
    )
```

profile of v0, /device:TPU:0, one launch (start us, length us, event | category | flops | bytes accessed | tf_op | source)
XLA Modules:
  0.0 2658.8 jit_solution(7697553967098281096)
XLA Ops:
  10.7 56.3 %all-gather.7.cloned.1.call-done = bf16[2048,2048]{1,0:T(8,128)(2,1)} async-done(((bf16[256,2048]{1,0:T(8,128)(2,1)}), bf16[2048,2048]{1,0:T(8,128)(2,1)}) %all-gather.7.cloned.1.call-update) | async-done | bytes 8388624 | tf_op jit(solution)/shard_map/all_gather | solution.py:165
  67.0 5.7 convolution_convert_fusion
  78.9 115.4 %all-gather.5.cloned.1.call-done = bf16[6144,2048]{1,0:T(8,128)(2,1)} async-done(((bf16[768,2048]{1,0:T(8,128)(2,1)}), bf16[6144,2048]{1,0:T(8,128)(2,1)}) %all-gather.5.cloned.1.call-update) | async-done | bytes 25165840 | tf_op jit(solution)/shard_map/all_gather | solution.py:164
  194.3 12.9 fusion.5
  213.7 4.8 all-to-all-start
  226.3 63.2 %all-to-all-done = bf16[1,256,8,768]{3,1,0,2:T(8,128)(2,1)S(1)} async-done(((bf16[1,256,8,768]{3,1,0,2:T(8,128)(2,1)}), bf16[1,256,8,768]{3,1,0,2:T(8,128)(2,1)S(1)}, u32[]{:S(2)}, u32[]{:S(2)}) %all-to-all-start) | async-done | bytes 3145760 | tf_op jit(solution)/shard_map/all_to_all | solution.py:171
  315.7 5.8 multiply_reduce_fusion
  351.5 7.1 fusion.57
  358.6 8.8 copy.162
  367.3 5.7 all-to-all-start.3
  375.5 8.1 fusion.73
  383.7 58.6 %all-to-all-done.3 = bf16[1,1024,2,768]{3,2,0,1:T(2,128)(2,1)} async-done(((bf16[1,1024,2,768]{3,2,0,1:T(2,128)(2,1)}), bf16[1,1024,2,768]{3,2,0,1:T(2,128)(2,1)}, u32[]{:S(2)}, u32[]{:S(2)}) %all-to-all-start.3) | async-done | bytes 3145760 | tf_op jit(solution)/shard_map/all_to_all | solution.py:231
  447.8 21.7 fusion.62
  469.5 44.0 %pad_maximum_fusion.1 = f32[8,1024,2048]{2,1,0:T(8,128)} fusion(f32[8,256,2048]{2,1,0:T(8,128)} %bitcast.181, f32[8,768,2048]{2,1,0:T(8,128)} %fusion.62), kind=kLoop, calls=%fused_computation.1 | loop fusion | flops 16777216 | bytes 134217728 | tf_op jit(solution)/shard_map/concatenate | solution.py:243
  514.7 20.5 convolution_add_fusion
  535.1 27.3 %convert_reduce_fusion = (f32[8192]{0:T(1024)}, bf16[256,8192]{1,0:T(8,128)(2,1)}) fusion(f32[256,8192]{1,0:T(8,128)} %convolution_add_fusion, bf16[8192,2048]{1,0:T(8,128)(2,1)} %all-gather.11.cloned.1.call-done, bf16[1,256,2048]{2,1,0:T(8,128)(2,1)S(1)} %copy-done.11), kind=kOutput, calls=%fused_computation.10 | convolution fusion | flops 8615092224 | bytes 47218688 | tf_op jit(solution)/shard_map/dot_general | solution.py:26
  562.5 40.8 %fusion.101 = f32[8192,2048]{0,1:T(8,128)} fusion(bf16[256,8192]{1,0:T(8,128)(2,1)} %get-tuple-element.202, bf16[1,256,2048]{2,1,0:T(8,128)(2,1)S(1)} %copy-done.4, f32[2048]{0:T(1024)S(1)} %copy-done.45, f32[2048]{0:T(1024)S(1)} %copy-done.38, f32[256]{0:T(256)S(1)} %add_rsqrt_fusion, f32[256]{0:T(256)S(1)} %broadcast_multiply_fusion.5), kind=kOutput, calls=%fused_computation.162 | convolution fusion | flops 8593080320 | bytes 72370176 | tf_op jit(solution)/shard_map/dot_general | solution.py:20
  603.3 30.0 %fusion.71 = f32[8192,2048]{0,1:T(8,128)} fusion(bf16[1,256,2048]{2,1,0:T(8,128)(2,1)S(1)} %copy-done.11, f32[256,8192]{1,0:T(8,128)} %convolution_add_fusion), kind=kOutput, calls=%fused_computation.110 | convolution fusion | flops 8600420352 | bytes 76546048 | tf_op jit(solution)/shard_map/dot_general | solution.py:20
  633.3 90.0 %pad_maximum_fusion = f32[8192,4096]{0,1:T(8,128)} fusion(f32[8192,2048]{0,1:T(8,128)} %fusion.71, f32[8192,2048]{0,1:T(8,128)} %fusion.101), kind=kLoop, calls=%fused_computation | loop fusion | flops 33554432 | bytes 268435456 | tf_op jit(solution)/shard_map/concatenate | solution.py:199
  726.6 17.5 fusion.107
  744.1 13.7 fusion.43
  761.1 145.7 %reduce-scatter.3.cloned.1.call-done = f32[1024,2048]{1,0:T(8,128)} async-done(((f32[8192,2048]{1,0:T(8,128)}), f32[1024,2048]{1,0:T(8,128)}) %reduce-scatter.3.cloned.1.call-update) | async-done | bytes 8388624 | tf_op jit(solution)/shard_map/reduce_scatter | solution.py:242
  909.9 6.3 slice.137
  916.2 735.3 %reduce-scatter.5.cloned.1.call-done = f32[1024,4096]{0,1:T(8,128)} async-done(((f32[8192,4096]{0,1:T(8,128)}), f32[1024,4096]{0,1:T(8,128)}) %reduce-scatter.5.cloned.1.call-update) | async-done | bytes 16777232 | tf_op jit(solution)/shard_map/reduce_scatter | solution.py:198
  1651.5 11.3 fusion.104
  1664.1 7.1 fusion.16
  1671.2 23.5 fusion.30
  1694.7 88.4 %all-reduce.5.cloned.1.call-done = (f32[2048]{0:T(1024)}, f32[2048]{0:T(1024)}, f32[2048]{0:T(1024)}, f32[2048]{0:T(1024)}, f32[6144]{0:T(1024)}, /*index=5*/f32[2048]{0:T(1024)}, f32[8192]{0:T(1024)}) async-done(((f32[2048]{0:T(1024)}, f32[2048]{0:T(1024)}, f32[2048]{0:T(1024)}, f32[2048]{0:T(1024)}, f32[6144]{0:T(1024)}, /*index=5*/f32[2048]{0:T(1024)}, f32[8192]{0:T(1024)}), (f32[2048]{0:T(1024)}, ...) | async-done | bytes 98320 | tf_op jit(solution)/shard_map/psum | solution.py:266
  1791.8 833.2 %all-reduce.7.cloned.1.call-done = (f32[768,2048]{1,0:T(8,128)}, f32[256,2048]{1,0:T(8,128)}, f32[1024,2048]{0,1:T(8,128)}, f32[1024,2048]{0,1:T(8,128)}) async-done(((f32[768,2048]{1,0:T(8,128)}, f32[256,2048]{1,0:T(8,128)}, f32[1024,2048]{0,1:T(8,128)}, f32[1024,2048]{0,1:T(8,128)}), (f32[768,2048]{1,0:T(8,128)}, f32[256,2048]{1,0:T(8,128)}, f32[1024,2048]{0,1:T(8,128)}, ...) | async-done | bytes 25165840 | tf_op jit(solution)/shard_map/psum | solution.py:252
  2624.9 9.1 copy.166
  2634.1 9.1 copy.167
  2643.8 6.4 copy.197
  (200 shorter events, 110.3 us)
Async XLA Ops:
  7.2 59.8 %all-gather.7.cloned.1.call-start = ((), (), s32[]{:S(2)}) async-start(), calls=%async_computation.7 | async-start | bytes 9437184 | tf_op jit(solution)/shard_map/all_gather | solution.py:165
  7.9 186.4 %all-gather.5.cloned.1.call-start = ((), (), s32[]{:S(2)}) async-start(), calls=%async_computation.6 | async-start | bytes 28311552 | tf_op jit(solution)/shard_map/all_gather | solution.py:164
  8.7 504.9 %all-gather.9.cloned.1.call-start = ((), (), s32[]{:S(2)}) async-start(), calls=%async_computation.8 | async-start | bytes 37748736 | tf_op jit(solution)/shard_map/all_gather | solution.py:188
  9.4 57.6 %copy-start.9 = (bf16[1,256,2048]{2,1,0:T(8,128)(2,1)S(1)}, bf16[1,256,2048]{2,1,0:T(8,128)(2,1)}, u32[]{:S(2)}) copy-start(bf16[1,256,2048]{2,1,0:T(8,128)(2,1)} %param.29) | copy-start | bytes 3145732
  9.4 525.7 %all-gather.11.cloned.1.call-start = ((), (), s32[]{:S(2)}) async-start(), calls=%async_computation.9 | async-start | bytes 37748736 | tf_op jit(solution)/shard_map/all_gather | solution.py:189
  10.2 552.2 %copy-start.40 = (f32[256]{0:T(256)}, f32[256]{0:T(256)S(1)}, u32[]{:S(2)}) copy-start(f32[256]{0:T(256)S(1)} %broadcast_multiply_fusion.5) | copy-start | bytes 3076
  10.7 551.8 %copy-start.42 = (f32[256]{0:T(256)}, f32[256]{0:T(256)S(1)}, u32[]{:S(2)}) copy-start(f32[256]{0:T(256)S(1)} %add_rsqrt_fusion) | copy-start | bytes 3076
  72.7 121.5 %copy-start.36 = (f32[2048]{0:T(1024)S(1)}, f32[2048]{0:T(1024)}, u32[]{:S(2)}) copy-start(f32[2048]{0:T(1024)} %param.17) | copy-start | bytes 24580
  72.8 121.5 %copy-start.44 = (f32[2048]{0:T(1024)S(1)}, f32[2048]{0:T(1024)}, u32[]{:S(2)}) copy-start(f32[2048]{0:T(1024)} %param.18) | copy-start | bytes 24580
  72.8 121.5 %copy-start.48 = (f32[6144]{0:T(1024)S(1)}, f32[6144]{0:T(1024)}, u32[]{:S(2)}) copy-start(f32[6144]{0:T(1024)} %param.22) | copy-start | bytes 73732
  74.3 138.4 %all-to-all-start.2 = ((bf16[1,256,8,256]{3,1,0,2:T(8,128)(2,1)}), bf16[1,256,8,256]{3,1,0,2:T(8,128)(2,1)S(1)}, u32[]{:S(2)}, u32[]{:S(2)}) async-start(bf16[1,256,8,256]{3,1,0,2:T(8,128)(2,1)} %copy.148), calls=%async_computation.2 | async-start | bytes 2097152 | tf_op jit(solution)/shard_map/all_to_all | solution.py:213
  213.7 75.8 %all-to-all-start = ((bf16[1,256,8,768]{3,1,0,2:T(8,128)(2,1)}), bf16[1,256,8,768]{3,1,0,2:T(8,128)(2,1)S(1)}, u32[]{:S(2)}, u32[]{:S(2)}) async-start(bf16[1,256,8,768]{3,1,0,2:T(8,128)(2,1)} %copy.141), calls=%async_computation | async-start | bytes 6291456 | tf_op jit(solution)/shard_map/all_to_all | solution.py:171
  311.2 56.2 %all-to-all-start.1 = ((bf16[1,1024,2,256]{3,2,0,1:T(2,128)(2,1)}), bf16[1,1024,2,256]{3,2,0,1:T(2,128)(2,1)}, u32[]{:S(2)}, u32[]{:S(2)}) async-start(bf16[1,1024,2,256]{3,2,0,1:T(2,128)(2,1)} %copy.145), calls=%async_computation.1 | async-start | bytes 2097152 | tf_op jit(solution)/shard_map/all_to_all | solution.py:181
  331.0 9.4 copy-start.17
  367.3 8.2 copy-start.10
  367.3 74.9 %all-to-all-start.3 = ((bf16[1,1024,2,768]{3,2,0,1:T(2,128)(2,1)}), bf16[1,1024,2,768]{3,2,0,1:T(2,128)(2,1)}, u32[]{:S(2)}, u32[]{:S(2)}) async-start(bf16[1,1024,2,768]{3,2,0,1:T(2,128)(2,1)} %copy.162), calls=%async_computation.3 | async-start | bytes 6291456 | tf_op jit(solution)/shard_map/all_to_all | solution.py:231
  373.0 533.8 %reduce-scatter.3.cloned.1.call-start = ((), (), s32[]{:S(2)}) async-start(), calls=%async_computation.10 | async-start | bytes 75497472 | tf_op jit(solution)/shard_map/reduce_scatter | solution.py:242
  375.5 8.1 copy-start.22
  444.5 24.9 copy-start.1
  513.5 21.6 copy-start.11
  513.5 1138.0 %reduce-scatter.5.cloned.1.call-start = ((), (), s32[]{:S(2)}) async-start(), calls=%async_computation.11 | async-start | bytes 150994944 | tf_op jit(solution)/shard_map/reduce_scatter | solution.py:198
  723.3 1059.8 %all-reduce.5.cloned.1.call-start = ((), (), s32[]{:S(2)}) async-start(), calls=%async_computation.12 | async-start | bytes 196608 | tf_op jit(solution)/shard_map/psum | solution.py:266
  726.5 17.5 copy-start.5
  726.5 17.5 copy-start.7
  726.5 17.6 copy-start.37
  726.5 17.6 copy-start.39
  726.5 17.6 copy-start.41
  726.5 17.6 copy-start.43
  744.1 13.8 copy-start.12
  761.0 1863.9 %all-reduce.7.cloned.1.call-start = ((), (), s32[]{:S(2)}) async-start(), calls=%async_computation.13 | async-start | bytes 50331648 | tf_op jit(solution)/shard_map/psum | solution.py:252
  1664.1 7.1 copy-start.50
  1785.2 858.0 %copy-start.46 = (f32[256]{0:T(256)}, f32[256]{0:T(256)S(1)}, u32[]{:S(2)}) copy-start(f32[256]{0:T(256)S(1)} %dynamic_slice.49) | copy-start | bytes 3076
  (33 other events, 101.9 us)
Sparse Core Ops, SparseCore 0:
  9.9 57.0 all-gather.6
  68.9 125.3 all-gather.4
  196.2 160.7 all-gather.8
  358.7 160.7 all-gather.10
  523.0 383.7 reduce-scatter.2
  910.6 740.8 reduce-scatter.4
  1659.1 123.9 all-reduce.4
  1787.2 837.7 all-reduce.6
where the time goes:
time: 2670 us; the launch traced here: 2660 us
  waiting for transfers between devices  2100 us (79%)
  matrix products  255 us (10%)
  other arithmetic  153 us (6%)
  local copies, waits for them, and re-layouts  117 us (4%)
    psum x1, waiting for transfers between devices, per_device(): lax.psum((qkv_local, dense_local, up_grad, down_grad), 'sp')  833 us
    reduce_scatter x1, waiting for transfers between devices, per_device(): lax.psum_scatter(jnp.concatenate([contract_rows(grad_cols, normed_mlp), c...  735 us
    reduce_scatter x1, waiting for transfers between devices, per_device(): lax.psum_scatter(jnp.concatenate([qkv_term, dense_term], axis=1).reshape(...  146 us
    all_gather x1, waiting for transfers between devices, per_device(): lax.all_gather(w_qkv, 'fsdp', axis=0, tiled=True)  115 us
    dot_general x4, matrix products, contract_rows(): lax.dot_general(former, latter, (((0,), (0,)), ((), ())), preferred_eleme...  101 us
    concatenate x1, other arithmetic, per_device(): jnp.concatenate([contract_rows(grad_cols, normed_mlp), contract_rows(acti...  90 us
    psum x1, waiting for transfers between devices, per_device(): lax.psum((gain_one, shift_one, gain_two, shift_two, bias_qkv, bias_out, b...  88.4 us
    dot_general x4, matrix products, times_transposed(): lax.dot_general(former, latter, (((1,), (1,)), ((), ())), preferred_eleme...  67.8 us
  transfers between devices with their start and end apart: 12, of which 8 were waited for; matrix products, arithmetic and copies ran while one was open for 18% of the time, Pallas kernels for 0%

commit v1 on v0

v1 whole, which is shorter than its diff:
```python
import math

import jax
import jax.numpy as jnp
from jax import lax
from jax.sharding import PartitionSpec as P

HEADS = 8
HEAD_DIM = 256
ROT = 64


EPSILON = 1e-05
NEGATIVE = -1e30
ROOT_HALF = 0.7071067811865476
ROOT_TWO_PI = 2.5066282746310002
SCALE = 1.0 / math.sqrt(HEAD_DIM)


def rounded(array):
    return lax.reduce_precision(array.astype(jnp.float32), 8, 7).astype(jnp.bfloat16)


def contract_rows(former, latter):
    return lax.dot_general(
        former, latter, (((0,), (0,)), ((), ())), preferred_element_type=jnp.float32
    )


def times_transposed(former, latter):
    return lax.dot_general(
        former, latter, (((1,), (1,)), ((), ())), preferred_element_type=jnp.float32
    )


def times(former, latter):
    return jnp.dot(former, latter, preferred_element_type=jnp.float32)


def norm_scaled(inputs):
    average = jnp.mean(inputs, axis=-1, keepdims=True)
    centred = inputs - average
    variance = jnp.mean(centred * centred, axis=-1, keepdims=True)
    inverse = lax.rsqrt(variance + EPSILON)
    return centred * inverse, inverse


def gelu_pair(hidden):
    cumulative = 0.5 * (1.0 + jax.scipy.special.erf(hidden * ROOT_HALF))
    return (
        hidden * cumulative,
        cumulative + hidden * jnp.exp(-0.5 * hidden * hidden) / ROOT_TWO_PI,
    )


def rotary_tables(segment_rows):
    length = segment_rows.shape[-1]
    places = jnp.arange(length, dtype=jnp.int32)
    changes = jnp.concatenate(
        [
            jnp.ones_like(segment_rows[..., :1]),
            (segment_rows[..., 1:] != segment_rows[..., :-1]).astype(jnp.int32),
        ],
        axis=-1,
    )
    first_place = lax.cummax(changes * places, axis=segment_rows.ndim - 1)
    position = (places - first_place).astype(jnp.float32)
    exponent = jnp.arange(0, ROT, 2).astype(jnp.float32) / ROT
    frequency = 1.0 / jnp.power(10000.0, exponent)
    angles = position[..., None] * frequency
    angles = jnp.concatenate([angles, angles], axis=-1)
    return (jnp.cos(angles), jnp.sin(angles))


def rotate(heads_part, cos_table, sin_table):
    half_rot = ROT // 2
    turned = heads_part[..., :ROT]
    swapped = jnp.concatenate([-turned[..., half_rot:], turned[..., :half_rot]], axis=-1)
    turned = turned * cos_table[..., None, :] + swapped * sin_table[..., None, :]
    return jnp.concatenate([turned, heads_part[..., ROT:]], axis=-1)


def unrotate(grads_part, cos_table, sin_table):
    half_rot = ROT // 2
    turned = grads_part[..., :ROT]
    along_sin = turned * sin_table[..., None, :]
    back_turn = jnp.concatenate([along_sin[..., half_rot:], -along_sin[..., :half_rot]], axis=-1)
    turned = turned * cos_table[..., None, :] + back_turn
    return jnp.concatenate([turned, grads_part[..., ROT:]], axis=-1)


def build_mask(segment_rows):
    places = jnp.arange(segment_rows.shape[-1], dtype=jnp.int32)
    return (segment_rows[:, :, None] == segment_rows[:, None, :]) & (
        places[None, :] <= places[:, None]
    )


def attention_scores(queries, keys_rot):
    return (
        jnp.einsum("bqhd,bkhd->bhqk", queries, keys_rot, preferred_element_type=jnp.float32) * SCALE
    )


def attend_forward(queries, keys_rot, values, mask):
    scores = jnp.where(mask[:, None], attention_scores(queries, keys_rot), NEGATIVE)
    row_top = jnp.max(scores, axis=-1, keepdims=True)
    exponent = jnp.exp(scores - row_top)
    row_total = jnp.sum(exponent, axis=-1, keepdims=True)
    attention = (exponent / row_total).astype(jnp.bfloat16)
    context = jnp.einsum("bhqk,bkhd->bqhd", attention, values, preferred_element_type=jnp.float32)
    return (context.astype(jnp.bfloat16), row_top + jnp.log(row_total))


def attend_backward(queries, keys_rot, values, mask, log_total, context_grad):
    scores = attention_scores(queries, keys_rot)
    attention = jnp.where(mask[:, None], jnp.exp(scores - log_total), 0.0)
    value_grad = jnp.einsum(
        "bhqk,bqhd->bkhd",
        attention.astype(jnp.bfloat16),
        context_grad,
        preferred_element_type=jnp.float32,
    )
    attention_grad = jnp.einsum(
        "bqhd,bkhd->bhqk", context_grad, values, preferred_element_type=jnp.float32
    )
    row_centre = jnp.sum(attention * attention_grad, axis=-1, keepdims=True)
    score_grad = (attention * (attention_grad - row_centre)).astype(jnp.bfloat16)
    query_grad = (
        jnp.einsum("bhqk,bkhd->bqhd", score_grad, keys_rot, preferred_element_type=jnp.float32)
        * SCALE
    )
    key_grad = (
        jnp.einsum("bhqk,bqhd->bkhd", score_grad, queries, preferred_element_type=jnp.float32)
        * SCALE
    )
    return (query_grad, key_grad, value_grad)


def sum_over_line(partial):
    inward = lax.ppermute(partial, "sp", [(0, 1), (3, 2)])
    half = rounded(partial.astype(jnp.float32) + inward.astype(jnp.float32))
    other = lax.ppermute(half, "sp", [(1, 2), (2, 1)])
    whole = rounded(half.astype(jnp.float32) + other.astype(jnp.float32))
    outward = lax.ppermute(whole, "sp", [(1, 0), (2, 3)])
    place = lax.axis_index("sp")
    inner = (place == 1) | (place == 2)
    return jnp.where(inner, whole, outward).astype(jnp.float32)


def sum_over_sp(partial):
    partial = rounded(partial)
    if lax.axis_size("sp") == 4:
        return sum_over_line(partial)
    return lax.psum(partial, "sp").astype(jnp.float32)


def per_device(
    hidden_in,
    segments,
    ln1_gain,
    ln1_bias,
    ln2_gain,
    ln2_bias,
    w_qkv,
    b_qkv,
    w_dense,
    b_dense,
    w_up,
    b_up,
    w_down,
    b_down,
    cotangent,
):
    seq_local, shard_len, width = hidden_in.shape
    seq_len = segments.shape[1]
    nf, ns = lax.axis_size("fsdp"), lax.axis_size("sp")
    f_place, s_place = lax.axis_index("fsdp"), lax.axis_index("sp")
    seqs = seq_local * nf
    group = seqs // ns
    piece = shard_len // nf
    tokens = group * seq_len
    per_head = max(1, nf // HEADS)
    head_count = max(1, HEADS // nf)
    head_sets = [[head * per_head + k for k in range(per_head)] for head in range(nf // per_head)]

    def gather_tokens(block):
        part = lax.all_to_all(block, "fsdp", split_axis=1, concat_axis=0, tiled=True)
        part = lax.all_to_all(part, "sp", split_axis=0, concat_axis=1, tiled=True)
        return lax.all_gather(part, "fsdp", axis=0, tiled=True).reshape(tokens, width)

    def scatter_tokens(partial):
        part = partial.reshape(nf * group, ns * piece, width)
        part = lax.psum_scatter(part, "fsdp", scatter_dimension=0, tiled=True)
        part = lax.all_to_all(part, "sp", split_axis=1, concat_axis=0, tiled=True)
        return lax.all_to_all(part, "fsdp", split_axis=0, concat_axis=1, tiled=True)

    def in_order(array):
        array = array.reshape(nf, group, ns, piece, -1)
        return array.transpose(1, 2, 0, 3, 4).reshape(group, seq_len, -1)

    def out_of_order(array):
        array = array.reshape(group, ns, nf, piece, -1)
        return array.transpose(2, 0, 1, 3, 4).reshape(tokens, -1)

    def over_head(array, axis):
        if per_head == 1:
            return array
        return lax.all_gather(
            array, "fsdp", axis=axis, tiled=True, axis_index_groups=head_sets
        )

    def own_columns(array):
        if per_head == 1:
            return array
        share = array.shape[-1] // per_head
        return lax.dynamic_slice_in_dim(array, (f_place % per_head) * share, share, array.ndim - 1)

    def own_part(vector):
        share = vector.shape[0] // nf
        return lax.dynamic_slice_in_dim(vector, f_place * share, share, 0)

    gathered = gather_tokens(hidden_in)
    upstream = gather_tokens(cotangent)
    rows = lax.all_gather(segments, "fsdp", axis=0, tiled=True)
    rows = lax.dynamic_slice_in_dim(rows, s_place * group, group, 0)

    dense_in = lax.all_to_all(w_dense, "fsdp", split_axis=1, concat_axis=0, tiled=True)
    head_qkv = over_head(w_qkv, 0)
    head_dense = over_head(dense_in, 1)
    head_bias = lax.dynamic_slice_in_dim(
        b_qkv, (f_place // per_head) * head_qkv.shape[0], head_qkv.shape[0], 0
    )

    scaled, _ = norm_scaled(gathered.astype(jnp.float32))
    normed = (scaled * ln1_gain + ln1_bias).astype(jnp.bfloat16)
    normed_mlp = (scaled * ln2_gain + ln2_bias).astype(jnp.bfloat16)

    hidden = times_transposed(normed_mlp, w_up) + own_part(b_up)
    activated, slope = gelu_pair(hidden)
    activated = activated.astype(jnp.bfloat16)
    hidden_grad = (times_transposed(upstream, w_down) * slope).astype(jnp.bfloat16)
    down_term = contract_rows(activated, upstream)
    up_term = contract_rows(hidden_grad, normed_mlp)
    mlp_norm_grad = times(hidden_grad, w_up)

    packed = (times_transposed(normed, head_qkv) + head_bias).astype(jnp.bfloat16)
    packed = in_order(packed).reshape(group, seq_len, head_count, 3 * HEAD_DIM)
    cos_table, sin_table = rotary_tables(rows)
    queries = rotate(packed[..., :HEAD_DIM].astype(jnp.float32), cos_table, sin_table).astype(
        jnp.bfloat16
    )
    keys_rot = rotate(
        packed[..., HEAD_DIM : 2 * HEAD_DIM].astype(jnp.float32), cos_table, sin_table
    ).astype(jnp.bfloat16)
    values = packed[..., 2 * HEAD_DIM :]
    mask = build_mask(rows)
    context, log_total = attend_forward(queries, keys_rot, values, mask)
    context = own_columns(out_of_order(context))
    partial_out = times_transposed(context, dense_in) + times(activated, w_down)
    context_grad = in_order(times(upstream, head_dense).astype(jnp.bfloat16)).reshape(
        group, seq_len, head_count, HEAD_DIM
    )
    query_grad, key_grad, value_grad = attend_backward(
        queries, keys_rot, values, mask, log_total, context_grad
    )
    packed_grad = jnp.concatenate(
        [
            unrotate(query_grad, cos_table, sin_table),
            unrotate(key_grad, cos_table, sin_table),
            value_grad,
        ],
        axis=-1,
    ).astype(jnp.bfloat16)
    packed_grad = own_columns(out_of_order(packed_grad))
    attn_norm_grad = times(packed_grad, w_qkv)
    qkv_term = contract_rows(packed_grad, normed)
    dense_term = contract_rows(upstream, context).astype(jnp.bfloat16)
    dense_term = lax.all_to_all(dense_term, "fsdp", split_axis=0, concat_axis=1, tiled=True)

    vectors = jnp.stack(
        [
            jnp.sum(attn_norm_grad * scaled, axis=0),
            jnp.sum(attn_norm_grad, axis=0),
            jnp.sum(mlp_norm_grad * scaled, axis=0),
            jnp.sum(mlp_norm_grad, axis=0),
        ],
        axis=1,
    )
    vectors = lax.psum_scatter(vectors, "fsdp", scatter_dimension=0, tiled=True)
    bias_out = own_part(jnp.sum(upstream.astype(jnp.float32), axis=0))
    bias_qkv = jnp.sum(packed_grad.astype(jnp.float32), axis=0)
    bias_up = jnp.sum(hidden_grad.astype(jnp.float32), axis=0)
    vectors, bias_out, bias_qkv, bias_up = lax.psum((vectors, bias_out, bias_qkv, bias_up), "sp")

    output = scatter_tokens(rounded(partial_out))
    weighted = scatter_tokens(rounded(attn_norm_grad * ln1_gain + mlp_norm_grad * ln2_gain))
    inputs = hidden_in.astype(jnp.float32)
    output = (inputs + (output.astype(jnp.float32) + (b_dense + b_down))).astype(jnp.bfloat16)
    own_scaled, own_inverse = norm_scaled(inputs)
    weighted = weighted.astype(jnp.float32)
    first_mean = jnp.mean(weighted, axis=-1, keepdims=True)
    second_mean = jnp.mean(weighted * own_scaled, axis=-1, keepdims=True)
    input_grad = (
        cotangent.astype(jnp.float32)
        + own_inverse * (weighted - first_mean - own_scaled * second_mean)
    ).astype(jnp.bfloat16)

    grad_down_w = sum_over_sp(down_term)
    grad_up_w = sum_over_sp(up_term)
    grad_qkv_w = sum_over_sp(qkv_term)
    grad_dense_w = sum_over_sp(dense_term)
    return (
        output,
        input_grad,
        vectors[:, 0],
        vectors[:, 1],
        vectors[:, 2],
        vectors[:, 3],
        grad_qkv_w,
        bias_qkv,
        grad_dense_w,
        bias_out,
        grad_up_w,
        bias_up,
        grad_down_w,
        bias_out,
    )


def solution(mesh):
    rows = P("fsdp", "sp", None)
    first = P("fsdp", None)
    return jax.shard_map(
        per_device,
        mesh=mesh,
        in_specs=(
            rows,
            first,
            P(),
            P(),
            P(),
            P(),
            first,
            P(),
            first,
            P(),
            first,
            P(),
            first,
            P(),
            rows,
        ),
        out_specs=(
            rows,
            rows,
            P("fsdp"),
            P("fsdp"),
            P("fsdp"),
            P("fsdp"),
            first,
            P("fsdp"),
            first,
            P("fsdp"),
            first,
            P("fsdp"),
            first,
            P("fsdp"),
        ),
        check_vma=False,
    )
```

time: 2670 us -> 1070 us (0.40)
  waiting for transfers between devices: 2100 us -> 276 us
  blocking collectives: 0 us -> 257 us
  starting transfers between devices: 19.7 us -> 115 us
  matrix products: 255 us -> 168 us
  local copies, waits for them, and re-layouts: 117 us -> 79.8 us
    psum x2 -> x0, waiting for transfers between devices: 922 us -> none  [the longest x1 833 us: per_device(): lax.psum((qkv_local, dense_local, up_grad, down_grad), 'sp')]
    reduce_scatter x2, waiting for transfers between devices: 881 us -> 0.04 us  [scatter_tokens(): part = lax.psum_scatter(part, 'fsdp', scatter_dimension=0, tiled=True)]
    ppermute x0 -> x12, waiting for transfers between devices: none -> 180 us  [the longest x4 180 us: sum_over_line(): inward = lax.ppermute(partial, 'sp', [(0, 1), (3, 2)])]
    all_gather x4 -> x2, waiting for transfers between devices: 172 us -> 0.01 us  [gather_tokens(): lax.all_gather(part, 'fsdp', axis=0, tiled=True).reshape(tokens, width)]
    concatenate x3 -> x1, other arithmetic: 134 us -> 1.33 us  [rotary_tables(): angles = jnp.concatenate([angles, angles], axis=-1)]
    psum x0 -> x1, blocking collectives: none -> 127 us  [per_device(): lax.psum((vectors, bias_out, bias_qkv, bias_up), 'sp')]
    all_to_all x0 -> x4, blocking collectives: none -> 104 us  [the longest x2 56.6 us: gather_tokens(): part = lax.all_to_all(part, 'sp', split_axis=0, concat_axis=1, tiled=True)]
    convert_element_type x1 -> x18, other arithmetic: 0.35 us -> 87.4 us  [the longest x9 45 us: rounded(): lax.reduce_precision(array.astype(jnp.float32), 8, 7).astype(jnp.bfloat16)]
  transfers between devices with their start and end apart: 12 -> 23, of which waited for: 8 -> 7; matrix products, arithmetic and copies ran while one was open for 18% -> 22% of each run, Pallas kernels for 0% -> 0%
where the time goes in v1:
time: 1070 us; the launch traced here: 1060 us
  waiting for transfers between devices  276 us (26%)
  blocking collectives  257 us (24%)
  matrix products  168 us (16%)
  other arithmetic  151 us (14%)
  starting transfers between devices  115 us (11%)
  local copies, waits for them, and re-layouts  79.8 us (7%)
  between operations  15.1 us (1%)
    ppermute x4, waiting for transfers between devices, sum_over_line(): inward = lax.ppermute(partial, 'sp', [(0, 1), (3, 2)])  180 us
    psum x1, blocking collectives, per_device(): lax.psum((vectors, bias_out, bias_qkv, bias_up), 'sp')  127 us
    all_to_all x2, waiting for transfers between devices, scatter_tokens(): part = lax.all_to_all(part, 'sp', split_axis=1, concat_axis=0, tiled=True)  89.9 us
    all_to_all x2, starting transfers between devices, scatter_tokens(): part = lax.all_to_all(part, 'sp', split_axis=1, concat_axis=0, tiled=True)  68.4 us
    all_to_all x2, blocking collectives, gather_tokens(): part = lax.all_to_all(part, 'sp', split_axis=0, concat_axis=1, tiled=True)  56.6 us
    dot_general x4, matrix products, times_transposed(): lax.dot_general(former, latter, (((1,), (1,)), ((), ())), preferred_eleme...  52 us
    dot_general x4, matrix products, times(): return jnp.dot(former, latter, preferred_element_type=jnp.float32)  49.7 us
    all_to_all x2, blocking collectives, gather_tokens(): lax.all_to_all(block, 'fsdp', split_axis=1, concat_axis=0, tiled=True)  47.4 us
  transfers between devices with their start and end apart: 23, of which 7 were waited for; matrix products, arithmetic and copies ran while one was open for 22% of the time, Pallas kernels for 0%

profile of v1, /device:TPU:0, one launch (start us, length us, event | category | flops | bytes accessed | tf_op | source)
XLA Modules:
  0.0 1062.1 jit_solution(14219116837195556078)
XLA Ops:
  12.1 9.0 reduce.19
  23.7 20.6 %all_to_all.146 = bf16[8,2,32768]{2,1,0:T(2,128)(2,1)} all-to-all(bf16[8,2,32768]{2,1,0:T(2,128)(2,1)} %reshape.579), channel_id=1, replica_groups=mesh['fsdp'=8,'sp'=4] {'fsdp'}, dimensions={0} | all-to-all | bytes 2097152 | tf_op jit(solution)/shard_map/all_to_all | solution.py:188
  52.3 30.2 %all_to_all.147 = bf16[8,32,2048]{2,1,0:T(8,128)(2,1)S(1)} all-to-all(bf16[8,32,2048]{2,1,0:T(8,128)(2,1)S(1)} %bitcast.199), channel_id=1, replica_groups=mesh['fsdp'=8,'sp'=4] {'sp'}, dimensions={0} | all-to-all | bytes 2097152 | tf_op jit(solution)/shard_map/all_to_all | solution.py:189
  88.0 9.2 reduce.20
  99.8 26.8 %all_to_all.148 = bf16[8,2,32768]{2,1,0:T(2,128)(2,1)} all-to-all(bf16[8,2,32768]{2,1,0:T(2,128)(2,1)} %reshape.581), channel_id=1, replica_groups=mesh['fsdp'=8,'sp'=4] {'fsdp'}, dimensions={0} | all-to-all | bytes 2097152 | tf_op jit(solution)/shard_map/all_to_all | solution.py:188
  134.6 26.5 %all_to_all.149 = bf16[8,32,2048]{2,1,0:T(8,128)(2,1)S(1)} all-to-all(bf16[8,32,2048]{2,1,0:T(8,128)(2,1)S(1)} %bitcast.200), channel_id=1, replica_groups=mesh['fsdp'=8,'sp'=4] {'sp'}, dimensions={0} | all-to-all | bytes 2097152 | tf_op jit(solution)/shard_map/all_to_all | solution.py:189
  168.7 26.7 %all-gather = s32[8,1,1024]{2,1,0:T(1,128)S(1)} all-gather(s32[1,1,1024]{2,1,0:T(1,128)S(1)} %bitcast.233), channel_id=1, replica_groups=mesh['fsdp'=8,'sp'=4] {'fsdp'}, dimensions={0}, use_global_device_ids=true | all-gather | bytes 36864 | tf_op jit(solution)/shard_map/all_gather | solution.py:225
  212.1 7.4 add_convert_fusion.2
  219.4 7.1 add_convert_fusion.3
  287.8 7.0 concatenate.117
  298.7 15.7 %multiply_convert_fusion.1 = (bf16[2048,1024]{1,0:T(8,128)(2,1)}, f32[2048,1024]{1,0:T(8,128)}) fusion(f32[1024]{0:T(1024)S(1)} %dynamic_slice.14, bf16[2048,2048]{1,0:T(8,128)(2,1)} %get-tuple-element.26, bf16[1024,2048]{1,0:T(8,128)(2,1)S(1)} %copy-done.39), kind=kOutput, calls=%fused_computation.29 | convolution fusion | flops 8602517504 | bytes 25169920 | tf_op jit(solution)/shard_map/dot_general | solution.py:31
  314.4 17.5 %convert_reduce_fusion.2 = (f32[1024]{0:T(1024)}, bf16[2048,1024]{1,0:T(8,128)(2,1)}) fusion(f32[2048,1024]{1,0:T(8,128)} %get-tuple-element.60, f32[1024]{0:T(1024)S(1)} %dynamic_slice.14, bf16[2048,2048]{1,0:T(8,128)(2,1)S(1)} %bitcast.176, bf16[1024,2048]{1,0:T(8,128)(2,1)} %param.27), kind=kOutput, calls=%fused_computation.22 | convolution fusion | flops 8617196544 | bytes 25174016 | tf_op jit(solution)/shard_map/dot_general | solution.py:31
  331.9 14.1 %fusion.59 = f32[2048,2048]{1,0:T(8,128)} fusion(bf16[2048,1024]{1,0:T(8,128)(2,1)} %get-tuple-element.62, bf16[1024,2048]{1,0:T(8,128)(2,1)S(1)} %copy-done.39), kind=kOutput, calls=%fused_computation.148 | convolution fusion | flops 8589934592 | bytes 25165824 | tf_op jit(solution)/shard_map/dot_general | solution.py:37
  346.0 17.8 %multiply_reduce_fusion.1 = (f32[2048]{0:T(1024)S(1)}, f32[2048]{0:T(1024)S(1)}, f32[2048]{0:T(1024)S(1)}, f32[2048]{0:T(1024)S(1)}, bf16[2048,2048]{1,0:T(8,128)(2,1)}) fusion(bf16[16,128,2048]{2,1,0:T(8,128)(2,1)} %all-gather.4.cloned.1.call-done, f32[2048]{0:T(1024)S(1)} %get-tuple-element.48, f32[2048]{0:T(1024)S(1)} %get-tuple-element.49, ...), kind=kOutput, calls=%fused_computation.5 | convolution fusion | flops 6501163008 | bytes 39911424 | tf_op jit(solution)/shard_map/dot_general | solution.py:37
  365.0 7.5 fusion.31
  373.6 15.8 %reduce-precision_convert_fusion.7 = bf16[1024,2048]{1,0:T(8,128)(2,1)} fusion(bf16[2048,1024]{1,0:T(8,128)(2,1)} %get-tuple-element.62, bf16[2048,2048]{1,0:T(8,128)(2,1)} %get-tuple-element.26), kind=kOutput, calls=%fused_computation.25 | convolution fusion | flops 8594128896 | bytes 16777216 | tf_op jit(solution)/shard_map/dot_general | solution.py:25
  395.1 11.7 %fusion.58 = f32[2048,2048]{1,0:T(8,128)} fusion(bf16[2048,1024]{1,0:T(8,128)(2,1)S(1)} %copy-done.41, bf16[1024,2048]{1,0:T(8,128)(2,1)S(1)} %copy-done.40), kind=kOutput, calls=%fused_computation.147 | convolution fusion | flops 8589934592 | bytes 25165824 | tf_op jit(solution)/shard_map/dot_general | solution.py:37
  406.8 11.7 %reduce-precision_convert_fusion.1 = bf16[2048,2048]{1,0:T(8,128)(2,1)} fusion(f32[2048,2048]{1,0:T(8,128)} %fusion.58, bf16[2048,256]{1,0:T(8,128)(2,1)S(1)} %bitcast.188, bf16[2048,256]{1,0:T(8,128)(2,1)S(1)} %bitcast.212), kind=kOutput, calls=%fused_computation.7 | convolution fusion | flops 2160066560 | bytes 27262976 | tf_op jit(solution)/shard_map/dot_general | solution.py:31
  418.5 14.7 %reduce-precision_convert_fusion.4 = bf16[1024,2048]{1,0:T(8,128)(2,1)} fusion(bf16[2048,1024]{1,0:T(8,128)(2,1)} %get-tuple-element.59, bf16[2048,2048]{1,0:T(8,128)(2,1)} %bitcast.173), kind=kOutput, calls=%fused_computation.21 | convolution fusion | flops 8594128896 | bytes 16777216 | tf_op jit(solution)/shard_map/dot_general | solution.py:25
  436.5 6.3 add_convert_fusion
  442.8 8.3 reduce-precision_convert_fusion.10
  454.0 30.2 %collective-permute-done.6 = bf16[1024,2048]{1,0:T(8,128)(2,1)} collective-permute-done((bf16[1024,2048]{1,0:T(8,128)(2,1)}, bf16[1024,2048]{1,0:T(8,128)(2,1)}, u32[]{:S(2)}, u32[]{:S(2)}) %collective-permute-start.6) | collective-permute-done | bytes 4194336 | tf_op jit(solution)/shard_map/ppermute | solution.py:141
  484.3 7.9 reduce-precision_convert_fusion.6
  501.8 72.4 %collective-permute-done.9 = bf16[1024,2048]{1,0:T(8,128)(2,1)} collective-permute-done((bf16[1024,2048]{1,0:T(8,128)(2,1)}, bf16[1024,2048]{1,0:T(8,128)(2,1)}, u32[]{:S(2)}, u32[]{:S(2)}) %collective-permute-start.9) | collective-permute-done | bytes 4194336 | tf_op jit(solution)/shard_map/ppermute | solution.py:141
  574.1 7.7 reduce-precision_convert_fusion.3
  584.6 56.3 %collective-permute-done = bf16[768,2048]{1,0:T(8,128)(2,1)} collective-permute-done((bf16[768,2048]{1,0:T(8,128)(2,1)}, bf16[768,2048]{1,0:T(8,128)(2,1)}, u32[]{:S(2)}, u32[]{:S(2)}) %collective-permute-start) | collective-permute-done | bytes 3145760 | tf_op jit(solution)/shard_map/ppermute | solution.py:141
  655.6 20.9 %collective-permute-done.3 = bf16[256,2048]{1,0:T(8,128)(2,1)S(1)} collective-permute-done((bf16[256,2048]{1,0:T(8,128)(2,1)S(1)}, bf16[256,2048]{1,0:T(8,128)(2,1)S(1)}, u32[]{:S(2)}, u32[]{:S(2)}) %collective-permute-start.3) | collective-permute-done | bytes 1048608 | tf_op jit(solution)/shard_map/ppermute | solution.py:141
  677.6 7.7 reduce-precision_convert_fusion.5
  697.3 63.8 %all-to-all-start.7 = ((bf16[2,128,2048]{2,0,1:T(2,128)(2,1)}), bf16[2,128,2048]{2,0,1:T(2,128)(2,1)}, u32[]{:S(2)}, u32[]{:S(2)}) async-start(bf16[2,128,2048]{2,0,1:T(2,128)(2,1)} %copy.202), calls=%async_computation.9 | async-start | bytes 2097152 | tf_op jit(solution)/shard_map/all_to_all | solution.py:195
  761.2 7.7 reduce-precision_convert_fusion.2
  777.8 89.9 %all-to-all-done.7 = bf16[2,128,2048]{2,0,1:T(2,128)(2,1)} async-done(((bf16[2,128,2048]{2,0,1:T(2,128)(2,1)}), bf16[2,128,2048]{2,0,1:T(2,128)(2,1)}, u32[]{:S(2)}, u32[]{:S(2)}) %all-to-all-start.7) | async-done | bytes 1048608 | tf_op jit(solution)/shard_map/all_to_all | solution.py:195
  878.6 126.6 %all-reduce.1 = (f32[256,4]{0,1:T(4,128)S(1)}, f32[768]{0:T(1024)}, f32[256]{0:T(256)S(1)}, f32[1024]{0:T(1024)}) all-reduce(f32[256,4]{0,1:T(4,128)S(1)} %copy.219, f32[768]{0:T(1024)S(1)} %convert_reduce_fusion.3, f32[256]{0:T(256)S(1)} %dynamic_slice.15, f32[1024]{0:T(1024)S(1)} %copy-done.37), channel_id=1, replica_groups=mesh['fsdp'=8,'sp'=4] {'sp'}, use_global_device_ids=true, to_apply=%region_18.19 | all-reduce | flops 3072 | bytes 24576 | tf_op jit(solution)/shard_map/psum | solution.py:294
  (234 shorter events, 244.4 us)
Async XLA Ops:
  7.2 212.3 %copy-start = (bf16[768,2048]{1,0:T(8,128)(2,1)S(1)}, bf16[768,2048]{1,0:T(8,128)(2,1)}, u32[]{:S(2)}) copy-start(bf16[768,2048]{1,0:T(8,128)(2,1)} %param.21) | copy-start | bytes 9437188
  7.2 195.9 %all-gather.4.cloned.1.call-start = ((), (), s32[]{:S(2)}) async-start(), calls=%async_computation.13 | async-start | bytes 9437184 | tf_op jit(solution)/shard_map/all_gather | solution.py:190
  83.5 147.9 %all-gather.6.cloned.1.call-start = ((), (), s32[]{:S(2)}) async-start(), calls=%async_computation.15 | async-start | bytes 9437184 | tf_op jit(solution)/shard_map/all_gather | solution.py:190
  132.3 36.4 %copy-start.36 = (s32[1,1024]{1,0:T(1,128)S(1)}, s32[1,1024]{1,0:T(1,128)}, u32[]{:S(2)}) copy-start(s32[1,1024]{1,0:T(1,128)} %param.16) | copy-start | bytes 12292
  164.4 36.5 %all-to-all-start.2 = ((bf16[256,8,256]{0,2,1:T(8,128)(2,1)}), bf16[256,8,256]{0,2,1:T(8,128)(2,1)}, u32[]{:S(2)}, u32[]{:S(2)}) async-start(bf16[256,8,256]{0,2,1:T(8,128)(2,1)} %bitcast.204), calls=%async_computation.2 | async-start | bytes 2097152 | tf_op jit(solution)/shard_map/all_to_all | solution.py:228
  168.7 525.4 %reduce-scatter.8.cloned.1.call-start = ((), (), s32[]{:S(2)}) async-start(), calls=%async_computation.16 | async-start | bytes 9437184 | tf_op jit(solution)/shard_map/reduce_scatter | solution.py:194
  363.8 410.5 %reduce-scatter.6.cloned.1.call-start = ((), (), s32[]{:S(2)}) async-start(), calls=%async_computation.14 | async-start | bytes 9437184 | tf_op jit(solution)/shard_map/reduce_scatter | solution.py:194
  373.6 21.4 %copy-start.40 = (bf16[1024,2048]{1,0:T(8,128)(2,1)S(1)}, bf16[1024,2048]{1,0:T(8,128)(2,1)}, u32[]{:S(2)}) copy-start(bf16[1024,2048]{1,0:T(8,128)(2,1)} %param.27) | copy-start | bytes 12582916
  373.6 21.4 %copy-start.41 = (bf16[2048,1024]{1,0:T(8,128)(2,1)S(1)}, bf16[2048,1024]{1,0:T(8,128)(2,1)}, u32[]{:S(2)}) copy-start(bf16[2048,1024]{1,0:T(8,128)(2,1)} %get-tuple-element.59) | copy-start | bytes 12582916
  389.4 94.8 %collective-permute-start.6 = (bf16[1024,2048]{1,0:T(8,128)(2,1)}, bf16[1024,2048]{1,0:T(8,128)(2,1)}, u32[]{:S(2)}, u32[]{:S(2)}) collective-permute-start(bf16[1024,2048]{1,0:T(8,128)(2,1)} %reduce-precision_convert_fusion.7), channel_id=1, source_target_pairs={{0,1},{3,2},{4,5},{7,6},{8,9},{11,10},{12,13},{15,14},{16,17},{19,... | collective-permute-start | bytes 12582920 | tf_op jit(solution)/shard_map/ppermute | solution.py:141
  433.2 140.9 %collective-permute-start.9 = (bf16[1024,2048]{1,0:T(8,128)(2,1)}, bf16[1024,2048]{1,0:T(8,128)(2,1)}, u32[]{:S(2)}, u32[]{:S(2)}) collective-permute-start(bf16[1024,2048]{1,0:T(8,128)(2,1)} %reduce-precision_convert_fusion.4), channel_id=1, source_target_pairs={{0,1},{3,2},{4,5},{7,6},{8,9},{11,10},{12,13},{15,14},{16,17},{19,... | collective-permute-start | bytes 12582920 | tf_op jit(solution)/shard_map/ppermute | solution.py:141
  442.7 52.1 %slice-start.2 = ((s8[8388608]{0:T(1024)(128)(4,1)}), s8[4194304]{0:T(1024)(128)(4,1)S(1)}, s32[]{:S(2)}) async-start(s8[8388608]{0:T(1024)(128)(4,1)} %bitcast.177), calls=%async_computation.20 | async-start | bytes 8388608
  442.8 52.1 %slice-start.3 = ((s8[8388608]{0:T(1024)(128)(4,1)}), s8[4194304]{0:T(1024)(128)(4,1)S(1)}, s32[]{:S(2)}) async-start(s8[8388608]{0:T(1024)(128)(4,1)} %bitcast.177), calls=%async_computation.21 | async-start | bytes 8388608
  451.1 189.8 %collective-permute-start = (bf16[768,2048]{1,0:T(8,128)(2,1)}, bf16[768,2048]{1,0:T(8,128)(2,1)}, u32[]{:S(2)}, u32[]{:S(2)}) collective-permute-start(bf16[768,2048]{1,0:T(8,128)(2,1)} %reduce-precision_convert_fusion.10), channel_id=1, source_target_pairs={{0,1},{3,2},{4,5},{7,6},{8,9},{11,10},{12,13},{15,14},{16,17},{19,... | collective-permute-start | bytes 9437192 | tf_op jit(solution)/shard_map/ppermute | solution.py:141
  492.1 185.5 %collective-permute-start.7 = (bf16[1024,2048]{1,0:T(8,128)(2,1)}, bf16[1024,2048]{1,0:T(8,128)(2,1)}, u32[]{:S(2)}, u32[]{:S(2)}) collective-permute-start(bf16[1024,2048]{1,0:T(8,128)(2,1)} %reduce-precision_convert_fusion.6), channel_id=1, source_target_pairs={{1,2},{2,1},{5,6},{6,5},{9,10},{10,9},{13,14},{14,13},{17,18},{18,... | collective-permute-start | bytes 12582920 | tf_op jit(solution)/shard_map/ppermute | solution.py:143
  498.2 151.1 %all-to-all-start.9 = ((bf16[8,256,256]{1,2,0:T(8,128)(2,1)}), bf16[8,256,256]{1,2,0:T(8,128)(2,1)S(1)}, u32[]{:S(2)}, u32[]{:S(2)}) async-start(bf16[8,256,256]{1,2,0:T(8,128)(2,1)} %bitcast.164), calls=%async_computation.11 | async-start | bytes 2097152 | tf_op jit(solution)/shard_map/all_to_all | solution.py:279
  581.8 73.1 %copy-start.5 = (bf16[1,256,2048]{2,1,0:T(8,128)(2,1)S(1)}, bf16[1,256,2048]{2,1,0:T(8,128)(2,1)}, u32[]{:S(2)}) copy-start(bf16[1,256,2048]{2,1,0:T(8,128)(2,1)} %param.15) | copy-start | bytes 3145732
  581.8 179.4 %collective-permute-start.10 = (bf16[1024,2048]{1,0:T(8,128)(2,1)}, bf16[1024,2048]{1,0:T(8,128)(2,1)}, u32[]{:S(2)}, u32[]{:S(2)}) collective-permute-start(bf16[1024,2048]{1,0:T(8,128)(2,1)} %reduce-precision_convert_fusion.3), channel_id=1, source_target_pairs={{1,2},{2,1},{5,6},{6,5},{9,10},{10,9},{13,14},{14,13},{17,18},{18,... | collective-permute-start | bytes 12582920 | tf_op jit(solution)/shard_map/ppermute | solution.py:143
  647.0 39.6 %collective-permute-start.1 = (bf16[768,2048]{1,0:T(8,128)(2,1)}, bf16[768,2048]{1,0:T(8,128)(2,1)}, u32[]{:S(2)}, u32[]{:S(2)}) collective-permute-start(bf16[768,2048]{1,0:T(8,128)(2,1)} %reduce-precision_convert_fusion.9), channel_id=1, source_target_pairs={{1,2},{2,1},{5,6},{6,5},{9,10},{10,9},{13,14},{14,13},{17,18},{18,... | collective-permute-start | bytes 9437192 | tf_op jit(solution)/shard_map/ppermute | solution.py:143
  650.1 26.4 %collective-permute-start.3 = (bf16[256,2048]{1,0:T(8,128)(2,1)S(1)}, bf16[256,2048]{1,0:T(8,128)(2,1)S(1)}, u32[]{:S(2)}, u32[]{:S(2)}) collective-permute-start(bf16[256,2048]{1,0:T(8,128)(2,1)S(1)} %copy.206), channel_id=1, source_target_pairs={{0,1},{3,2},{4,5},{7,6},{8,9},{11,10},{12,13},{15,14},{16,17},{19,... | collective-permute-start | bytes 3145736 | tf_op jit(solution)/shard_map/ppermute | solution.py:141
  676.9 93.4 %collective-permute-start.4 = (bf16[256,2048]{1,0:T(8,128)(2,1)S(1)}, bf16[256,2048]{1,0:T(8,128)(2,1)S(1)}, u32[]{:S(2)}, u32[]{:S(2)}) collective-permute-start(bf16[256,2048]{1,0:T(8,128)(2,1)S(1)} %reduce-precision_convert_fusion.12), channel_id=1, source_target_pairs={{1,2},{2,1},{5,6},{6,5},{9,10},{10,9},{13,14},{14,13},{17,18},{18,... | collective-permute-start | bytes 3145736 | tf_op jit(solution)/shard_map/ppermute | solution.py:143
  685.3 334.4 %collective-permute-start.8 = (bf16[1024,2048]{1,0:T(8,128)(2,1)}, bf16[1024,2048]{1,0:T(8,128)(2,1)}, u32[]{:S(2)}, u32[]{:S(2)}) collective-permute-start(bf16[1024,2048]{1,0:T(8,128)(2,1)} %reduce-precision_convert_fusion.5), channel_id=1, source_target_pairs={{1,0},{2,3},{5,4},{6,7},{9,8},{10,11},{13,12},{14,15},{17,16},{18,... | collective-permute-start | bytes 12582920 | tf_op jit(solution)/shard_map/ppermute | solution.py:145
  692.7 322.0 %collective-permute-start.2 = (bf16[768,2048]{1,0:T(8,128)(2,1)}, bf16[768,2048]{1,0:T(8,128)(2,1)}, u32[]{:S(2)}, u32[]{:S(2)}) collective-permute-start(bf16[768,2048]{1,0:T(8,128)(2,1)} %reduce-precision_convert_fusion.8), channel_id=1, source_target_pairs={{1,0},{2,3},{5,4},{6,7},{9,8},{10,11},{13,12},{14,15},{17,16},{18,... | collective-permute-start | bytes 9437192 | tf_op jit(solution)/shard_map/ppermute | solution.py:145
  697.3 170.4 %all-to-all-start.7 = ((bf16[2,128,2048]{2,0,1:T(2,128)(2,1)}), bf16[2,128,2048]{2,0,1:T(2,128)(2,1)}, u32[]{:S(2)}, u32[]{:S(2)}) async-start(bf16[2,128,2048]{2,0,1:T(2,128)(2,1)} %copy.202), calls=%async_computation.9 | async-start | bytes 2097152 | tf_op jit(solution)/shard_map/all_to_all | solution.py:195
  761.1 116.5 %reduce-scatter.10.cloned.1.call-start = ((), (), s32[]{:S(2)}) async-start(), calls=%async_computation.17 | async-start | bytes 1179648
  768.9 265.4 %collective-permute-start.11 = (bf16[1024,2048]{1,0:T(8,128)(2,1)}, bf16[1024,2048]{1,0:T(8,128)(2,1)}, u32[]{:S(2)}, u32[]{:S(2)}) collective-permute-start(bf16[1024,2048]{1,0:T(8,128)(2,1)} %reduce-precision_convert_fusion.2), channel_id=1, source_target_pairs={{1,0},{2,3},{5,4},{6,7},{9,8},{10,11},{13,12},{14,15},{17,16},{18,... | collective-permute-start | bytes 12582920 | tf_op jit(solution)/shard_map/ppermute | solution.py:145
  771.6 234.2 %collective-permute-start.5 = (bf16[256,2048]{1,0:T(8,128)(2,1)}, bf16[256,2048]{1,0:T(8,128)(2,1)}, u32[]{:S(2)}, u32[]{:S(2)}) collective-permute-start(bf16[256,2048]{1,0:T(8,128)(2,1)} %reduce-precision_convert_fusion.11), channel_id=1, source_target_pairs={{1,0},{2,3},{5,4},{6,7},{9,8},{10,11},{13,12},{14,15},{17,16},{18,... | collective-permute-start | bytes 3145736 | tf_op jit(solution)/shard_map/ppermute | solution.py:145
  774.3 102.7 %copy-start.4 = (bf16[2,4,8,32,768]{4,3,2,1,0:T(8,128)(2,1)S(1)}, bf16[2,4,8,32,768]{4,3,2,1,0:T(8,128)(2,1)}, u32[]{:S(2)}) copy-start(bf16[2,4,8,32,768]{4,3,2,1,0:T(8,128)(2,1)} %concatenate.117) | copy-start | bytes 9437188
  867.7 143.4 %all-to-all-start.3 = ((bf16[2,128,2048]{2,0,1:T(2,128)(2,1)}), bf16[2,128,2048]{2,0,1:T(2,128)(2,1)}, u32[]{:S(2)}, u32[]{:S(2)}) async-start(bf16[2,128,2048]{2,0,1:T(2,128)(2,1)} %copy.186), calls=%async_computation.4 | async-start | bytes 2097152 | tf_op jit(solution)/shard_map/all_to_all | solution.py:195
  1005.2 49.4 %copy-start.38 = (f32[256]{0:T(256)}, f32[256]{0:T(256)S(1)}, u32[]{:S(2)}) copy-start(f32[256]{0:T(256)S(1)} %get-tuple-element.92) | copy-start | bytes 3076
  1011.2 18.9 %all-to-all-start.8 = ((bf16[8,32,2048]{2,1,0:T(8,128)(2,1)}), bf16[8,32,2048]{2,1,0:T(8,128)(2,1)S(1)}, u32[]{:S(2)}, u32[]{:S(2)}) async-start(bf16[8,32,2048]{2,1,0:T(8,128)(2,1)} %bitcast.55), calls=%async_computation.10 | async-start | bytes 2097152 | tf_op jit(solution)/shard_map/all_to_all | solution.py:196
  1030.1 19.7 %all-to-all-start.4 = ((bf16[8,32,2048]{2,1,0:T(8,128)(2,1)}), bf16[8,32,2048]{2,1,0:T(8,128)(2,1)}, u32[]{:S(2)}, u32[]{:S(2)}) async-start(bf16[8,32,2048]{2,1,0:T(8,128)(2,1)} %bitcast.27), calls=%async_computation.5 | async-start | bytes 2097152 | tf_op jit(solution)/shard_map/all_to_all | solution.py:196
  (37 other events, 272.3 us)
Sparse Core Ops, SparseCore 0:
  83.7 59.1 all-gather.3
  162.2 62.2 all-gather.5
  364.0 71.4 reduce-scatter.7
  439.7 78.5 reduce-scatter.5
  774.4 44.9 reduce-scatter.9

commit v2 on v1

--- a/solution.py
+++ b/solution.py
@@ -3,7 +3,11 @@
 import jax
 import jax.numpy as jnp
 from jax import lax
+from jax.experimental import pallas as pl
+from jax.experimental.pallas import tpu as pltpu
 from jax.sharding import PartitionSpec as P
+
+MESH = pl.DeviceIdType.MESH
 
 HEADS = 8
 HEAD_DIM = 256
@@ -153,6 +157,135 @@
     if lax.axis_size("sp") == 4:
         return sum_over_line(partial)
     return lax.psum(partial, "sp").astype(jnp.float32)
+
+
+def gather_kernel(x_ref, c_ref, xg_ref, cg_ref, held, s1, r1, s2, r2, s3, r3, local):
+    f, s = lax.axis_index("fsdp"), lax.axis_index("sp")
+    core, col, row = f % 2, (f // 2) % 2, f // 4
+    f_x, f_y, f_c = f + 2 - 4 * col, f + 4 - 8 * row, f + 1 - 2 * core
+    f_d = f_x + 4 - 8 * row
+    piece = xg_ref.shape[3]
+    barrier = pltpu.get_barrier_semaphore()
+    for k in range(1, 8):
+        pl.semaphore_signal(barrier, inc=1, device_id=((f + k) % 8, s), device_id_type=MESH)
+    for k in range(1, 4):
+        pl.semaphore_signal(barrier, inc=1, device_id=(f, (s + k) % 4), device_id_type=MESH)
+    pl.semaphore_wait(barrier, 10)
+    pairs = ((x_ref, xg_ref), (c_ref, cg_ref))
+    sent = []
+
+    def send(src, dst, send_sem, recv_sem, device):
+        copy = pltpu.make_async_remote_copy(
+            src_ref=src, dst_ref=dst, send_sem=send_sem, recv_sem=recv_sem,
+            device_id=device, device_id_type=MESH,
+        )
+        copy.start()
+        sent.append(copy)
+
+    def arrived(ref, recv_sem):
+        pltpu.make_async_remote_copy(
+            src_ref=ref, dst_ref=ref, send_sem=s1.at[0, 0], recv_sem=recv_sem,
+            device_id=(f_c, s), device_id_type=MESH,
+        ).wait_recv()
+
+    kept = []
+    for a, (src, _) in enumerate(pairs):
+        own = pltpu.make_async_copy(src.at[pl.ds(f * piece, piece)], held.at[a, f], local.at[a, 0])
+        own.start()
+        kept.append(own)
+        for k in range(1, 8):
+            j = (f + k) % 8
+            send(src.at[pl.ds(j * piece, piece)], held.at[a, f], s1.at[a, k], r1.at[a, k], (j, s))
+
+    def to_planes(a):
+        out = pairs[a][1]
+        kept[a].wait()
+        for k in range(1, 8):
+            arrived(held.at[a, (f + 8 - k) % 8], r1.at[a, k])
+        for k in range(1, 4):
+            plane = (s + k) % 4
+            send(held.at[a, pl.ds(2 * plane, 2)], out.at[:, s, f], s2.at[a, k], r2.at[a, k], (f, plane))
+        own = pltpu.make_async_copy(held.at[a, pl.ds(2 * s, 2)], out.at[:, s, f], local.at[a, 1])
+        own.start()
+        return own
+
+    def spread(a, k):
+        out = pairs[a][1]
+        z = (s + 4 - k) % 4
+        if k:
+            arrived(out.at[:, z, f], r2.at[a, k])
+        ref = out.at[:, z, f]
+        send(ref, ref, s3.at[a, 0, k], r3.at[a, 0, k], (f_x, s))
+        send(ref, ref, s3.at[a, 1, k], r3.at[a, 1, k], (f_y, s))
+        send(ref, ref, s3.at[a, 2, k], r3.at[a, 2, k], (f_c, s))
+
+    def pass_on(a, k):
+        out = pairs[a][1]
+        z = (s + 4 - k) % 4
+        ref = out.at[:, z, f_x]
+        arrived(ref, r3.at[a, 0, k])
+        send(out.at[0, z, f_x], out.at[0, z, f_x], s3.at[a, 5, k], r3.at[a, 5, k], (f_y, s))
+        send(ref, ref, s3.at[a, 3, k], r3.at[a, 3, k], (f_c, s))
+        ref = out.at[:, z, f_y]
+        arrived(ref, r3.at[a, 1, k])
+        send(out.at[1, z, f_y], out.at[1, z, f_y], s3.at[a, 6, k], r3.at[a, 6, k], (f_x, s))
+        send(ref, ref, s3.at[a, 4, k], r3.at[a, 4, k], (f_c, s))
+
+    def pass_corner(a, k):
+        out = pairs[a][1]
+        z = (s + 4 - k) % 4
+        for half in range(2):
+            ref = out.at[half, z, f_d]
+            arrived(ref, r3.at[a, 5 + half, k])
+            send(ref, ref, s3.at[a, 7 + half, k], r3.at[a, 7 + half, k], (f_c, s))
+
+    def from_core(a, k):
+        out = pairs[a][1]
+        z = (s + 4 - k) % 4
+        g_x, g_y = f_c + 2 - 4 * col, f_c + 4 - 8 * row
+        g_d = g_x + 4 - 8 * row
+        arrived(out.at[:, z, f_c], r3.at[a, 2, k])
+        arrived(out.at[:, z, g_x], r3.at[a, 3, k])
+        arrived(out.at[:, z, g_y], r3.at[a, 4, k])
+        for half in range(2):
+            arrived(out.at[half, z, g_d], r3.at[a, 7 + half, k])
+
+    own0 = to_planes(0)
+    own1 = to_planes(1)
+    steps = [(a, k) for a in range(2) for k in range(4)]
+    for i in range(len(steps) + 2):
+        if i < len(steps):
+            a, k = steps[i]
+            if k == 0:
+                (own0 if a == 0 else own1).wait()
+            spread(a, k)
+        if 0 <= i - 1 < len(steps):
+            pass_on(*steps[i - 1])
+        if 0 <= i - 2 < len(steps):
+            pass_corner(*steps[i - 2])
+    for a, k in steps:
+        from_core(a, k)
+    for copy in sent:
+        copy.wait_send()
+
+
+def gather_both(x, c):
+    rows, width = x.shape
+    piece = rows // 8
+    shape = jax.ShapeDtypeStruct((2, 4, 8, piece, width), x.dtype)
+    dma = pltpu.SemaphoreType.DMA
+    return pl.pallas_call(
+        gather_kernel,
+        out_shape=(shape, shape),
+        in_specs=[pl.BlockSpec(memory_space=pl.ANY)] * 2,
+        out_specs=[pl.BlockSpec(memory_space=pl.ANY)] * 2,
+        scratch_shapes=[
+            pltpu.VMEM((2, 8, piece, width), x.dtype),
+            dma((2, 8)), dma((2, 8)), dma((2, 4)), dma((2, 4)), dma((2, 9, 4)), dma((2, 9, 4)), dma((2, 2)),
+        ],
+        compiler_params=pltpu.CompilerParams(collective_id=1, has_side_effects=True),
+        name="gather_tokens",
+    )(x, c)
 
 
 def per_device(
@@ -187,10 +320,10 @@
     def gather_tokens(block):
         part = lax.all_to_all(block, "fsdp", split_axis=1, concat_axis=0, tiled=True)
         part = lax.all_to_all(part, "sp", split_axis=0, concat_axis=1, tiled=True)
-        return lax.all_gather(part, "fsdp", axis=0, tiled=True).reshape(tokens, width)
+        return in_order(lax.all_gather(part, "fsdp", axis=0, tiled=True)).reshape(tokens, width)
 
     def scatter_tokens(partial):
-        part = partial.reshape(nf * group, ns * piece, width)
+        part = out_of_order(partial).reshape(nf * group, ns * piece, width)
         part = lax.psum_scatter(part, "fsdp", scatter_dimension=0, tiled=True)
         part = lax.all_to_all(part, "sp", split_axis=1, concat_axis=0, tiled=True)
         return lax.all_to_all(part, "fsdp", split_axis=0, concat_axis=1, tiled=True)
@@ -220,8 +353,12 @@
         share = vector.shape[0] // nf
         return lax.dynamic_slice_in_dim(vector, f_place * share, share, 0)
 
-    gathered = gather_tokens(hidden_in)
-    upstream = gather_tokens(cotangent)
+    if (nf, ns, seq_local) == (8, 4, 1):
+        gathered, upstream = (
+            array.reshape(tokens, width) for array in gather_both(hidden_in[0], cotangent[0])
+        )
+    else:
+        gathered, upstream = gather_tokens(hidden_in), gather_tokens(cotangent)
     rows = lax.all_gather(segments, "fsdp", axis=0, tiled=True)
     rows = lax.dynamic_slice_in_dim(rows, s_place * group, group, 0)
 
@@ -245,7 +382,7 @@
     mlp_norm_grad = times(hidden_grad, w_up)
 
     packed = (times_transposed(normed, head_qkv) + head_bias).astype(jnp.bfloat16)
-    packed = in_order(packed).reshape(group, seq_len, head_count, 3 * HEAD_DIM)
+    packed = packed.reshape(group, seq_len, head_count, 3 * HEAD_DIM)
     cos_table, sin_table = rotary_tables(rows)
     queries = rotate(packed[..., :HEAD_DIM].astype(jnp.float32), cos_table, sin_table).astype(
         jnp.bfloat16
@@ -256,9 +393,9 @@
     values = packed[..., 2 * HEAD_DIM :]
     mask = build_mask(rows)
     context, log_total = attend_forward(queries, keys_rot, values, mask)
-    context = own_columns(out_of_order(context))
+    context = own_columns(context.reshape(tokens, -1))
     partial_out = times_transposed(context, dense_in) + times(activated, w_down)
-    context_grad = in_order(times(upstream, head_dense).astype(jnp.bfloat16)).reshape(
+    context_grad = times(upstream, head_dense).astype(jnp.bfloat16).reshape(
         group, seq_len, head_count, HEAD_DIM
     )
     query_grad, key_grad, value_grad = attend_backward(
@@ -272,7 +409,7 @@
         ],
         axis=-1,
     ).astype(jnp.bfloat16)
-    packed_grad = own_columns(out_of_order(packed_grad))
+    packed_grad = own_columns(packed_grad.reshape(tokens, -1))
     attn_norm_grad = times(packed_grad, w_qkv)
     qkv_term = contract_rows(packed_grad, normed)
     dense_term = contract_rows(upstream, context).astype(jnp.bfloat16)

time: 1070 us -> 1000 us (0.935)
  blocking collectives: 257 us -> 100 us
  Pallas kernels: 0 us -> 107 us
  local copies, waits for them, and re-layouts: 79.8 us -> 58.4 us
  other arithmetic: 151 us -> 133 us
  waiting for transfers between devices: 276 us -> 291 us
    pallas_call x0 -> x1, Pallas kernels: none -> 107 us  [gather_both(): pl.pallas_call(gather_kernel, out_shape=(shape, shape), in_specs=[pl.Bloc...]
    all_to_all x4 -> x0, blocking collectives: 104 us -> none  [the longest x2 56.6 us: gather_tokens(): part = lax.all_to_all(part, 'sp', split_axis=0, concat_axis=1, tiled=True)]
    unnamed x6 -> x4, waiting for transfers between devices: 0.08 us -> 36.7 us
    psum x1, blocking collectives: 127 us -> 91.1 us  [per_device(): lax.psum((vectors, bias_out, bias_qkv, bias_up), 'sp')]
    unnamed x107 -> x100, local copies, waits for them, and re-layouts: 39.6 us -> 10.4 us
    ppermute x4, waiting for transfers between devices: 180 us -> 157 us  [sum_over_line(): inward = lax.ppermute(partial, 'sp', [(0, 1), (3, 2)])]
    all_gather x1, blocking collectives: 26.7 us -> 9.19 us  [per_device(): rows = lax.all_gather(segments, 'fsdp', axis=0, tiled=True)]
    unnamed x6 -> x4, other arithmetic: 18.4 us -> 1.45 us
  transfers between devices with their start and end apart: 23 -> 21, of which waited for: 7 -> 8; matrix products, arithmetic and copies ran while one was open for 22% -> 27% of each run, Pallas kernels for 0% -> 11%
where the time goes in v2:
time: 1000 us; the launch traced here: 993 us
  waiting for transfers between devices  291 us (29%)
  matrix products  169 us (17%)
  other arithmetic  133 us (13%)
  starting transfers between devices  118 us (12%)
  Pallas kernels  107 us (11%)
  blocking collectives  100 us (10%)
  local copies, waits for them, and re-layouts  58.4 us (6%)
  between operations  15 us (2%)
    ppermute x4, waiting for transfers between devices, sum_over_line(): inward = lax.ppermute(partial, 'sp', [(0, 1), (3, 2)])  157 us
    pallas_call x1, Pallas kernels, gather_both(): pl.pallas_call(gather_kernel, out_shape=(shape, shape), in_specs=[pl.Bloc...  107 us
    all_to_all x2, waiting for transfers between devices, scatter_tokens(): part = lax.all_to_all(part, 'sp', split_axis=1, concat_axis=0, tiled=True)  91.6 us
    psum x1, blocking collectives, per_device(): lax.psum((vectors, bias_out, bias_qkv, bias_up), 'sp')  91.1 us
    all_to_all x2, starting transfers between devices, scatter_tokens(): part = lax.all_to_all(part, 'sp', split_axis=1, concat_axis=0, tiled=True)  67.3 us
    dot_general x4, matrix products, times(): return jnp.dot(former, latter, preferred_element_type=jnp.float32)  51.9 us
    dot_general x4, matrix products, times_transposed(): lax.dot_general(former, latter, (((1,), (1,)), ((), ())), preferred_eleme...  50.3 us
    convert_element_type x8, other arithmetic, rounded(): lax.reduce_precision(array.astype(jnp.float32), 8, 7).astype(jnp.bfloat16)  44.1 us
  transfers between devices with their start and end apart: 21, of which 8 were waited for; matrix products, arithmetic and copies ran while one was open for 27% of the time, Pallas kernels for 11%

profile of v2, /device:TPU:0, one launch (start us, length us, event | category | flops | bytes accessed | tf_op | source)
XLA Modules:
  0.0 992.6 jit_solution(6389223373730351314)
XLA Ops:
  16.1 107.4 %gather_tokens.1 = (bf16[2,4,8,32,2048]{4,3,2,1,0:T(8,128)(2,1)}, bf16[2,4,8,32,2048]{4,3,2,1,0:T(8,128)(2,1)}) custom-call(bf16[256,2048]{1,0:T(8,128)(2,1)} %bitcast.149, bf16[256,2048]{1,0:T(8,128)(2,1)} %bitcast.171), custom_call_target="tpu_custom_call" | custom-call | tf_op jit(solution)/shard_map/gather_tokens/pallas_call | solution.py:277
  134.9 9.6 add_convert_fusion.1
  144.5 6.9 add_convert_fusion.2
  156.2 9.2 all-gather
  167.4 15.9 %multiply_convert_fusion.1 = (bf16[2048,1024]{1,0:T(8,128)(2,1)}, f32[2048,1024]{1,0:T(8,128)}) fusion(f32[1024]{0:T(1024)S(1)} %dynamic_slice.14, bf16[2048,2048]{1,0:T(8,128)(2,1)} %get-tuple-element.30, bf16[1024,2048]{1,0:T(8,128)(2,1)} %param.25), kind=kOutput, calls=%fused_computation.28 | convolution fusion | flops 8602517504 | bytes 25169920 | tf_op jit(solution)/shard_map/dot_general | solution.py:35
  183.3 15.8 %convert_reduce_fusion.2 = (f32[1024]{0:T(1024)}, bf16[2048,1024]{1,0:T(8,128)(2,1)S(1)}) fusion(f32[2048,1024]{1,0:T(8,128)} %get-tuple-element.60, f32[1024]{0:T(1024)S(1)} %dynamic_slice.14, bf16[2048,2048]{1,0:T(8,128)(2,1)} %bitcast.152, bf16[1024,2048]{1,0:T(8,128)(2,1)S(1)} %copy-done.43), kind=kOutput, calls=%fused_computation.21 | convolution fusion | flops 8617196544 | bytes 25174016 | tf_op jit(solution)/shard_map/dot_general | solution.py:35
  199.1 12.1 %fusion.58 = f32[2048,2048]{1,0:T(8,128)} fusion(bf16[2048,1024]{1,0:T(8,128)(2,1)S(1)} %get-tuple-element.62, bf16[1024,2048]{1,0:T(8,128)(2,1)S(1)} %copy-done.42), kind=kOutput, calls=%fused_computation.143 | convolution fusion | flops 8589934592 | bytes 25165824 | tf_op jit(solution)/shard_map/dot_general | solution.py:41
  272.1 7.0 concatenate.117
  279.0 17.9 %multiply_reduce_fusion.1 = (f32[2048]{0:T(1024)S(1)}, f32[2048]{0:T(1024)S(1)}, f32[2048]{0:T(1024)S(1)}, f32[2048]{0:T(1024)S(1)}, bf16[2048,2048]{1,0:T(8,128)(2,1)}) fusion(bf16[2,4,8,32,2048]{4,3,2,1,0:T(8,128)(2,1)} %get-tuple-element.16, f32[2048]{0:T(1024)S(1)} %rsqrt.20, f32[2048]{0:T(1024)S(1)} %div.48, f32[2048,2048]{1,0:T(8,128)} %fusion.58, ...), kind=kOutput, calls=%fused_computation.4 | convolution fusion | flops 6501163008 | bytes 39911424 | tf_op jit(solution)/shard_map/dot_general | solution.py:41
  297.0 8.3 copy.92
  305.3 14.1 %reduce-precision_convert_fusion.7 = bf16[1024,2048]{1,0:T(8,128)(2,1)} fusion(bf16[2048,1024]{1,0:T(8,128)(2,1)} %copy-done.44, bf16[2048,2048]{1,0:T(8,128)(2,1)} %get-tuple-element.30), kind=kOutput, calls=%fused_computation.24 | convolution fusion | flops 8594128896 | bytes 16777216 | tf_op jit(solution)/shard_map/dot_general | solution.py:29
  319.5 7.3 collective-permute-start.6
  326.8 7.6 fusion.31
  335.4 15.8 %fusion.57 = f32[2048,2048]{1,0:T(8,128)} fusion(bf16[2048,1024]{1,0:T(8,128)(2,1)} %get-tuple-element.59, bf16[1024,2048]{1,0:T(8,128)(2,1)} %param.27), kind=kOutput, calls=%fused_computation.142 | convolution fusion | flops 8589934592 | bytes 25165824 | tf_op jit(solution)/shard_map/dot_general | solution.py:41
  351.1 11.7 %reduce-precision_convert_fusion.1 = bf16[2048,2048]{1,0:T(8,128)(2,1)} fusion(f32[2048,2048]{1,0:T(8,128)} %fusion.57, bf16[2048,256]{1,0:T(8,128)(2,1)S(1)} %bitcast.174, bf16[2048,256]{1,0:T(8,128)(2,1)S(1)} %bitcast.173), kind=kOutput, calls=%fused_computation.6 | convolution fusion | flops 2160066560 | bytes 27262976 | tf_op jit(solution)/shard_map/dot_general | solution.py:35
  362.9 8.5 copy.79
  371.4 14.2 %reduce-precision_convert_fusion.4 = bf16[1024,2048]{1,0:T(8,128)(2,1)} fusion(bf16[2048,1024]{1,0:T(8,128)(2,1)} %get-tuple-element.59, bf16[2048,2048]{1,0:T(8,128)(2,1)} %bitcast.154), kind=kOutput, calls=%fused_computation.20 | convolution fusion | flops 8594128896 | bytes 16777216 | tf_op jit(solution)/shard_map/dot_general | solution.py:29
  389.2 11.4 %reduce-precision_convert_fusion.10 = bf16[768,2048]{1,0:T(8,128)(2,1)} fusion(bf16[2048,768]{1,0:T(8,128)(2,1)S(1)} %copy-done.13, bf16[2048,2048]{1,0:T(8,128)(2,1)} %copy-done.18), kind=kOutput, calls=%fused_computation.38 | convolution fusion | flops 6445596672 | bytes 14680064 | tf_op jit(solution)/shard_map/dot_general | solution.py:29
  403.6 12.4 %collective-permute-done.6 = bf16[1024,2048]{1,0:T(8,128)(2,1)} collective-permute-done((bf16[1024,2048]{1,0:T(8,128)(2,1)}, bf16[1024,2048]{1,0:T(8,128)(2,1)}, u32[]{:S(2)}, u32[]{:S(2)}) %collective-permute-start.6) | collective-permute-done | bytes 4194336 | tf_op jit(solution)/shard_map/ppermute | solution.py:145
  416.0 8.0 reduce-precision_convert_fusion.6
  434.5 71.4 %collective-permute-done.9 = bf16[1024,2048]{1,0:T(8,128)(2,1)} collective-permute-done((bf16[1024,2048]{1,0:T(8,128)(2,1)}, bf16[1024,2048]{1,0:T(8,128)(2,1)}, u32[]{:S(2)}, u32[]{:S(2)}) %collective-permute-start.9) | collective-permute-done | bytes 4194336 | tf_op jit(solution)/shard_map/ppermute | solution.py:145
  505.9 7.7 reduce-precision_convert_fusion.3
  516.3 56.5 %collective-permute-done = bf16[768,2048]{1,0:T(8,128)(2,1)} collective-permute-done((bf16[768,2048]{1,0:T(8,128)(2,1)}, bf16[768,2048]{1,0:T(8,128)(2,1)}, u32[]{:S(2)}, u32[]{:S(2)}) %collective-permute-start) | collective-permute-done | bytes 3145760 | tf_op jit(solution)/shard_map/ppermute | solution.py:145
  590.0 17.0 %collective-permute-done.3 = bf16[256,2048]{1,0:T(8,128)(2,1)S(1)} collective-permute-done((bf16[256,2048]{1,0:T(8,128)(2,1)S(1)}, bf16[256,2048]{1,0:T(8,128)(2,1)S(1)}, u32[]{:S(2)}, u32[]{:S(2)}) %collective-permute-start.3) | collective-permute-done | bytes 1048608 | tf_op jit(solution)/shard_map/ppermute | solution.py:145
  610.1 7.8 reduce-precision_convert_fusion.5
  628.8 63.0 %all-to-all-start.3 = ((bf16[2,128,2048]{2,0,1:T(2,128)(2,1)}), bf16[2,128,2048]{2,0,1:T(2,128)(2,1)S(1)}, u32[]{:S(2)}, u32[]{:S(2)}) async-start(bf16[2,128,2048]{2,0,1:T(2,128)(2,1)} %copy.93), calls=%async_computation.5 | async-start | bytes 2097152 | tf_op jit(solution)/shard_map/all_to_all | solution.py:328
  691.9 7.8 reduce-precision_convert_fusion.2
  707.9 91.6 %all-to-all-done.3 = bf16[2,128,2048]{2,0,1:T(2,128)(2,1)S(1)} async-done(((bf16[2,128,2048]{2,0,1:T(2,128)(2,1)}), bf16[2,128,2048]{2,0,1:T(2,128)(2,1)S(1)}, u32[]{:S(2)}, u32[]{:S(2)}) %all-to-all-start.3) | async-done | bytes 1048608 | tf_op jit(solution)/shard_map/all_to_all | solution.py:328
  808.2 36.7 %reduce-scatter.10.cloned.1.call-done = f32[256,4]{1,0:T(8,128)} async-done(((f32[2048,4]{1,0:T(8,128)}), f32[256,4]{1,0:T(8,128)}) %reduce-scatter.10.cloned.1.call-update) | async-done | bytes 4112
  845.8 91.1 %all-reduce.1 = (f32[256,4]{0,1:T(4,128)S(1)}, f32[768]{0:T(1024)}, f32[256]{0:T(256)S(1)}, f32[1024]{0:T(1024)}) all-reduce(f32[256,4]{0,1:T(4,128)S(1)} %copy.108, f32[768]{0:T(1024)S(1)} %convert_reduce_fusion.3, f32[256]{0:T(256)S(1)} %dynamic_slice.15, f32[1024]{0:T(1024)S(1)} %copy-done.40), channel_id=1, replica_groups=mesh['fsdp'=8,'sp'=4] {'sp'}, use_global_device_ids=true, to_apply=%region_18.19 | all-reduce | flops 3072 | bytes 24576 | tf_op jit(solution)/shard_map/psum | solution.py:431
  950.2 6.1 select_convert_fusion.1
  964.8 6.1 select_convert_fusion
  (211 shorter events, 193.9 us)
Async XLA Ops:
  7.2 137.3 %copy-start = (bf16[768,2048]{1,0:T(8,128)(2,1)S(1)}, bf16[768,2048]{1,0:T(8,128)(2,1)}, u32[]{:S(2)}) copy-start(bf16[768,2048]{1,0:T(8,128)(2,1)} %param.21) | copy-start | bytes 9437188
  9.6 217.8 %all-to-all-start = ((bf16[256,8,256]{0,2,1:T(8,128)(2,1)}), bf16[256,8,256]{0,2,1:T(8,128)(2,1)}, u32[]{:S(2)}, u32[]{:S(2)}) async-start(bf16[256,8,256]{0,2,1:T(8,128)(2,1)} %bitcast.168), calls=%async_computation | async-start | bytes 2097152 | tf_op jit(solution)/shard_map/all_to_all | solution.py:365
  14.8 610.8 %reduce-scatter.8.cloned.1.call-start = ((), (), s32[]{:S(2)}) async-start(), calls=%async_computation.10 | async-start | bytes 9437184 | tf_op jit(solution)/shard_map/reduce_scatter | solution.py:327
  167.4 15.9 %copy-start.43 = (bf16[1024,2048]{1,0:T(8,128)(2,1)S(1)}, bf16[1024,2048]{1,0:T(8,128)(2,1)}, u32[]{:S(2)}) copy-start(bf16[1024,2048]{1,0:T(8,128)(2,1)} %param.27) | copy-start | bytes 12582916
  305.3 21.5 %copy-start.17 = (pred[1024,1024]{0,1:T(8,128)(4,1)S(1)}, pred[1024,1024]{0,1:T(8,128)(4,1)}, u32[]{:S(2)}) copy-start(pred[1024,1024]{0,1:T(8,128)(4,1)} %iota_compare_fusion) | copy-start | bytes 3145732
  305.3 399.3 %reduce-scatter.6.cloned.1.call-start = ((), (), s32[]{:S(2)}) async-start(), calls=%async_computation.9 | async-start | bytes 9437184 | tf_op jit(solution)/shard_map/reduce_scatter | solution.py:327
  319.5 96.6 %collective-permute-start.6 = (bf16[1024,2048]{1,0:T(8,128)(2,1)}, bf16[1024,2048]{1,0:T(8,128)(2,1)}, u32[]{:S(2)}, u32[]{:S(2)}) collective-permute-start(bf16[1024,2048]{1,0:T(8,128)(2,1)} %reduce-precision_convert_fusion.7), channel_id=1, source_target_pairs={{0,1},{3,2},{4,5},{7,6},{8,9},{11,10},{12,13},{15,14},{16,17},{19,... | collective-permute-start | bytes 12582920 | tf_op jit(solution)/shard_map/ppermute | solution.py:145
  371.4 17.8 %copy-start.13 = (bf16[2048,768]{1,0:T(8,128)(2,1)S(1)}, bf16[2048,768]{1,0:T(8,128)(2,1)}, u32[]{:S(2)}) copy-start(bf16[2048,768]{1,0:T(8,128)(2,1)} %concatenate.117) | copy-start | bytes 9437188
  371.4 55.2 %slice-start = ((s8[8388608]{0:T(1024)(128)(4,1)}), s8[4194304]{0:T(1024)(128)(4,1)S(1)}, s32[]{:S(2)}) async-start(s8[8388608]{0:T(1024)(128)(4,1)} %bitcast.155), calls=%async_computation.12 | async-start | bytes 8388608
  385.6 41.0 %slice-start.1 = ((s8[8388608]{0:T(1024)(128)(4,1)}), s8[4194304]{0:T(1024)(128)(4,1)S(1)}, s32[]{:S(2)}) async-start(s8[8388608]{0:T(1024)(128)(4,1)} %bitcast.155), calls=%async_computation.13 | async-start | bytes 8388608
  385.6 120.3 %collective-permute-start.9 = (bf16[1024,2048]{1,0:T(8,128)(2,1)}, bf16[1024,2048]{1,0:T(8,128)(2,1)}, u32[]{:S(2)}, u32[]{:S(2)}) collective-permute-start(bf16[1024,2048]{1,0:T(8,128)(2,1)} %reduce-precision_convert_fusion.4), channel_id=1, source_target_pairs={{0,1},{3,2},{4,5},{7,6},{8,9},{11,10},{12,13},{15,14},{16,17},{19,... | collective-permute-start | bytes 12582920 | tf_op jit(solution)/shard_map/ppermute | solution.py:145
  400.5 26.1 %copy-start.26 = (bf16[2,1024,1,256]{3,1,0,2:T(8,128)(2,1)S(1)}, bf16[2,1024,1,256]{3,1,0,2:T(8,128)(2,1)}, u32[]{:S(2)}) copy-start(bf16[2,1024,1,256]{3,1,0,2:T(8,128)(2,1)} %copy-done.25) | copy-start | bytes 3145732
  400.5 172.2 %collective-permute-start = (bf16[768,2048]{1,0:T(8,128)(2,1)}, bf16[768,2048]{1,0:T(8,128)(2,1)}, u32[]{:S(2)}, u32[]{:S(2)}) collective-permute-start(bf16[768,2048]{1,0:T(8,128)(2,1)} %reduce-precision_convert_fusion.10), channel_id=1, source_target_pairs={{0,1},{3,2},{4,5},{7,6},{8,9},{11,10},{12,13},{15,14},{16,17},{19,... | collective-permute-start | bytes 9437192 | tf_op jit(solution)/shard_map/ppermute | solution.py:145
  424.0 186.1 %collective-permute-start.7 = (bf16[1024,2048]{1,0:T(8,128)(2,1)}, bf16[1024,2048]{1,0:T(8,128)(2,1)}, u32[]{:S(2)}, u32[]{:S(2)}) collective-permute-start(bf16[1024,2048]{1,0:T(8,128)(2,1)} %reduce-precision_convert_fusion.6), channel_id=1, source_target_pairs={{1,2},{2,1},{5,6},{6,5},{9,10},{10,9},{13,14},{14,13},{17,18},{18,... | collective-permute-start | bytes 12582920 | tf_op jit(solution)/shard_map/ppermute | solution.py:147
  430.3 149.2 %all-to-all-start.5 = ((bf16[8,256,256]{2,1,0:T(8,128)(2,1)}), bf16[8,256,256]{2,1,0:T(8,128)(2,1)}, u32[]{:S(2)}, u32[]{:S(2)}) async-start(bf16[8,256,256]{2,1,0:T(8,128)(2,1)} %bitcast.54), calls=%async_computation.7 | async-start | bytes 2097152 | tf_op jit(solution)/shard_map/all_to_all | solution.py:416
  513.6 178.2 %collective-permute-start.10 = (bf16[1024,2048]{1,0:T(8,128)(2,1)}, bf16[1024,2048]{1,0:T(8,128)(2,1)}, u32[]{:S(2)}, u32[]{:S(2)}) collective-permute-start(bf16[1024,2048]{1,0:T(8,128)(2,1)} %reduce-precision_convert_fusion.3), channel_id=1, source_target_pairs={{1,2},{2,1},{5,6},{6,5},{9,10},{10,9},{13,14},{14,13},{17,18},{18,... | collective-permute-start | bytes 12582920 | tf_op jit(solution)/shard_map/ppermute | solution.py:147
  577.2 42.0 %collective-permute-start.1 = (bf16[768,2048]{1,0:T(8,128)(2,1)S(1)}, bf16[768,2048]{1,0:T(8,128)(2,1)}, u32[]{:S(2)}, u32[]{:S(2)}) collective-permute-start(bf16[768,2048]{1,0:T(8,128)(2,1)S(1)} %reduce-precision_convert_fusion.9), channel_id=1, source_target_pairs={{1,2},{2,1},{5,6},{6,5},{9,10},{10,9},{13,14},{14,13},{17,18},{18,... | collective-permute-start | bytes 9437192 | tf_op jit(solution)/shard_map/ppermute | solution.py:147
  580.9 26.1 %collective-permute-start.3 = (bf16[256,2048]{1,0:T(8,128)(2,1)S(1)}, bf16[256,2048]{1,0:T(8,128)(2,1)S(1)}, u32[]{:S(2)}, u32[]{:S(2)}) collective-permute-start(bf16[256,2048]{1,0:T(8,128)(2,1)S(1)} %bitcast.166), channel_id=1, source_target_pairs={{0,1},{3,2},{4,5},{7,6},{8,9},{11,10},{12,13},{15,14},{16,17},{19,... | collective-permute-start | bytes 3145736 | tf_op jit(solution)/shard_map/ppermute | solution.py:145
  608.4 93.0 %collective-permute-start.4 = (bf16[256,2048]{1,0:T(8,128)(2,1)}, bf16[256,2048]{1,0:T(8,128)(2,1)}, u32[]{:S(2)}, u32[]{:S(2)}) collective-permute-start(bf16[256,2048]{1,0:T(8,128)(2,1)} %reduce-precision_convert_fusion.12), channel_id=1, source_target_pairs={{1,2},{2,1},{5,6},{6,5},{9,10},{10,9},{13,14},{14,13},{17,18},{18,... | collective-permute-start | bytes 3145736 | tf_op jit(solution)/shard_map/ppermute | solution.py:147
  617.8 332.4 %collective-permute-start.8 = (bf16[1024,2048]{1,0:T(8,128)(2,1)}, bf16[1024,2048]{1,0:T(8,128)(2,1)}, u32[]{:S(2)}, u32[]{:S(2)}) collective-permute-start(bf16[1024,2048]{1,0:T(8,128)(2,1)} %reduce-precision_convert_fusion.5), channel_id=1, source_target_pairs={{1,0},{2,3},{5,4},{6,7},{9,8},{10,11},{13,12},{14,15},{17,16},{18,... | collective-permute-start | bytes 12582920 | tf_op jit(solution)/shard_map/ppermute | solution.py:149
  624.2 321.0 %collective-permute-start.2 = (bf16[768,2048]{1,0:T(8,128)(2,1)}, bf16[768,2048]{1,0:T(8,128)(2,1)}, u32[]{:S(2)}, u32[]{:S(2)}) collective-permute-start(bf16[768,2048]{1,0:T(8,128)(2,1)} %reduce-precision_convert_fusion.8), channel_id=1, source_target_pairs={{1,0},{2,3},{5,4},{6,7},{9,8},{10,11},{13,12},{14,15},{17,16},{18,... | collective-permute-start | bytes 9437192 | tf_op jit(solution)/shard_map/ppermute | solution.py:149
  628.8 170.7 %all-to-all-start.3 = ((bf16[2,128,2048]{2,0,1:T(2,128)(2,1)}), bf16[2,128,2048]{2,0,1:T(2,128)(2,1)S(1)}, u32[]{:S(2)}, u32[]{:S(2)}) async-start(bf16[2,128,2048]{2,0,1:T(2,128)(2,1)} %copy.93), calls=%async_computation.5 | async-start | bytes 2097152 | tf_op jit(solution)/shard_map/all_to_all | solution.py:328
  699.7 104.6 %copy-start.37 = (f32[2048]{0:T(1024)S(1)}, f32[2048]{0:T(1024)}, u32[]{:S(2)}) copy-start(f32[2048]{0:T(1024)} %param.24) | copy-start | bytes 24580
  699.7 104.6 %copy-start.38 = (f32[2048]{0:T(1024)S(1)}, f32[2048]{0:T(1024)}, u32[]{:S(2)}) copy-start(f32[2048]{0:T(1024)} %param.28) | copy-start | bytes 24580
  699.7 265.1 %collective-permute-start.11 = (bf16[1024,2048]{1,0:T(8,128)(2,1)}, bf16[1024,2048]{1,0:T(8,128)(2,1)}, u32[]{:S(2)}, u32[]{:S(2)}) collective-permute-start(bf16[1024,2048]{1,0:T(8,128)(2,1)} %reduce-precision_convert_fusion.2), channel_id=1, source_target_pairs={{1,0},{2,3},{5,4},{6,7},{9,8},{10,11},{13,12},{14,15},{17,16},{18,... | collective-permute-start | bytes 12582920 | tf_op jit(solution)/shard_map/ppermute | solution.py:149
  701.3 144.5 %copy-start.40 = (f32[1024]{0:T(1024)S(1)}, f32[1024]{0:T(1024)}, u32[]{:S(2)}) copy-start(f32[1024]{0:T(1024)} %get-tuple-element.61) | copy-start | bytes 12292
  703.3 234.2 %collective-permute-start.5 = (bf16[256,2048]{1,0:T(8,128)(2,1)S(1)}, bf16[256,2048]{1,0:T(8,128)(2,1)}, u32[]{:S(2)}, u32[]{:S(2)}) collective-permute-start(bf16[256,2048]{1,0:T(8,128)(2,1)S(1)} %reduce-precision_convert_fusion.11), channel_id=1, source_target_pairs={{1,0},{2,3},{5,4},{6,7},{9,8},{10,11},{13,12},{14,15},{17,16},{18,... | collective-permute-start | bytes 3145736 | tf_op jit(solution)/shard_map/ppermute | solution.py:149
  799.5 142.2 %all-to-all-start.1 = ((bf16[2,128,2048]{2,0,1:T(2,128)(2,1)}), bf16[2,128,2048]{2,0,1:T(2,128)(2,1)}, u32[]{:S(2)}, u32[]{:S(2)}) async-start(bf16[2,128,2048]{2,0,1:T(2,128)(2,1)} %copy.80), calls=%async_computation.2 | async-start | bytes 2097152 | tf_op jit(solution)/shard_map/all_to_all | solution.py:328
  803.8 41.1 %reduce-scatter.10.cloned.1.call-start = ((), (), s32[]{:S(2)}) async-start(), calls=%async_computation.11 | async-start | bytes 1179648
  936.9 48.1 %copy-start.41 = (f32[256]{0:T(256)}, f32[256]{0:T(256)S(1)}, u32[]{:S(2)}) copy-start(f32[256]{0:T(256)S(1)} %get-tuple-element.92) | copy-start | bytes 3076
  941.6 18.9 %all-to-all-start.4 = ((bf16[8,32,2048]{2,1,0:T(8,128)(2,1)}), bf16[8,32,2048]{2,1,0:T(8,128)(2,1)S(1)}, u32[]{:S(2)}, u32[]{:S(2)}) async-start(bf16[8,32,2048]{2,1,0:T(8,128)(2,1)} %bitcast.44), calls=%async_computation.6 | async-start | bytes 2097152 | tf_op jit(solution)/shard_map/all_to_all | solution.py:329
  960.6 19.7 %all-to-all-start.2 = ((bf16[8,32,2048]{2,1,0:T(8,128)(2,1)}), bf16[8,32,2048]{2,1,0:T(8,128)(2,1)}, u32[]{:S(2)}, u32[]{:S(2)}) async-start(bf16[8,32,2048]{2,1,0:T(8,128)(2,1)} %bitcast.22), calls=%async_computation.3 | async-start | bytes 2097152 | tf_op jit(solution)/shard_map/all_to_all | solution.py:329
  (36 other events, 240.4 us)
Sparse Core Ops, SparseCore 0:
  305.4 71.9 reduce-scatter.7
  381.8 79.7 reduce-scatter.5
  808.3 36.4 reduce-scatter.9

commit v3 on v2

--- a/solution.py
+++ b/solution.py
@@ -1,3 +1,4 @@
+import functools
 import math
 
 import jax
@@ -139,24 +140,6 @@
         * SCALE
     )
     return (query_grad, key_grad, value_grad)
-
-
-def sum_over_line(partial):
-    inward = lax.ppermute(partial, "sp", [(0, 1), (3, 2)])
-    half = rounded(partial.astype(jnp.float32) + inward.astype(jnp.float32))
-    other = lax.ppermute(half, "sp", [(1, 2), (2, 1)])
-    whole = rounded(half.astype(jnp.float32) + other.astype(jnp.float32))
-    outward = lax.ppermute(whole, "sp", [(1, 0), (2, 3)])
-    place = lax.axis_index("sp")
-    inner = (place == 1) | (place == 2)
-    return jnp.where(inner, whole, outward).astype(jnp.float32)
-
-
-def sum_over_sp(partial):
-    partial = rounded(partial)
-    if lax.axis_size("sp") == 4:
-        return sum_over_line(partial)
-    return lax.psum(partial, "sp").astype(jnp.float32)
 
 
 def gather_kernel(x_ref, c_ref, xg_ref, cg_ref, held, s1, r1, s2, r2, s3, r3, local):
@@ -286,6 +269,375 @@
         compiler_params=pltpu.CompilerParams(collective_id=1, has_side_effects=True),
         name="gather_tokens",
     )(x, c)
+
+
+def reduce_kernel(
+    sizes, steps,
+    down_ref, up_ref, qkv_ref, dense_ref, out_ref, back_ref, vec_ref, bias_ref,
+    g_down, g_up, g_qkv, g_dense, o_out, o_back, o_small,
+    line_a, line_b, turned, own, paired, block, crossed, reduced, homed, vec_in, small, small_in,
+    in_s, in_r, mid_s, mid_r, end_s, end_r, own_l, keep_l,
+    turn_s, turn_r, pair_s, pair_r, block_l, cross_s, cross_r, home_s, home_r, back_s, back_r, local,
+    vec_s, vec_r, small_s, small_r,
+):
+    f, s = lax.axis_index("fsdp"), lax.axis_index("sp")
+    core, col, row = f % 2, (f // 2) % 2, f // 4
+    f_x, f_y, f_c = f + 2 - 4 * col, f + 4 - 8 * row, f + 1 - 2 * core
+    f_d = f_x + 4 - 8 * row
+    is_end = (s == 0) | (s == 3)
+    is_mid = (s == 1) | (s == 2)
+    inner = 1 + s // 3
+    outer = 3 * (s // 2)
+    facing = 3 - s
+    barrier = pltpu.get_barrier_semaphore()
+    for k in range(1, 8):
+        pl.semaphore_signal(barrier, inc=1, device_id=((f + k) % 8, s), device_id_type=MESH)
+    for k in range(1, 4):
+        pl.semaphore_signal(barrier, inc=1, device_id=(f, (s + k) % 4), device_id_type=MESH)
+    pl.semaphore_wait(barrier, 10)
+    sent = []
+
+    def send(src, dst, send_sem, recv_sem, device, track=True):
+        copy = pltpu.make_async_remote_copy(
+            src_ref=src, dst_ref=dst, send_sem=send_sem, recv_sem=recv_sem,
+            device_id=device, device_id_type=MESH,
+        )
+        copy.start()
+        if track:
+            sent.append(copy)
+        return copy
+
+    def arrived(ref, recv_sem):
+        pltpu.make_async_remote_copy(
+            src_ref=ref, dst_ref=ref, send_sem=vec_s.at[0], recv_sem=recv_sem,
+            device_id=(f_c, s), device_id_type=MESH,
+        ).wait_recv()
+
+    def copied(src, dst, sem):
+        copy = pltpu.make_async_copy(src, dst, sem)
+        copy.start()
+        return copy
+
+    part = turned.shape[0]
+    span = dense_ref.shape[1]
+    columns = pl.ds(pl.multiple_of(f * span, span), span)
+    vec_own = copied(vec_ref.at[f], vec_in.at[f], local.at[0])
+    turn_own = copied(dense_ref.at[pl.ds(f * part, part)], turned.at[:, columns], local.at[1])
+    bias_own = copied(bias_ref, small.at[pl.ds(8, 8)], local.at[2])
+    for k in range(1, 8):
+        j = (f + k) % 8
+        send(vec_ref.at[j], vec_in.at[f], vec_s.at[k], vec_r.at[k], (j, s))
+
+    chunks = []
+    offset = 0
+    for ref, result, rows_of in (
+        (down_ref, g_down, sizes[0]), (up_ref, g_up, sizes[1]), (qkv_ref, g_qkv, sizes[2]), (turned, g_dense, sizes[3]),
+    ):
+        first = 0
+        for rows in rows_of:
+            chunks.append((ref, result, first, rows, offset))
+            first += rows
+            offset += rows
+    count = len(chunks)
+    ahead = 5
+
+    def from_end(k):
+        ref, _, first, rows, at = chunks[k]
+        return pltpu.make_async_remote_copy(
+            src_ref=ref.at[pl.ds(first, rows)], dst_ref=line_a.at[pl.ds(at, rows)],
+            send_sem=in_s.at[k], recv_sem=in_r.at[k], device_id=(f, inner), device_id_type=MESH,
+        )
+
+    def across(k):
+        _, _, _, rows, at = chunks[k]
+        return pltpu.make_async_remote_copy(
+            src_ref=line_a.at[pl.ds(at, rows)], dst_ref=line_b.at[pl.ds(at, rows)],
+            send_sem=mid_s.at[k], recv_sem=mid_r.at[k], device_id=(f, facing), device_id_type=MESH,
+        )
+
+    def to_end(k):
+        _, result, first, rows, at = chunks[k]
+        return pltpu.make_async_remote_copy(
+            src_ref=line_b.at[pl.ds(at, rows)], dst_ref=result.at[pl.ds(first, rows)],
+            send_sem=end_s.at[k], recv_sem=end_r.at[k], device_id=(f, outer), device_id_type=MESH,
+        )
+
+    def load_own(k):
+        ref, _, first, rows, _ = chunks[k]
+        return pltpu.make_async_copy(
+            ref.at[pl.ds(first, rows)], own.at[k % 3, pl.ds(0, rows)], own_l.at[k % 3]
+        )
+
+    def keep(k):
+        _, result, first, rows, at = chunks[k]
+        return pltpu.make_async_copy(
+            line_b.at[pl.ds(at, rows)], result.at[pl.ds(first, rows)], keep_l.at[k]
+        )
+
+    tile = 16
+
+    def add_rows(target, target_at, left, left_at, right, rows):
+        @pl.loop(0, rows // tile)
+        def _(i):
+            at = pl.multiple_of(i * tile, tile)
+            total = (
+                left[pl.ds(left_at + at, tile), :].astype(jnp.float32)
+                + right[pl.ds(at, tile), :].astype(jnp.float32)
+            )
+            target[pl.ds(target_at + at, tile), :] = total.astype(target.dtype)
+
+    def mid_in(k):
+        _, _, _, rows, at = chunks[k]
+        load_own(k).wait()
+        from_end(k).wait_recv()
+        add_rows(line_a, at, line_a, at, own.at[k % 3], rows)
+        across(k).start()
+        if k + 3 < count:
+            load_own(k + 3).start()
+
+    def mid_out(k):
+        _, _, _, rows, at = chunks[k]
+        across(k).wait_recv()
+        add_rows(line_b, at, line_b, at, line_a.at[pl.ds(at, rows)], rows)
+        to_end(k).start()
+        keep(k).start()
+
+    pairs = ((out_ref, o_out), (back_ref, o_back))
+    order = (f_d // 2, f_x // 2, f_y // 2, f // 2)
+    for a, (ref, _) in enumerate(pairs):
+        for n, q in enumerate(order):
+            send(ref.at[:, :, q, 1 - core], paired.at[a, n], pair_s.at[a, n], pair_r.at[a, n], (f_c, s))
+    for k in range(1, 8):
+        j = (f + k) % 8
+        send(dense_ref.at[pl.ds(j * part, part)], turned.at[:, columns], turn_s.at[k], turn_r.at[k], (j, s))
+
+    def load_block(i):
+        a, n = i // 4, i % 4
+        return pltpu.make_async_copy(
+            pairs[a][0].at[:, :, order[n], core], block.at[i % 2], block_l.at[i % 2]
+        )
+
+    load_block(0).start()
+    load_block(1).start()
+
+    def add_pair(i):
+        a, n = i // 4, i % 4
+        load_block(i).wait()
+        arrived(paired.at[a, n], pair_r.at[a, n])
+
+        @pl.loop(0, 8)
+        def _(m):
+            b, z = m // 4, m % 4
+            total = paired[a, n, b, z].astype(jnp.float32) + block[i % 2, b, z].astype(jnp.float32)
+            paired[a, n, b, z] = total.astype(paired.dtype)
+
+        if n < 3:
+            send(paired.at[a, n], crossed.at[a, n], cross_s.at[a, n], cross_r.at[a, n], ((f_d, f_x, f_y)[n], s))
+        if i + 2 < 8:
+            load_block(i + 2).start()
+
+    placed = {}
+
+    def add_chips(a):
+        for n in range(3):
+            arrived(crossed.at[a, n], cross_r.at[a, n])
+
+        @pl.loop(0, 8)
+        def _(m):
+            b, z = m // 4, m % 4
+            total = paired[a, 3, b, z].astype(jnp.float32)
+            for n in range(3):
+                total = total + crossed[a, n, b, z].astype(jnp.float32)
+            reduced[a, b, z] = total.astype(reduced.dtype)
+
+        for k in range(1, 4):
+            z = (s + k) % 4
+            send(reduced.at[a, :, z], homed.at[a, s], home_s.at[a, k], home_r.at[a, k], (f, z))
+        placed["along", a] = copied(reduced.at[a, :, s], homed.at[a, s], local.at[3 + a])
+
+    def go_home(a):
+        result = pairs[a][1]
+        placed["along", a].wait()
+        for k in range(1, 4):
+            arrived(homed.at[a, (s + 4 - k) % 4], home_r.at[a, k])
+        for k in range(1, 8):
+            j = (f + k) % 8
+            send(homed.at[a, j // 2, j % 2], result.at[f], back_s.at[a, k], back_r.at[a, k], (j, s))
+        placed["home", a] = copied(homed.at[a, f // 2, core], result.at[f], local.at[5 + a])
+
+    def add_vectors():
+        vec_own.wait()
+        bias_own.wait()
+        for k in range(1, 8):
+            arrived(vec_in.at[(f + 8 - k) % 8], vec_r.at[k])
+        total = vec_in[0]
+        for j in range(1, 8):
+            total = total + vec_in[j]
+        small[0:8, :] = total
+        for k in range(1, 4):
+            send(small, small_in.at[s], small_s.at[k], small_r.at[k], (f, (s + k) % 4))
+        placed["small"] = copied(small, small_in.at[s], local.at[7])
+
+    def add_small():
+        placed["small"].wait()
+        for k in range(1, 4):
+            arrived(small_in.at[(s + 4 - k) % 4], small_r.at[k])
+        total = small_in[0]
+        for z in range(1, 4):
+            total = total + small_in[z]
+        o_small[...] = total
+
+    def turn_done():
+        turn_own.wait()
+        for k in range(1, 8):
+            j = (f + 8 - k) % 8
+            at = pl.ds(pl.multiple_of(j * span, span), span)
+            arrived(turned.at[:, at], turn_r.at[k])
+
+    def tasks(name):
+        if name == "vec":
+            add_vectors()
+        elif name == "small":
+            add_small()
+        elif name == "turn":
+            turn_done()
+        elif name[0] == "p":
+            add_pair(int(name[1:]))
+        elif name[0] == "c":
+            add_chips(int(name[1:]))
+        elif name[0] == "h":
+            go_home(int(name[1:]))
+
+    @pl.when(is_end)
+    def _():
+        for k in range(ahead):
+            from_end(k).start()
+
+    @pl.when(is_mid)
+    def _():
+        for k in range(3):
+            load_own(k).start()
+
+    for k in range(count + 1):
+        for name in steps.get(k, ()):
+            tasks(name)
+
+        @pl.when(is_mid)
+        def _():
+            if k < count:
+                mid_in(k)
+            if k >= 1:
+                mid_out(k - 1)
+
+        @pl.when(is_end)
+        def _():
+            if k >= 1:
+                to_end(k - 1).wait_recv()
+                if k - 1 + ahead < count:
+                    from_end(k - 1 + ahead).start()
+
+    for name in steps.get(count + 1, ()):
+        tasks(name)
+    for a in range(2):
+        placed["home", a].wait()
+        for k in range(1, 8):
+            arrived(pairs[a][1].at[(f + 8 - k) % 8], back_r.at[a, k])
+    for copy in sent:
+        copy.wait_send()
+
+    @pl.when(is_end)
+    def _():
+        for k in range(count):
+            from_end(k).wait_send()
+
+    @pl.when(is_mid)
+    def _():
+        for k in range(count):
+            across(k).wait_send()
+            to_end(k).wait_send()
+            keep(k).wait()
+
+
+STEPS = {
+    0: ("p0", "p1", "p2", "p3", "vec"),
+    1: ("p4", "p5"),
+    2: ("p6", "p7"),
+    3: ("small",),
+    5: ("c0",),
+    7: ("h0",),
+    8: ("c1", "turn"),
+    10: ("h1",),
+}
+
+
+def reduce_all(down, up, qkv, dense, out_part, back_part, vec, bias, sizes, steps=STEPS):
+    width = down.shape[1]
+    dtype = down.dtype
+    total = sum(sum(rows) for rows in sizes)
+    count = sum(len(rows) for rows in sizes)
+    largest = max(max(rows) for rows in sizes)
+    piece = out_part.shape[4]
+    dma = pltpu.SemaphoreType.DMA
+    grads = [jax.ShapeDtypeStruct((sum(rows), width), dtype) for rows in sizes]
+    token = jax.ShapeDtypeStruct((8, piece, width), dtype)
+    span = dense.shape[1]
+    anywhere = pl.BlockSpec(memory_space=pl.ANY)
+    vmem = pltpu.VMEM
+    return pl.pallas_call(
+        functools.partial(reduce_kernel, sizes, steps),
+        out_shape=(*grads, token, token, jax.ShapeDtypeStruct((16, vec.shape[2]), jnp.float32)),
+        in_specs=[anywhere] * 8,
+        out_specs=[anywhere] * 6 + [pl.BlockSpec(memory_space=pltpu.VMEM)],
+        scratch_shapes=[
+            vmem((total, width), dtype), vmem((total, width), dtype), vmem((sum(sizes[3]), width), dtype),
+            vmem((3, largest, width), dtype),
+            vmem((2, 4, 2, 4, piece, width), dtype), vmem((2, 2, 4, piece, width), dtype),
+            vmem((2, 3, 2, 4, piece, width), dtype), vmem((2, 2, 4, piece, width), dtype),
+            vmem((2, 4, 2, piece, width), dtype),
+            vmem((8, 8, vec.shape[2]), jnp.float32), vmem((16, vec.shape[2]), jnp.float32),
+            vmem((4, 16, vec.shape[2]), jnp.float32),
+            dma((count,)), dma((count,)), dma((count,)), dma((count,)), dma((count,)), dma((count,)),
+            dma((3,)), dma((count,)),
+            dma((8,)), dma((8,)), dma((2, 4)), dma((2, 4)), dma((2,)), dma((2, 3)), dma((2, 3)),
+            dma((2, 4)), dma((2, 4)), dma((2, 8)), dma((2, 8)), dma((8,)),
+            dma((8,)), dma((8,)), dma((4,)), dma((4,)),
+        ],
+        compiler_params=pltpu.CompilerParams(
+            collective_id=2, has_side_effects=True, vmem_limit_bytes=60 * 1024 * 1024
+        ),
+        name="reduce_all",
+    )(down, up, qkv, dense, out_part, back_part, vec, bias)
+
+
+def cut(rows, unit, first=False, last=False):
+    sizes = [4 * unit] * (rows // (4 * unit))
+    if first:
+        sizes[:1] = [unit, unit, 2 * unit]
+    if last:
+        sizes[-1:] = [2 * unit, unit, unit]
+    return tuple(sizes)
+
+
+def reduce_tokens(terms, partial_out, partial_back, vectors, biases):
+    down, up, qkv, dense = (term.astype(jnp.bfloat16) for term in terms)
+    sizes = (
+        cut(down.shape[0], 64, first=True),
+        cut(up.shape[0], 64),
+        cut(qkv.shape[0], 64),
+        cut(dense.shape[0] // 8, 64, last=True),
+    )
+    *grads, output, weighted, sums = reduce_all(
+        down,
+        up,
+        qkv,
+        dense,
+        partial_out.astype(jnp.bfloat16),
+        partial_back.astype(jnp.bfloat16),
+        vectors,
+        biases,
+        sizes,
+    )
+    return [grad.astype(jnp.float32) for grad in grads], output, weighted, sums
 
 
 def per_device(
@@ -353,7 +705,8 @@
         share = vector.shape[0] // nf
         return lax.dynamic_slice_in_dim(vector, f_place * share, share, 0)
 
-    if (nf, ns, seq_local) == (8, 4, 1):
+    fast = (nf, ns, seq_local, HEADS) == (8, 4, 1, 8)
+    if fast:
         gathered, upstream = (
             array.reshape(tokens, width) for array in gather_both(hidden_in[0], cotangent[0])
         )
@@ -413,25 +766,46 @@
     attn_norm_grad = times(packed_grad, w_qkv)
     qkv_term = contract_rows(packed_grad, normed)
     dense_term = contract_rows(upstream, context).astype(jnp.bfloat16)
-    dense_term = lax.all_to_all(dense_term, "fsdp", split_axis=0, concat_axis=1, tiled=True)
-
+
+    partial_back = attn_norm_grad * ln1_gain + mlp_norm_grad * ln2_gain
     vectors = jnp.stack(
         [
             jnp.sum(attn_norm_grad * scaled, axis=0),
             jnp.sum(attn_norm_grad, axis=0),
             jnp.sum(mlp_norm_grad * scaled, axis=0),
             jnp.sum(mlp_norm_grad, axis=0),
-        ],
-        axis=1,
-    )
-    vectors = lax.psum_scatter(vectors, "fsdp", scatter_dimension=0, tiled=True)
+        ]
+    )
     bias_out = own_part(jnp.sum(upstream.astype(jnp.float32), axis=0))
     bias_qkv = jnp.sum(packed_grad.astype(jnp.float32), axis=0)
     bias_up = jnp.sum(hidden_grad.astype(jnp.float32), axis=0)
-    vectors, bias_out, bias_qkv, bias_up = lax.psum((vectors, bias_out, bias_qkv, bias_up), "sp")
-
-    output = scatter_tokens(rounded(partial_out))
-    weighted = scatter_tokens(rounded(attn_norm_grad * ln1_gain + mlp_norm_grad * ln2_gain))
+    if fast:
+        share = width // nf
+        vectors = jnp.pad(vectors.reshape(4, nf, share).transpose(1, 0, 2), ((0, 0), (0, 4), (0, 0)))
+        biases = jnp.concatenate([bias_out, bias_qkv, bias_up]).reshape(8, share)
+        token_shape = (group, ns, 4, 2, piece, width)
+        grads, output, weighted, sums = reduce_tokens(
+            (down_term, up_term, qkv_term, dense_term),
+            partial_out.reshape(token_shape),
+            partial_back.reshape(token_shape),
+            vectors,
+            biases,
+        )
+        grad_down_w, grad_up_w, grad_qkv_w, grad_dense_w = grads
+        output = output.reshape(hidden_in.shape)
+        weighted = weighted.reshape(hidden_in.shape)
+        vectors = sums[:4]
+        bias_out, bias_qkv, bias_up = sums[8], sums[9:12].reshape(-1), sums[12:16].reshape(-1)
+    else:
+        vectors = lax.psum_scatter(vectors, "fsdp", scatter_dimension=1, tiled=True)
+        vectors, bias_out, bias_qkv, bias_up = lax.psum((vectors, bias_out, bias_qkv, bias_up), "sp")
+        output = scatter_tokens(rounded(partial_out))
+        weighted = scatter_tokens(rounded(partial_back))
+        dense_term = lax.all_to_all(dense_term, "fsdp", split_axis=0, concat_axis=1, tiled=True)
+        grad_down_w, grad_up_w, grad_qkv_w, grad_dense_w = (
+            lax.psum(term.astype(jnp.bfloat16), "sp").astype(jnp.float32)
+            for term in (down_term, up_term, qkv_term, dense_term)
+        )
     inputs = hidden_in.astype(jnp.float32)
     output = (inputs + (output.astype(jnp.float32) + (b_dense + b_down))).astype(jnp.bfloat16)
     own_scaled, own_inverse = norm_scaled(inputs)
@@ -443,17 +817,13 @@
         + own_inverse * (weighted - first_mean - own_scaled * second_mean)
     ).astype(jnp.bfloat16)
 
-    grad_down_w = sum_over_sp(down_term)
-    grad_up_w = sum_over_sp(up_term)
-    grad_qkv_w = sum_over_sp(qkv_term)
-    grad_dense_w = sum_over_sp(dense_term)
     return (
         output,
         input_grad,
-        vectors[:, 0],
-        vectors[:, 1],
-        vectors[:, 2],
-        vectors[:, 3],
+        vectors[0],
+        vectors[1],
+        vectors[2],
+        vectors[3],
         grad_qkv_w,
         bias_qkv,
         grad_dense_w,

time: 1000 us -> 810 us (0.81)
  Pallas kernels: 107 us -> 500 us
  waiting for transfers between devices: 291 us -> 0.01 us
  starting transfers between devices: 118 us -> 5.17 us
  blocking collectives: 100 us -> 9.16 us
  other arithmetic: 133 us -> 87.9 us
  local copies, waits for them, and re-layouts: 58.4 us -> 30.9 us
  between operations: 15 us -> 1.8 us
    pallas_call x0 -> x1, Pallas kernels: none -> 395 us  [reduce_all(): pl.pallas_call(functools.partial(reduce_kernel, sizes, steps), out_shape=...]
    ppermute x12 -> x0, waiting for transfers between devices: 157 us -> none  [the longest x4 157 us: sum_over_line(): inward = lax.ppermute(partial, 'sp', [(0, 1), (3, 2)])]
    all_to_all x5 -> x0, waiting for transfers between devices: 97.4 us -> none  [the longest x2 91.6 us: scatter_tokens(): part = lax.all_to_all(part, 'sp', split_axis=1, concat_axis=0, tiled=True)]
    psum x1 -> x0, blocking collectives: 91.1 us -> none  [per_device(): lax.psum((vectors, bias_out, bias_qkv, bias_up), 'sp')]
    all_to_all x5 -> x0, starting transfers between devices: 79.3 us -> none  [the longest x2 67.3 us: scatter_tokens(): part = lax.all_to_all(part, 'sp', split_axis=1, concat_axis=0, tiled=True)]
    convert_element_type x13 -> x5, other arithmetic: 66.4 us -> 19.5 us  [the longest x4 17.1 us: reduce_tokens(): grad.astype(jnp.float32)]
    unnamed x4 -> x0, waiting for transfers between devices: 36.7 us -> none
    ppermute x12 -> x0, starting transfers between devices: 32.9 us -> none  [the longest x4 18.3 us: sum_over_line(): inward = lax.ppermute(partial, 'sp', [(0, 1), (3, 2)])]
  transfers between devices with their start and end apart: 21 -> 1, of which waited for: 8 -> 0; matrix products, arithmetic and copies ran while one was open for 27% -> 19% of each run, Pallas kernels for 11% -> 13%
where the time goes in v3:
time: 810 us; the launch traced here: 802 us
  Pallas kernels  500 us (62%)
  matrix products  166 us (20%)
  other arithmetic  87.9 us (11%)
  local copies, waits for them, and re-layouts  30.9 us (4%)
  blocking collectives  9.16 us (1%)
    pallas_call x1, Pallas kernels, reduce_all(): pl.pallas_call(functools.partial(reduce_kernel, sizes, steps), out_shape=...  395 us
    pallas_call x1, Pallas kernels, gather_both(): pl.pallas_call(gather_kernel, out_shape=(shape, shape), in_specs=[pl.Bloc...  105 us
    dot_general x4, matrix products, times_transposed(): lax.dot_general(former, latter, (((1,), (1,)), ((), ())), preferred_eleme...  51.4 us
    dot_general x4, matrix products, times(): return jnp.dot(former, latter, preferred_element_type=jnp.float32)  47.4 us
    dot_general x4, matrix products, contract_rows(): lax.dot_general(former, latter, (((0,), (0,)), ((), ())), preferred_eleme...  45.4 us
    convert_element_type x4, other arithmetic, reduce_tokens(): grad.astype(jnp.float32)  17.1 us
  transfers between devices with their start and end apart: 1, of which 0 were waited for; matrix products, arithmetic and copies ran while one was open for 19% of the time, Pallas kernels for 13%

profile of v3, /device:TPU:0, one launch (start us, length us, event | category | flops | bytes accessed | tf_op | source)
XLA Modules:
  0.0 801.5 jit_solution(15760429201400989813)
XLA Ops:
  3.1 5.2 all-to-all-start
  11.6 105.4 %gather_tokens.1 = (bf16[2,4,8,32,2048]{4,3,2,1,0:T(8,128)(2,1)}, bf16[2,4,8,32,2048]{4,3,2,1,0:T(8,128)(2,1)}) custom-call(bf16[256,2048]{1,0:T(8,128)(2,1)} %bitcast.135, bf16[256,2048]{1,0:T(8,128)(2,1)} %bitcast.153), custom_call_target="tpu_custom_call" | custom-call | tf_op jit(solution)/shard_map/gather_tokens/pallas_call | solution.py:260
  117.0 4.7 convert_reduce_fusion.1
  121.8 8.5 %convert_reduce_fusion = (f32[2048]{0:T(1024)}, f32[2,4,8,32]{3,2,1,0:T(8,128)S(1)}) fusion(bf16[2,4,8,32,2048]{4,3,2,1,0:T(8,128)(2,1)} %get-tuple-element.24, f32[2,4,8,32]{3,2,1,0:T(8,128)S(1)} %broadcast_multiply_fusion, bf16[2,4,8,32,2048]{4,3,2,1,0:T(8,128)(2,1)} %get-tuple-element.23), kind=kLoop, calls=%fused_computation.2 | loop fusion | flops 25161728 | bytes 16801792 | tf_op jit(solution)/shard_map/reduce_sum | solution.py:779
  131.2 9.6 %add_convert_fusion.2 = (bf16[2048,2048]{1,0:T(8,128)(2,1)S(1)}, bf16[2048,2048]{1,0:T(8,128)(2,1)}) fusion(bf16[2,4,8,32,2048]{4,3,2,1,0:T(8,128)(2,1)} %get-tuple-element.23, f32[2048]{0:T(1024)S(1)} %copy-done.35, f32[2048]{0:T(1024)S(1)} %copy-done.37, f32[2048]{0:T(1024)S(1)} %rsqrt.20, f32[2048]{0:T(1024)S(1)} %div.48, f32[2048]{0:T(1024)S(1)} %copy-done.36, ...), kind=kLoop, calls=%fused_computation.7 | loop fusion | flops 37748736 | bytes 25214976 | tf_op jit(solution)/shard_map/convert_element_type | solution.py:726
  140.8 6.9 add_convert_fusion.4
  152.6 9.2 %all-gather = s32[8,1,1024]{2,1,0:T(1,128)S(1)} all-gather(s32[1,1,1024]{2,1,0:T(1,128)S(1)} %bitcast.173), channel_id=1, replica_groups=mesh['fsdp'=8,'sp'=4] {'fsdp'}, dimensions={0}, use_global_device_ids=true | all-gather | bytes 36864 | tf_op jit(solution)/shard_map/all_gather | solution.py:715
  168.0 5.0 fusion.41
  173.1 3.3 fusion.9
  176.4 3.4 fusion.8
  179.8 6.1 fusion.31
  186.6 15.3 %multiply_convert_fusion.1 = (bf16[2048,1024]{1,0:T(8,128)(2,1)S(1)}, f32[2048,1024]{1,0:T(8,128)}) fusion(f32[1024]{0:T(1024)S(1)} %dynamic_slice.12, bf16[2048,2048]{1,0:T(8,128)(2,1)} %get-tuple-element.40, bf16[1024,2048]{1,0:T(8,128)(2,1)} %param.25), kind=kOutput, calls=%fused_computation.24 | convolution fusion | flops 8602517504 | bytes 25169920 | tf_op jit(solution)/shard_map/dot_general | solution.py:36
  201.9 13.2 %convolution_convert_fusion.1.down_ref = bf16[1024,2048]{1,0:T(8,128)(2,1)} fusion(bf16[2048,1024]{1,0:T(8,128)(2,1)S(1)} %get-tuple-element.66, bf16[2048,2048]{1,0:T(8,128)(2,1)} %bitcast.140), kind=kOutput, calls=%fused_computation.37 | convolution fusion | flops 8592031744 | bytes 16777216 | tf_op jit(solution)/shard_map/dot_general | solution.py:30
  215.1 11.7 %fusion.56 = f32[2048,2048]{1,0:T(8,128)} fusion(bf16[2048,1024]{1,0:T(8,128)(2,1)S(1)} %get-tuple-element.66, bf16[1024,2048]{1,0:T(8,128)(2,1)S(1)} %copy-done.46), kind=kOutput, calls=%fused_computation.130 | convolution fusion | flops 8589934592 | bytes 25165824 | tf_op jit(solution)/shard_map/dot_general | solution.py:42
  226.8 16.9 %convert_reduce_fusion.2 = (f32[1024]{0:T(1024)S(1)}, bf16[2048,1024]{1,0:T(8,128)(2,1)}) fusion(f32[2048,1024]{1,0:T(8,128)} %get-tuple-element.67, f32[1024]{0:T(1024)S(1)} %dynamic_slice.12, bf16[2048,2048]{1,0:T(8,128)(2,1)} %bitcast.141, bf16[1024,2048]{1,0:T(8,128)(2,1)S(1)} %copy-done.46), kind=kOutput, calls=%fused_computation.18 | convolution fusion | flops 8617196544 | bytes 25174016 | tf_op jit(solution)/shard_map/dot_general | solution.py:36
  243.7 12.7 %convolution_convert_fusion.up_ref = bf16[1024,2048]{1,0:T(8,128)(2,1)} fusion(bf16[2048,1024]{1,0:T(8,128)(2,1)} %get-tuple-element.73, bf16[2048,2048]{1,0:T(8,128)(2,1)S(1)} %bitcast.139), kind=kOutput, calls=%fused_computation.36 | convolution fusion | flops 8592031744 | bytes 16777216 | tf_op jit(solution)/shard_map/dot_general | solution.py:30
  256.4 11.7 %fusion.57 = f32[2048,2048]{1,0:T(8,128)} fusion(bf16[2048,1024]{1,0:T(8,128)(2,1)S(1)} %copy-done.48, bf16[1024,2048]{1,0:T(8,128)(2,1)S(1)} %copy-done.47), kind=kOutput, calls=%fused_computation.131 | convolution fusion | flops 8589934592 | bytes 25165824 | tf_op jit(solution)/shard_map/dot_general | solution.py:42
  271.8 7.2 convolution_convert_fusion.3.dense_ref
  281.3 6.1 convolution_convert_fusion.4
  287.7 4.4 fusion.28
  292.1 5.0 multiply_reduce_fusion.3
  297.2 4.0 multiply_convert_fusion
  307.8 4.6 slice_multiply_fusion.2
  318.8 5.0 fusion.37
  323.8 7.0 concatenate.121
  330.8 12.3 %convolution_convert_fusion.2.qkv_ref = bf16[768,2048]{1,0:T(8,128)(2,1)} fusion(bf16[2048,768]{1,0:T(8,128)(2,1)} %concatenate.121, bf16[2048,2048]{1,0:T(8,128)(2,1)} %copy-done.15), kind=kOutput, calls=%fused_computation.38 | convolution fusion | flops 6444023808 | bytes 14680064 | tf_op jit(solution)/shard_map/dot_general | solution.py:30
  344.3 12.2 %add_convert_fusion.1 = bf16[2048,2048]{1,0:T(8,128)(2,1)} fusion(f32[2048,2048]{1,0:T(8,128)} %fusion.56, bf16[2048,256]{1,0:T(8,128)(2,1)} %bitcast.155, bf16[2048,256]{1,0:T(8,128)(2,1)} %bitcast.157), kind=kOutput, calls=%fused_computation.6 | convolution fusion | flops 2155872256 | bytes 27262976 | tf_op jit(solution)/shard_map/dot_general | solution.py:36
  356.6 17.8 %multiply_reduce_fusion.1 = (f32[2048]{0:T(1024)S(1)}, f32[2048]{0:T(1024)S(1)}, f32[2048]{0:T(1024)S(1)}, f32[2048]{0:T(1024)S(1)}, bf16[2048,2048]{1,0:T(8,128)(2,1)}) fusion(bf16[2,4,8,32,2048]{4,3,2,1,0:T(8,128)(2,1)} %get-tuple-element.23, f32[2048]{0:T(1024)S(1)} %copy-done.34, f32[2048]{0:T(1024)S(1)} %copy-done.32, f32[2048,2048]{1,0:T(8,128)} %fusion.57, ...), kind=kOutput, calls=%fused_computation.4 | convolution fusion | flops 6496968704 | bytes 39911424 | tf_op jit(solution)/shard_map/dot_general | solution.py:42
  375.1 394.7 %reduce_all.1 = (bf16[1024,2048]{1,0:T(8,128)(2,1)}, bf16[1024,2048]{1,0:T(8,128)(2,1)}, bf16[768,2048]{1,0:T(8,128)(2,1)}, bf16[256,2048]{1,0:T(8,128)(2,1)}, b...) custom-call(bf16[1024,2048]{1,0:T(8,128)(2,1)} %convolution_convert_fusion.1.down_ref, ...), custom_call_target="tpu_custom_call" | custom-call | tf_op jit(solution)/shard_map/reduce_all/pallas_call | solution.py:586
  783.6 5.4 convert_element_type.216
  789.1 4.4 convert_element_type.218
  793.6 4.4 convert_element_type.219
  (168 shorter events, 56.3 us)
Async XLA Ops:
  0.6 140.2 %copy-start = (bf16[768,2048]{1,0:T(8,128)(2,1)S(1)}, bf16[768,2048]{1,0:T(8,128)(2,1)}, u32[]{:S(2)}) copy-start(bf16[768,2048]{1,0:T(8,128)(2,1)} %param.21) | copy-start | bytes 9437188
  3.1 275.9 %all-to-all-start = ((bf16[256,8,256]{0,2,1:T(8,128)(2,1)}), bf16[256,8,256]{0,2,1:T(8,128)(2,1)}, u32[]{:S(2)}, u32[]{:S(2)}) async-start(bf16[256,8,256]{0,2,1:T(8,128)(2,1)} %bitcast.152), calls=%async_computation | async-start | bytes 2097152 | tf_op jit(solution)/shard_map/all_to_all | solution.py:718
  121.7 9.4 %copy-start.31 = (f32[2048]{0:T(1024)}, f32[2048]{0:T(1024)S(1)}, u32[]{:S(2)}) copy-start(f32[2048]{0:T(1024)S(1)} %div.48) | copy-start | bytes 24580
  121.7 9.4 %copy-start.35 = (f32[2048]{0:T(1024)S(1)}, f32[2048]{0:T(1024)}, u32[]{:S(2)}) copy-start(f32[2048]{0:T(1024)} %param.18) | copy-start | bytes 24580
  121.7 9.4 %copy-start.36 = (f32[2048]{0:T(1024)S(1)}, f32[2048]{0:T(1024)}, u32[]{:S(2)}) copy-start(f32[2048]{0:T(1024)} %param.20) | copy-start | bytes 24580
  121.7 9.4 %copy-start.37 = (f32[2048]{0:T(1024)S(1)}, f32[2048]{0:T(1024)}, u32[]{:S(2)}) copy-start(f32[2048]{0:T(1024)} %param.17) | copy-start | bytes 24580
  121.8 9.4 %copy-start.39 = (f32[2048]{0:T(1024)S(1)}, f32[2048]{0:T(1024)}, u32[]{:S(2)}) copy-start(f32[2048]{0:T(1024)} %param.19) | copy-start | bytes 24580
  130.4 10.4 %copy-start.33 = (f32[2048]{0:T(1024)}, f32[2048]{0:T(1024)S(1)}, u32[]{:S(2)}) copy-start(f32[2048]{0:T(1024)S(1)} %rsqrt.20) | copy-start | bytes 24580
  140.8 6.9 copy-start.15
  163.1 10.0 %copy-start.13 = (pred[1024,1024]{0,1:T(8,128)(4,1)S(1)}, pred[1024,1024]{0,1:T(8,128)(4,1)}, u32[]{:S(2)}) copy-start(pred[1024,1024]{0,1:T(8,128)(4,1)} %iota_compare_fusion) | copy-start | bytes 3145732
  163.1 10.0 %copy-start.21 = (bf16[2,1024,192]{2,1,0:T(8,128)(2,1)S(1)}, bf16[2,1024,192]{2,1,0:T(8,128)(2,1)}, u32[]{:S(2)}) copy-start(bf16[2,1024,192]{2,1,0:T(8,128)(2,1)} %get-tuple-element.43) | copy-start | bytes 2359300
  163.1 10.0 %copy-start.26 = (bf16[2,1024,192]{2,1,0:T(8,128)(2,1)S(1)}, bf16[2,1024,192]{2,1,0:T(8,128)(2,1)}, u32[]{:S(2)}) copy-start(bf16[2,1024,192]{2,1,0:T(8,128)(2,1)} %get-tuple-element.44) | copy-start | bytes 2359300
  201.8 13.2 %copy-start.46 = (bf16[1024,2048]{1,0:T(8,128)(2,1)S(1)}, bf16[1024,2048]{1,0:T(8,128)(2,1)}, u32[]{:S(2)}) copy-start(bf16[1024,2048]{1,0:T(8,128)(2,1)} %param.27) | copy-start | bytes 12582916
  215.1 28.6 %slice-start.2 = ((s8[8388608]{0:T(1024)(128)(4,1)}), s8[4194304]{0:T(1024)(128)(4,1)S(1)}, s32[]{:S(2)}) async-start(s8[8388608]{0:T(1024)(128)(4,1)} %bitcast.138), calls=%async_computation.3 | async-start | bytes 8388608
  226.8 16.9 %slice-start.3 = ((s8[8388608]{0:T(1024)(128)(4,1)}), s8[4194304]{0:T(1024)(128)(4,1)S(1)}, s32[]{:S(2)}) async-start(s8[8388608]{0:T(1024)(128)(4,1)} %bitcast.138), calls=%async_computation.4 | async-start | bytes 8388608
  243.7 12.7 %copy-start.47 = (bf16[1024,2048]{1,0:T(8,128)(2,1)S(1)}, bf16[1024,2048]{1,0:T(8,128)(2,1)}, u32[]{:S(2)}) copy-start(bf16[1024,2048]{1,0:T(8,128)(2,1)} %param.25) | copy-start | bytes 12582916
  243.7 12.7 %copy-start.48 = (bf16[2048,1024]{1,0:T(8,128)(2,1)S(1)}, bf16[2048,1024]{1,0:T(8,128)(2,1)}, u32[]{:S(2)}) copy-start(bf16[2048,1024]{1,0:T(8,128)(2,1)} %get-tuple-element.73) | copy-start | bytes 12582916
  256.4 11.8 %copy-start.43 = (f32[256]{0:T(256)S(1)}, f32[256]{0:T(256)}, u32[]{:S(2)}) copy-start(f32[256]{0:T(256)} %convert_reduce_fusion.4) | copy-start | bytes 3076
  256.4 11.8 %copy-start.2 = (bf16[1,256,2048]{2,1,0:T(8,128)(2,1)S(1)}, bf16[1,256,2048]{2,1,0:T(8,128)(2,1)}, u32[]{:S(2)}) copy-start(bf16[1,256,2048]{2,1,0:T(8,128)(2,1)} %param.15) | copy-start | bytes 3145732
  256.4 14.6 %copy-start.41 = (f32[2048]{0:T(1024)S(1)}, f32[2048]{0:T(1024)}, u32[]{:S(2)}) copy-start(f32[2048]{0:T(1024)} %param.24) | copy-start | bytes 24580
  256.4 14.6 %copy-start.42 = (f32[2048]{0:T(1024)S(1)}, f32[2048]{0:T(1024)}, u32[]{:S(2)}) copy-start(f32[2048]{0:T(1024)} %param.28) | copy-start | bytes 24580
  281.2 6.1 slice-start
  281.2 6.1 copy-start.14
  281.3 6.5 slice-start.1
  301.2 6.5 copy-start.6
  330.8 12.4 %copy-start.12 = (bf16[2048,768]{1,0:T(8,128)(2,1)S(1)}, bf16[2048,768]{1,0:T(8,128)(2,1)}, u32[]{:S(2)}) copy-start(bf16[2048,768]{1,0:T(8,128)(2,1)} %concatenate.121) | copy-start | bytes 9437188
  344.3 12.3 %copy-start.32 = (f32[2048]{0:T(1024)S(1)}, f32[2048]{0:T(1024)}, u32[]{:S(2)}) copy-start(f32[2048]{0:T(1024)} %copy-done.31) | copy-start | bytes 24580
  344.3 12.3 %copy-start.34 = (f32[2048]{0:T(1024)S(1)}, f32[2048]{0:T(1024)}, u32[]{:S(2)}) copy-start(f32[2048]{0:T(1024)} %copy-done.33) | copy-start | bytes 24580
  344.3 12.3 %copy-start.38 = (f32[2048]{0:T(1024)S(1)}, f32[2048]{0:T(1024)}, u32[]{:S(2)}) copy-start(f32[2048]{0:T(1024)} %param.17) | copy-start | bytes 24580
  344.3 12.3 %copy-start.40 = (f32[2048]{0:T(1024)S(1)}, f32[2048]{0:T(1024)}, u32[]{:S(2)}) copy-start(f32[2048]{0:T(1024)} %param.19) | copy-start | bytes 24580
  772.6 27.9 %copy-start.45 = (f32[1,256]{1,0:T(1,128)}, f32[1,256]{1,0:T(1,128)S(1)}, u32[]{:S(2)}) copy-start(f32[1,256]{1,0:T(1,128)S(1)} %get-tuple-element.61) | copy-start | bytes 3076
  777.6 11.5 %copy-start.20 = (bf16[1024,2048]{1,0:T(8,128)(2,1)S(1)}, bf16[1024,2048]{1,0:T(8,128)(2,1)}, u32[]{:S(2)}) copy-start(bf16[1024,2048]{1,0:T(8,128)(2,1)} %get-tuple-element.30) | copy-start | bytes 12582916
  (22 other events, 86.3 us)

commit v4 on v3

--- a/solution.py
+++ b/solution.py
@@ -142,7 +142,7 @@
     return (query_grad, key_grad, value_grad)
 
 
-def gather_kernel(x_ref, c_ref, xg_ref, cg_ref, held, s1, r1, s2, r2, s3, r3, local):
+def gather_kernel(x_ref, c_ref, seg_ref, xg_ref, cg_ref, segs_ref, held, seg_s, seg_r, seg_l, s1, r1, s2, r2, s3, r3, local):
     f, s = lax.axis_index("fsdp"), lax.axis_index("sp")
     core, col, row = f % 2, (f // 2) % 2, f // 4
     f_x, f_y, f_c = f + 2 - 4 * col, f + 4 - 8 * row, f + 1 - 2 * core
@@ -170,6 +170,22 @@
             src_ref=ref, dst_ref=ref, send_sem=s1.at[0, 0], recv_sem=recv_sem,
             device_id=(f_c, s), device_id_type=MESH,
         ).wait_recv()
+
+    holds = f // 2 == s
+    keep_seg = pltpu.make_async_copy(seg_ref, segs_ref.at[core], seg_l.at[0])
+    give_seg = [
+        pltpu.make_async_remote_copy(
+            src_ref=seg_ref, dst_ref=segs_ref.at[core], send_sem=seg_s.at[k], recv_sem=seg_r.at[core],
+            device_id=((f + k) % 8, s), device_id_type=MESH,
+        )
+        for k in range(1, 8)
+    ]
+
+    @pl.when(holds)
+    def _():
+        keep_seg.start()
+        for copy in give_seg:
+            copy.start()
 
     kept = []
     for a, (src, _) in enumerate(pairs):
@@ -248,33 +264,46 @@
             pass_corner(*steps[i - 2])
     for a, k in steps:
         from_core(a, k)
+    for b in range(2):
+
+        @pl.when(f != 2 * s + b)
+        def _():
+            arrived(segs_ref.at[b], seg_r.at[b])
+
+    @pl.when(holds)
+    def _():
+        keep_seg.wait()
+        for copy in give_seg:
+            copy.wait_send()
+
     for copy in sent:
         copy.wait_send()
 
 
-def gather_both(x, c):
+def gather_both(x, c, segments):
     rows, width = x.shape
     piece = rows // 8
     shape = jax.ShapeDtypeStruct((2, 4, 8, piece, width), x.dtype)
     dma = pltpu.SemaphoreType.DMA
     return pl.pallas_call(
         gather_kernel,
-        out_shape=(shape, shape),
-        in_specs=[pl.BlockSpec(memory_space=pl.ANY)] * 2,
-        out_specs=[pl.BlockSpec(memory_space=pl.ANY)] * 2,
+        out_shape=(shape, shape, jax.ShapeDtypeStruct((2, *segments.shape), segments.dtype)),
+        in_specs=[pl.BlockSpec(memory_space=pl.ANY)] * 3,
+        out_specs=[pl.BlockSpec(memory_space=pl.ANY)] * 3,
         scratch_shapes=[
             pltpu.VMEM((2, 8, piece, width), x.dtype),
+            dma((8,)), dma((2,)), dma((1,)),
             dma((2, 8)), dma((2, 8)), dma((2, 4)), dma((2, 4)), dma((2, 9, 4)), dma((2, 9, 4)), dma((2, 2)),
         ],
         compiler_params=pltpu.CompilerParams(collective_id=1, has_side_effects=True),
         name="gather_tokens",
-    )(x, c)
+    )(x, c, segments)
 
 
 def reduce_kernel(
     sizes, steps,
-    down_ref, up_ref, qkv_ref, dense_ref, out_ref, back_ref, vec_ref, bias_ref,
-    g_down, g_up, g_qkv, g_dense, o_out, o_back, o_small,
+    up_ref, qkv_ref, dense_ref, out_ref, back_ref, vec_ref, bias_ref,
+    g_up, g_qkv, g_dense, o_out, o_back, o_small,
     line_a, line_b, turned, own, paired, block, crossed, reduced, homed, vec_in, small, small_in,
     in_s, in_r, mid_s, mid_r, end_s, end_r, own_l, keep_l,
     turn_s, turn_r, pair_s, pair_r, block_l, cross_s, cross_r, home_s, home_r, back_s, back_r, local,
@@ -331,7 +360,7 @@
     chunks = []
     offset = 0
     for ref, result, rows_of in (
-        (down_ref, g_down, sizes[0]), (up_ref, g_up, sizes[1]), (qkv_ref, g_qkv, sizes[2]), (turned, g_dense, sizes[3]),
+        (up_ref, g_up, sizes[0]), (qkv_ref, g_qkv, sizes[1]), (turned, g_dense, sizes[2]),
     ):
         first = 0
         for rows in rows_of:
@@ -339,7 +368,7 @@
             first += rows
             offset += rows
     count = len(chunks)
-    ahead = 5
+    ahead = 4
 
     def from_end(k):
         ref, _, first, rows, at = chunks[k]
@@ -562,17 +591,16 @@
     0: ("p0", "p1", "p2", "p3", "vec"),
     1: ("p4", "p5"),
     2: ("p6", "p7"),
-    3: ("small",),
+    3: ("turn", "small"),
     5: ("c0",),
-    7: ("h0",),
-    8: ("c1", "turn"),
-    10: ("h1",),
+    7: ("h0", "c1"),
+    9: ("h1",),
 }
 
 
-def reduce_all(down, up, qkv, dense, out_part, back_part, vec, bias, sizes, steps=STEPS):
-    width = down.shape[1]
-    dtype = down.dtype
+def reduce_all(up, qkv, dense, out_part, back_part, vec, bias, sizes, steps=STEPS):
+    width = up.shape[1]
+    dtype = up.dtype
     total = sum(sum(rows) for rows in sizes)
     count = sum(len(rows) for rows in sizes)
     largest = max(max(rows) for rows in sizes)
@@ -586,10 +614,10 @@
     return pl.pallas_call(
         functools.partial(reduce_kernel, sizes, steps),
         out_shape=(*grads, token, token, jax.ShapeDtypeStruct((16, vec.shape[2]), jnp.float32)),
-        in_specs=[anywhere] * 8,
-        out_specs=[anywhere] * 6 + [pl.BlockSpec(memory_space=pltpu.VMEM)],
+        in_specs=[anywhere] * 7,
+        out_specs=[anywhere] * 5 + [pl.BlockSpec(memory_space=pltpu.VMEM)],
         scratch_shapes=[
-            vmem((total, width), dtype), vmem((total, width), dtype), vmem((sum(sizes[3]), width), dtype),
+            vmem((total, width), dtype), vmem((total, width), dtype), vmem((sum(sizes[-1]), width), dtype),
             vmem((3, largest, width), dtype),
             vmem((2, 4, 2, 4, piece, width), dtype), vmem((2, 2, 4, piece, width), dtype),
             vmem((2, 3, 2, 4, piece, width), dtype), vmem((2, 2, 4, piece, width), dtype),
@@ -606,7 +634,7 @@
             collective_id=2, has_side_effects=True, vmem_limit_bytes=60 * 1024 * 1024
         ),
         name="reduce_all",
-    )(down, up, qkv, dense, out_part, back_part, vec, bias)
+    )(up, qkv, dense, out_part, back_part, vec, bias)
 
 
 def cut(rows, unit, first=False, last=False):
@@ -619,15 +647,13 @@
 
 
 def reduce_tokens(terms, partial_out, partial_back, vectors, biases):
-    down, up, qkv, dense = (term.astype(jnp.bfloat16) for term in terms)
+    up, qkv, dense = (term.astype(jnp.bfloat16) for term in terms)
     sizes = (
-        cut(down.shape[0], 64, first=True),
-        cut(up.shape[0], 64),
+        cut(up.shape[0], 64, first=True),
         cut(qkv.shape[0], 64),
         cut(dense.shape[0] // 8, 64, last=True),
     )
     *grads, output, weighted, sums = reduce_all(
-        down,
         up,
         qkv,
         dense,
@@ -707,13 +733,16 @@
 
     fast = (nf, ns, seq_local, HEADS) == (8, 4, 1, 8)
     if fast:
-        gathered, upstream = (
-            array.reshape(tokens, width) for array in gather_both(hidden_in[0], cotangent[0])
-        )
+        gathered, upstream, rows = gather_both(
+            hidden_in[0], cotangent[0], segments.reshape(8, seq_len // 8)
+        )
+        gathered, upstream = (array.reshape(tokens, width) for array in (gathered, upstream))
+        rows = rows.reshape(group, seq_len)
+        w_dense, gathered = lax.optimization_barrier((w_dense, gathered))
     else:
         gathered, upstream = gather_tokens(hidden_in), gather_tokens(cotangent)
-    rows = lax.all_gather(segments, "fsdp", axis=0, tiled=True)
-    rows = lax.dynamic_slice_in_dim(rows, s_place * group, group, 0)
+        rows = lax.all_gather(segments, "fsdp", axis=0, tiled=True)
+        rows = lax.dynamic_slice_in_dim(rows, s_place * group, group, 0)
 
     dense_in = lax.all_to_all(w_dense, "fsdp", split_axis=1, concat_axis=0, tiled=True)
     head_qkv = over_head(w_qkv, 0)
@@ -729,8 +758,10 @@
     hidden = times_transposed(normed_mlp, w_up) + own_part(b_up)
     activated, slope = gelu_pair(hidden)
     activated = activated.astype(jnp.bfloat16)
+    down_term = contract_rows(activated, upstream).astype(jnp.bfloat16)
+    grad_down_w = lax.psum(down_term, "sp").astype(jnp.float32)
+    normed, down_term = lax.optimization_barrier((normed, down_term))
     hidden_grad = (times_transposed(upstream, w_down) * slope).astype(jnp.bfloat16)
-    down_term = contract_rows(activated, upstream)
     up_term = contract_rows(hidden_grad, normed_mlp)
     mlp_norm_grad = times(hidden_grad, w_up)
 
@@ -785,13 +816,13 @@
         biases = jnp.concatenate([bias_out, bias_qkv, bias_up]).reshape(8, share)
         token_shape = (group, ns, 4, 2, piece, width)
         grads, output, weighted, sums = reduce_tokens(
-            (down_term, up_term, qkv_term, dense_term),
+            (up_term, qkv_term, dense_term),
             partial_out.reshape(token_shape),
             partial_back.reshape(token_shape),
             vectors,
             biases,
         )
-        grad_down_w, grad_up_w, grad_qkv_w, grad_dense_w = grads
+        grad_up_w, grad_qkv_w, grad_dense_w = grads
         output = output.reshape(hidden_in.shape)
         weighted = weighted.reshape(hidden_in.shape)
         vectors = sums[:4]
@@ -802,9 +833,9 @@
         output = scatter_tokens(rounded(partial_out))
         weighted = scatter_tokens(rounded(partial_back))
         dense_term = lax.all_to_all(dense_term, "fsdp", split_axis=0, concat_axis=1, tiled=True)
-        grad_down_w, grad_up_w, grad_qkv_w, grad_dense_w = (
+        grad_up_w, grad_qkv_w, grad_dense_w = (
             lax.psum(term.astype(jnp.bfloat16), "sp").astype(jnp.float32)
-            for term in (down_term, up_term, qkv_term, dense_term)
+            for term in (up_term, qkv_term, dense_term)
         )
     inputs = hidden_in.astype(jnp.float32)
     output = (inputs + (output.astype(jnp.float32) + (b_dense + b_down))).astype(jnp.bfloat16)

time: 810 us -> 696 us (0.86)
  Pallas kernels: 500 us -> 383 us
  between operations: 1.8 us -> 14.9 us
  blocking collectives: 9.16 us -> 0 us
    pallas_call x1, Pallas kernels: 395 us -> 281 us  [reduce_all(): pl.pallas_call(functools.partial(reduce_kernel, sizes, steps), out_shape=...]
    all_gather x1 -> x0, blocking collectives: 9.16 us -> none  [per_device(): rows = lax.all_gather(segments, 'fsdp', axis=0, tiled=True)]
    convert_element_type x4 -> x3, other arithmetic: 17.1 us -> 12.7 us  [reduce_tokens(): grad.astype(jnp.float32)]
  transfers between devices with their start and end apart: 1 -> 2, of which waited for: 0 -> 0; matrix products, arithmetic and copies ran while one was open for 19% -> 40% of each run, Pallas kernels for 13% -> 41%
where the time goes in v4:
time: 696 us; the launch traced here: 691 us
  Pallas kernels  383 us (55%)
  matrix products  168 us (24%)
  other arithmetic  86.6 us (12%)
  local copies, waits for them, and re-layouts  33.3 us (5%)
  between operations  14.9 us (2%)
    pallas_call x1, Pallas kernels, reduce_all(): pl.pallas_call(functools.partial(reduce_kernel, sizes, steps), out_shape=...  281 us
    pallas_call x1, Pallas kernels, gather_both(): pl.pallas_call(gather_kernel, out_shape=(shape, shape, jax.ShapeDtypeStru...  102 us
    dot_general x4, matrix products, times_transposed(): lax.dot_general(former, latter, (((1,), (1,)), ((), ())), preferred_eleme...  52.1 us
    dot_general x4, matrix products, times(): return jnp.dot(former, latter, preferred_element_type=jnp.float32)  49.9 us
    dot_general x4, matrix products, contract_rows(): lax.dot_general(former, latter, (((0,), (0,)), ((), ())), preferred_eleme...  43.1 us
  transfers between devices with their start and end apart: 2, of which 0 were waited for; matrix products, arithmetic and copies ran while one was open for 40% of the time, Pallas kernels for 41%

profile of v4, /device:TPU:0, one launch (start us, length us, event | category | flops | bytes accessed | tf_op | source)
XLA Modules:
  0.0 690.7 jit_solution(6913391160152748548)
XLA Ops:
  7.2 102.2 %gather_tokens.1 = (bf16[2,4,8,32,2048]{4,3,2,1,0:T(8,128)(2,1)}, bf16[2,4,8,32,2048]{4,3,2,1,0:T(8,128)(2,1)}, s32[2,8,128]{2,1,0:T(8,128)}) custom-call(bf16[256,2048]{1,0:T(8,128)(2,1)} %bitcast.127, bf16[256,2048]{1,0:T(8,128)(2,1)} %bitcast.145, s32[8,128]{1,0:T(8,128)} %bitcast.166), custom_call_target="tpu_custom_call" | custom-call | tf_op jit(solution)/shard_map/gather_tokens/pallas_call | solution.py:288
  111.7 4.2 all-to-all-start
  116.0 4.7 convert_reduce_fusion
  124.8 9.1 %fusion.9 = bf16[2048,2048]{1,0:T(8,128)(2,1)} fusion(bf16[2048,2048]{1,0:T(8,128)(2,1)} %bitcast.117, f32[2048]{0:T(1024)S(1)} %copy-done.31, f32[2048]{0:T(1024)S(1)} %copy-done.32, f32[2048]{0:T(1024)S(1)} %add_rsqrt_fusion, f32[2048]{0:T(1024)S(1)} %broadcast_multiply_fusion), kind=kLoop, calls=%fused_computation.11 | loop fusion | flops 25165824 | bytes 16809984 | tf_op jit(solution)/shard_map/convert_element_type | solution.py:755
  133.9 14.0 %multiply_convert_fusion.1 = (bf16[2048,1024]{1,0:T(8,128)(2,1)S(1)}, f32[2048,1024]{1,0:T(8,128)}) fusion(f32[1024]{0:T(1024)S(1)} %dynamic_slice.9, bf16[1024,2048]{1,0:T(8,128)(2,1)S(1)} %copy-done.38, bf16[2048,2048]{1,0:T(8,128)(2,1)} %bitcast.118, f32[2048]{0:T(1024)S(1)} %copy-done.42, f32[2048]{0:T(1024)S(1)} %copy-done.43, ...), kind=kOutput, calls=%fused_computation.31 | convolution fusion | flops 8627683328 | bytes 25202688 | tf_op jit(solution)/shard_map/dot_general | solution.py:36
  149.9 11.0 %convolution_convert_fusion = bf16[1024,2048]{1,0:T(8,128)(2,1)} fusion(bf16[2048,1024]{1,0:T(8,128)(2,1)S(1)} %get-tuple-element.70, bf16[2048,2048]{1,0:T(8,128)(2,1)S(1)} %bitcast.135), kind=kOutput, calls=%fused_computation.43 | convolution fusion | flops 8592031744 | bytes 16777216 | tf_op jit(solution)/shard_map/dot_general | solution.py:30
  163.7 5.0 convert_reduce_fusion.1
  169.5 9.3 %add_convert_fusion.2 = bf16[2048,768]{1,0:T(8,128)(2,1)S(1)} fusion(f32[768]{0:T(1024)S(1)} %dynamic_slice.10, bf16[2048,2048]{1,0:T(8,128)(2,1)} %fusion.9, bf16[768,2048]{1,0:T(8,128)(2,1)S(1)} %copy-done), kind=kOutput, calls=%fused_computation.37 | convolution fusion | flops 6445596672 | bytes 14683136 | tf_op jit(solution)/shard_map/dot_general | solution.py:36
  185.4 3.5 slice_negate_fusion.2
  188.9 4.9 fusion.53
  193.9 3.3 fusion.21
  197.2 3.4 fusion.20
  200.6 6.8 fusion.43
  207.5 16.5 %convert_reduce_fusion.2 = (f32[1024]{0:T(1024)S(1)}, bf16[2048,1024]{1,0:T(8,128)(2,1)}) fusion(f32[2048,1024]{1,0:T(8,128)} %get-tuple-element.71, f32[1024]{0:T(1024)S(1)} %dynamic_slice.9, bf16[2048,2048]{1,0:T(8,128)(2,1)} %bitcast.130, bf16[1024,2048]{1,0:T(8,128)(2,1)S(1)} %copy-done.40), kind=kOutput, calls=%fused_computation.25 | convolution fusion | flops 8617196544 | bytes 25174016 | tf_op jit(solution)/shard_map/dot_general | solution.py:36
  224.0 14.5 %convolution_convert_fusion.1.up_ref = bf16[1024,2048]{1,0:T(8,128)(2,1)} fusion(bf16[2048,1024]{1,0:T(8,128)(2,1)} %get-tuple-element.77, bf16[2048,2048]{1,0:T(8,128)(2,1)S(1)} %bitcast.123, f32[2048]{0:T(1024)S(1)} %copy-done.42, f32[2048]{0:T(1024)S(1)} %copy-done.43, f32[2048]{0:T(1024)S(1)} %add_rsqrt_fusion, f32[2048]{0:T(1024)S(1)} %broadcast_multiply_fusion), kind=kOutput, calls=%fused_computation.44 | convolution fusion | flops 8617197568 | bytes 16809984 | tf_op jit(solution)/shard_map/dot_general | solution.py:30
  238.5 14.1 %fusion.72 = f32[2048,2048]{1,0:T(8,128)} fusion(bf16[2048,1024]{1,0:T(8,128)(2,1)} %get-tuple-element.77, bf16[1024,2048]{1,0:T(8,128)(2,1)S(1)} %copy-done.39), kind=kOutput, calls=%fused_computation.138 | convolution fusion | flops 8589934592 | bytes 25165824 | tf_op jit(solution)/shard_map/dot_general | solution.py:42
  252.7 11.7 %fusion.71 = f32[2048,2048]{1,0:T(8,128)} fusion(bf16[2048,1024]{1,0:T(8,128)(2,1)S(1)} %copy-done.45, bf16[1024,2048]{1,0:T(8,128)(2,1)S(1)} %copy-done.41), kind=kOutput, calls=%fused_computation.137 | convolution fusion | flops 8589934592 | bytes 25165824 | tf_op jit(solution)/shard_map/dot_general | solution.py:42
  267.4 7.2 %convolution_convert_fusion.3.dense_ref = bf16[2048,256]{1,0:T(8,128)(2,1)} fusion(bf16[2048,2048]{1,0:T(8,128)(2,1)} %bitcast.131, bf16[2048,256]{1,0:T(8,128)(2,1)} %bitcast.146), kind=kOutput, calls=%fused_computation.49 | convolution fusion | flops 2148007936 | bytes 10485760 | tf_op jit(solution)/shard_map/dot_general | solution.py:30
  276.9 6.2 convolution_convert_fusion.4
  283.4 4.5 fusion.40
  287.9 5.1 multiply_reduce_fusion
  293.0 4.2 multiply_convert_fusion
  303.9 4.6 slice_multiply_fusion.2
  314.9 5.0 fusion.49
  319.9 7.0 %concatenate.121 = bf16[2048,768]{1,0:T(8,128)(2,1)} concatenate(bf16[2048,64]{1,0:T(8,128)(2,1)} %bitcast.151, bf16[2048,192]{1,0:T(8,128)(2,1)} %bitcast.141, bf16[2048,64]{1,0:T(8,128)(2,1)} %bitcast.150, bf16[2048,192]{1,0:T(8,128)(2,1)} %bitcast.142, bf16[2048,256]{1,0:T(8,128)(2,1)} %bitcast.143), dimensions={1} | concatenate | bytes 6291456 | tf_op jit(solution)/shard_map/concatenate | solution.py:788
  329.9 18.0 %fusion.10 = (f32[2048]{0:T(1024)S(1)}, f32[2048]{0:T(1024)S(1)}, f32[2048]{0:T(1024)S(1)}, f32[2048]{0:T(1024)S(1)}, bf16[2048,2048]{1,0:T(8,128)(2,1)}) fusion(bf16[2048,2048]{1,0:T(8,128)(2,1)} %bitcast.119, f32[2048]{0:T(1024)S(1)} %add_rsqrt_fusion, f32[2048]{0:T(1024)S(1)} %broadcast_multiply_fusion, f32[2048,2048]{1,0:T(8,128)} %fusion.72, ...), kind=kOutput, calls=%fused_computation.12 | convolution fusion | flops 6496968704 | bytes 39911424 | tf_op jit(solution)/shard_map/dot_general | solution.py:42
  348.5 12.2 %add_convert_fusion.1 = bf16[2048,2048]{1,0:T(8,128)(2,1)} fusion(f32[2048,2048]{1,0:T(8,128)} %fusion.71, bf16[2048,256]{1,0:T(8,128)(2,1)S(1)} %bitcast.147, bf16[2048,256]{1,0:T(8,128)(2,1)} %bitcast.149), kind=kOutput, calls=%fused_computation.17 | convolution fusion | flops 2155872256 | bytes 27262976 | tf_op jit(solution)/shard_map/dot_general | solution.py:36
  360.7 10.4 %convolution_convert_fusion.2.qkv_ref = bf16[768,2048]{1,0:T(8,128)(2,1)} fusion(bf16[2048,768]{1,0:T(8,128)(2,1)S(1)} %copy-done.13, bf16[2048,2048]{1,0:T(8,128)(2,1)} %fusion.9), kind=kOutput, calls=%fused_computation.45 | convolution fusion | flops 6444023808 | bytes 14680064 | tf_op jit(solution)/shard_map/dot_general | solution.py:30
  371.1 281.2 %reduce_all.1 = (bf16[1024,2048]{1,0:T(8,128)(2,1)}, bf16[768,2048]{1,0:T(8,128)(2,1)}, bf16[256,2048]{1,0:T(8,128)(2,1)}, bf16[8,32,2048]{2,1,0:T(8,128)(2,1)},...) custom-call(bf16[1024,2048]{1,0:T(8,128)(2,1)} %convolution_convert_fusion.1.up_ref, ...), custom_call_target="tpu_custom_call" | custom-call | tf_op jit(solution)/shard_map/reduce_all/pallas_call | solution.py:614
  663.6 5.4 convert_element_type.207
  669.0 4.4 convert_element_type.209
  676.4 6.7 convert_element_type.210
  (166 shorter events, 55.6 us)
Async XLA Ops:
  7.2 162.3 %copy-start = (bf16[768,2048]{1,0:T(8,128)(2,1)S(1)}, bf16[768,2048]{1,0:T(8,128)(2,1)}, u32[]{:S(2)}) copy-start(bf16[768,2048]{1,0:T(8,128)(2,1)} %param.21) | copy-start | bytes 9437188
  111.7 162.9 %all-to-all-start = ((bf16[256,8,256]{0,2,1:T(8,128)(2,1)}), bf16[256,8,256]{0,2,1:T(8,128)(2,1)}, u32[]{:S(2)}, u32[]{:S(2)}) async-start(bf16[256,8,256]{0,2,1:T(8,128)(2,1)} %bitcast.144), calls=%async_computation | async-start | bytes 2097152 | tf_op jit(solution)/shard_map/all_to_all | solution.py:747
  115.9 560.5 %all-reduce.4.cloned.1.call-start = ((), (), s32[]{:S(2)}) async-start(), calls=%async_computation.1 | async-start | bytes 8388608 | tf_op jit(solution)/shard_map/psum | solution.py:762
  116.0 8.8 %copy-start.31 = (f32[2048]{0:T(1024)S(1)}, f32[2048]{0:T(1024)}, u32[]{:S(2)}) copy-start(f32[2048]{0:T(1024)} %param.18) | copy-start | bytes 24580
  116.0 8.8 %copy-start.32 = (f32[2048]{0:T(1024)S(1)}, f32[2048]{0:T(1024)}, u32[]{:S(2)}) copy-start(f32[2048]{0:T(1024)} %param.17) | copy-start | bytes 24580
  124.8 9.1 %copy-start.38 = (bf16[1024,2048]{1,0:T(8,128)(2,1)S(1)}, bf16[1024,2048]{1,0:T(8,128)(2,1)}, u32[]{:S(2)}) copy-start(bf16[1024,2048]{1,0:T(8,128)(2,1)} %param.25) | copy-start | bytes 12582916
  124.8 9.1 %copy-start.42 = (f32[2048]{0:T(1024)S(1)}, f32[2048]{0:T(1024)}, u32[]{:S(2)}) copy-start(f32[2048]{0:T(1024)} %param.20) | copy-start | bytes 24580
  124.8 9.1 %copy-start.43 = (f32[2048]{0:T(1024)S(1)}, f32[2048]{0:T(1024)}, u32[]{:S(2)}) copy-start(f32[2048]{0:T(1024)} %param.19) | copy-start | bytes 24580
  124.8 25.1 %slice-start.4 = ((s8[8388608]{0:T(1024)(128)(4,1)}), s8[4194304]{0:T(1024)(128)(4,1)S(1)}, s32[]{:S(2)}) async-start(s8[8388608]{0:T(1024)(128)(4,1)} %bitcast.133), calls=%async_computation.6 | async-start | bytes 8388608
  133.9 16.0 %slice-start.5 = ((s8[8388608]{0:T(1024)(128)(4,1)}), s8[4194304]{0:T(1024)(128)(4,1)S(1)}, s32[]{:S(2)}) async-start(s8[8388608]{0:T(1024)(128)(4,1)} %bitcast.133), calls=%async_computation.7 | async-start | bytes 8388608
  185.3 8.5 %copy-start.6 = (f32[2,1024,1,32]{3,1,0,2:T(8,128)}, f32[2,1024,1,32]{3,1,0,2:T(8,128)S(1)}, u32[]{:S(2)}) copy-start(f32[2,1024,1,32]{3,1,0,2:T(8,128)S(1)} %multiply_bitcast_fusion.2) | copy-start | bytes 786436
  185.4 8.5 %copy-start.14 = (pred[1024,1024]{0,1:T(8,128)(4,1)S(1)}, pred[1024,1024]{0,1:T(8,128)(4,1)}, u32[]{:S(2)}) copy-start(pred[1024,1024]{0,1:T(8,128)(4,1)} %iota_compare_fusion) | copy-start | bytes 3145732
  185.4 8.5 %copy-start.20 = (bf16[2,1024,192]{2,1,0:T(8,128)(2,1)S(1)}, bf16[2,1024,192]{2,1,0:T(8,128)(2,1)}, u32[]{:S(2)}) copy-start(bf16[2,1024,192]{2,1,0:T(8,128)(2,1)} %get-tuple-element.47) | copy-start | bytes 2359300
  185.4 8.5 %copy-start.26 = (bf16[2,1024,192]{2,1,0:T(8,128)(2,1)S(1)}, bf16[2,1024,192]{2,1,0:T(8,128)(2,1)}, u32[]{:S(2)}) copy-start(bf16[2,1024,192]{2,1,0:T(8,128)(2,1)} %get-tuple-element.48) | copy-start | bytes 2359300
  197.2 10.3 %copy-start.2 = (f32[2,1024,1024]{1,2,0:T(8,128)}, f32[2,1024,1024]{1,2,0:T(8,128)S(1)}, u32[]{:S(2)}) copy-start(f32[2,1024,1024]{1,2,0:T(8,128)S(1)} %get-tuple-element.73) | copy-start | bytes 25165828
  200.6 6.9 copy-start.40
  200.6 23.4 %slice-start = ((s8[8388608]{0:T(1024)(128)(4,1)}), s8[4194304]{0:T(1024)(128)(4,1)S(1)}, s32[]{:S(2)}) async-start(s8[8388608]{0:T(1024)(128)(4,1)} %bitcast.121), calls=%async_computation.2 | async-start | bytes 8388608
  207.5 16.5 %slice-start.1 = ((s8[8388608]{0:T(1024)(128)(4,1)}), s8[4194304]{0:T(1024)(128)(4,1)S(1)}, s32[]{:S(2)}) async-start(s8[8388608]{0:T(1024)(128)(4,1)} %bitcast.121), calls=%async_computation.3 | async-start | bytes 8388608
  224.0 14.5 %copy-start.39 = (bf16[1024,2048]{1,0:T(8,128)(2,1)S(1)}, bf16[1024,2048]{1,0:T(8,128)(2,1)}, u32[]{:S(2)}) copy-start(bf16[1024,2048]{1,0:T(8,128)(2,1)} %param.25) | copy-start | bytes 12582916
  238.5 14.1 %copy-start.41 = (bf16[1024,2048]{1,0:T(8,128)(2,1)S(1)}, bf16[1024,2048]{1,0:T(8,128)(2,1)}, u32[]{:S(2)}) copy-start(bf16[1024,2048]{1,0:T(8,128)(2,1)} %param.27) | copy-start | bytes 12582916
  238.5 14.1 %copy-start.45 = (bf16[2048,1024]{1,0:T(8,128)(2,1)S(1)}, bf16[2048,1024]{1,0:T(8,128)(2,1)}, u32[]{:S(2)}) copy-start(bf16[2048,1024]{1,0:T(8,128)(2,1)} %copy-done.44) | copy-start | bytes 12582916
  252.6 11.8 %copy-start.3 = (bf16[1,256,2048]{2,1,0:T(8,128)(2,1)S(1)}, bf16[1,256,2048]{2,1,0:T(8,128)(2,1)}, u32[]{:S(2)}) copy-start(bf16[1,256,2048]{2,1,0:T(8,128)(2,1)} %param.15) | copy-start | bytes 3145732
  252.6 14.7 %copy-start.34 = (f32[2048]{0:T(1024)S(1)}, f32[2048]{0:T(1024)}, u32[]{:S(2)}) copy-start(f32[2048]{0:T(1024)} %param.24) | copy-start | bytes 24580
  252.6 14.7 %copy-start.35 = (f32[2048]{0:T(1024)S(1)}, f32[2048]{0:T(1024)}, u32[]{:S(2)}) copy-start(f32[2048]{0:T(1024)} %param.28) | copy-start | bytes 24580
  276.9 6.2 copy-start.15
  276.9 6.5 slice-start.3
  297.2 6.6 copy-start.7
  314.9 15.0 %copy-start.33 = (f32[2048]{0:T(1024)S(1)}, f32[2048]{0:T(1024)}, u32[]{:S(2)}) copy-start(f32[2048]{0:T(1024)} %param.17) | copy-start | bytes 24580
  329.9 18.6 %copy-start.23 = (bf16[2,1024,1,256]{3,1,0,2:T(8,128)(2,1)S(1)}, bf16[2,1024,1,256]{3,1,0,2:T(8,128)(2,1)}, u32[]{:S(2)}) copy-start(bf16[2,1024,1,256]{3,1,0,2:T(8,128)(2,1)} %copy.64) | copy-start | bytes 3145732
  348.5 12.2 %copy-start.13 = (bf16[2048,768]{1,0:T(8,128)(2,1)S(1)}, bf16[2048,768]{1,0:T(8,128)(2,1)}, u32[]{:S(2)}) copy-start(bf16[2048,768]{1,0:T(8,128)(2,1)} %concatenate.121) | copy-start | bytes 9437188
  657.9 11.1 %copy-start.19 = (bf16[1024,2048]{1,0:T(8,128)(2,1)S(1)}, bf16[1024,2048]{1,0:T(8,128)(2,1)}, u32[]{:S(2)}) copy-start(bf16[1024,2048]{1,0:T(8,128)(2,1)} %get-tuple-element.37) | copy-start | bytes 12582916
  660.8 22.3 %copy-start.37 = (f32[1,256]{1,0:T(1,128)}, f32[1,256]{1,0:T(1,128)S(1)}, u32[]{:S(2)}) copy-start(f32[1,256]{1,0:T(1,128)S(1)} %get-tuple-element.65) | copy-start | bytes 3076
  (22 other events, 86.7 us)
Sparse Core Ops, SparseCore 0:
  161.1 155.2 all-reduce.3

commit v5 on v4

--- a/solution.py
+++ b/solution.py
@@ -51,16 +51,15 @@
 
 
 def gelu_pair(hidden):
-    cumulative = 0.5 * (1.0 + jax.scipy.special.erf(hidden * ROOT_HALF))
+    cumulative = 0.5 * (1.0 + lax.erf(hidden * ROOT_HALF))
     return (
         hidden * cumulative,
-        cumulative + hidden * jnp.exp(-0.5 * hidden * hidden) / ROOT_TWO_PI,
-    )
-
-
-def rotary_tables(segment_rows):
-    length = segment_rows.shape[-1]
-    places = jnp.arange(length, dtype=jnp.int32)
+        cumulative + hidden * (jnp.exp(-0.5 * hidden * hidden) * (1.0 / ROOT_TWO_PI)),
+    )
+
+
+def document_starts(segment_rows):
+    places = jnp.arange(segment_rows.shape[-1], dtype=jnp.int32)
     changes = jnp.concatenate(
         [
             jnp.ones_like(segment_rows[..., :1]),
@@ -68,13 +67,27 @@
         ],
         axis=-1,
     )
-    first_place = lax.cummax(changes * places, axis=segment_rows.ndim - 1)
-    position = (places - first_place).astype(jnp.float32)
-    exponent = jnp.arange(0, ROT, 2).astype(jnp.float32) / ROT
-    frequency = 1.0 / jnp.power(10000.0, exponent)
-    angles = position[..., None] * frequency
+    return places, lax.cummax(changes * places, axis=segment_rows.ndim - 1)
+
+
+def frequencies():
+    return 1.0 / jnp.power(10000.0, jnp.arange(0, ROT, 2).astype(jnp.float32) / ROT)
+
+
+def rotary_tables(segment_rows):
+    places, starts = document_starts(segment_rows)
+    angles = (places - starts).astype(jnp.float32)[..., None] * frequencies()
     angles = jnp.concatenate([angles, angles], axis=-1)
     return (jnp.cos(angles), jnp.sin(angles))
+
+
+def head_tables(segment_rows):
+    places, starts = document_starts(segment_rows)
+    angles = (places - starts).astype(jnp.float32)[:, None, :] * frequencies()[None, :, None]
+    starts = jnp.broadcast_to(
+        starts.astype(jnp.float32)[:, None, :], (starts.shape[0], ROT, starts.shape[1])
+    )
+    return jnp.concatenate([jnp.cos(angles), jnp.sin(angles), starts], axis=1)
 
 
 def rotate(heads_part, cos_table, sin_table):
@@ -142,7 +155,195 @@
     return (query_grad, key_grad, value_grad)
 
 
-def gather_kernel(x_ref, c_ref, seg_ref, xg_ref, cg_ref, segs_ref, held, seg_s, seg_r, seg_l, s1, r1, s2, r2, s3, r3, local):
+def whole_block(array):
+    return pl.BlockSpec(array.shape, lambda *_: (0,) * array.ndim, pipeline_mode=pl.Buffered(1))
+
+
+def eight_rows(array):
+    return jnp.sum(array.reshape(array.shape[0] // 8, 8, array.shape[1]), axis=0)
+
+
+def upstream_kernel(c_ref, slope_ref, down_ref, dense_ref, grad_ref, context_ref, c_sum_ref, h_sum_ref):
+    @pl.when(pl.program_id(0) == 0)
+    def _():
+        c_sum_ref[...] = jnp.zeros_like(c_sum_ref)
+        h_sum_ref[...] = jnp.zeros_like(h_sum_ref)
+
+    hidden_grad = (times_transposed(c_ref[...], down_ref[...]) * slope_ref[...]).astype(grad_ref.dtype)
+    grad_ref[...] = hidden_grad
+    context_ref[...] = times(c_ref[...], dense_ref[...]).astype(context_ref.dtype)
+    c_sum_ref[...] += eight_rows(c_ref[...].astype(jnp.float32))
+    h_sum_ref[...] += eight_rows(hidden_grad.astype(jnp.float32))
+
+
+def upstream_parts(c, slope, w_down, dense, rows=256):
+    tokens, width = c.shape
+    units, columns = w_down.shape[0], dense.shape[1]
+
+    def tile(size):
+        return pl.BlockSpec((rows, size), lambda i: (i, 0))
+
+    def total(size):
+        return pl.BlockSpec((8, size), lambda i: (0, 0))
+
+    return pl.pallas_call(
+        upstream_kernel,
+        grid=(tokens // rows,),
+        out_shape=(
+            jax.ShapeDtypeStruct((tokens, units), c.dtype), jax.ShapeDtypeStruct((tokens, columns), c.dtype),
+            jax.ShapeDtypeStruct((8, width), jnp.float32), jax.ShapeDtypeStruct((8, units), jnp.float32),
+        ),
+        in_specs=[tile(width), tile(units), whole_block(w_down), whole_block(dense)],
+        out_specs=[tile(units), tile(columns), total(width), total(units)],
+        compiler_params=pltpu.CompilerParams(vmem_limit_bytes=48 * 1024 * 1024),
+        cost_estimate=pl.CostEstimate(
+            flops=2 * tokens * width * (units + columns), transcendentals=0,
+            bytes_accessed=2 * tokens * (width + 3 * units + columns) + 2 * width * (units + columns),
+        ),
+        name="upstream_parts",
+    )(c, slope, w_down, dense)
+
+
+def attention_kernel(packed_ref, grad_ref, table_ref, context_ref, back_ref, sum_ref, q_ref, k_ref, low_ref, score_ref, turned_ref):
+    length = packed_ref.shape[0]
+    size = 256
+    lanes = 128
+    lane = lax.broadcasted_iota(jnp.int32, (size, lanes), 1)
+    half = ROT // 2
+
+    def tables(rows):
+        table = turned_ref[rows, :]
+        cosine = jnp.where(lane < half, table, jnp.where(lane < ROT, pltpu.roll(table, half, 1), 1.0))
+        sine = jnp.where(lane < half, pltpu.roll(table, lanes - half, 1), jnp.where(lane < ROT, table, 0.0))
+        return cosine, jnp.where(lane < half, -sine, sine)
+
+    def swapped(array):
+        return jnp.where(lane < half, pltpu.roll(array, lanes - half, 1), pltpu.roll(array, half, 1))
+
+    def turn(array, cosine, sine):
+        front = array[:, :lanes]
+        return jnp.concatenate([front * cosine + swapped(front) * sine, array[:, lanes:]], axis=1)
+
+    blocks = length // size
+    for i in range(blocks):
+        rows = pl.ds(i * size, size)
+        turned_ref[rows, :] = jnp.transpose(table_ref[0, :, rows])
+        cosine, sine = tables(rows)
+        for part, ref in enumerate((q_ref, k_ref)):
+            array = packed_ref[rows, part * HEAD_DIM : (part + 1) * HEAD_DIM].astype(jnp.float32)
+            ref[rows, :] = turn(array, cosine, sine).astype(ref.dtype)
+
+    values = pl.ds(2 * HEAD_DIM, HEAD_DIM)
+    for i in range(blocks):
+        rows = pl.ds(i * size, size)
+        reach = (i + 1) * size
+        keys = pl.ds(0, reach)
+        scores = times_transposed(q_ref[rows, :], k_ref[keys, :]) * SCALE
+        gradient = times_transposed(grad_ref[rows, :], packed_ref[keys, values])
+        place = lax.broadcasted_iota(jnp.int32, (size, reach), 1)
+        query = lax.broadcasted_iota(jnp.int32, (size, reach), 0) + i * size
+        start = turned_ref[rows, ROT : ROT + 1].astype(jnp.int32)
+        allowed = (place >= start) & (place <= query)
+        scores = jnp.where(allowed, scores, NEGATIVE)
+        exponent = jnp.exp(scores - jnp.max(scores, axis=-1, keepdims=True))
+        attention = exponent / jnp.sum(exponent, axis=-1, keepdims=True)
+        low = attention.astype(low_ref.dtype)
+        low_ref[rows, keys] = low
+        context_ref[rows, :] = times(low, packed_ref[keys, values]).astype(context_ref.dtype)
+        centre = jnp.sum(attention * gradient, axis=-1, keepdims=True)
+        score_grad = (attention * (gradient - centre)).astype(score_ref.dtype)
+        score_ref[rows, keys] = score_grad
+        query_grad = times(score_grad, k_ref[keys, :]) * SCALE
+        cosine, sine = tables(rows)
+        back_ref[rows, :HEAD_DIM] = turn(query_grad, cosine, -sine).astype(back_ref.dtype)
+
+    for j in range(blocks):
+        keys = pl.ds(j * size, size)
+        rows = pl.ds(j * size, length - j * size)
+        key_grad = contract_rows(score_ref[rows, keys], q_ref[rows, :]) * SCALE
+        cosine, sine = tables(keys)
+        back_ref[keys, HEAD_DIM : 2 * HEAD_DIM] = turn(key_grad, cosine, -sine).astype(back_ref.dtype)
+        value_grad = contract_rows(low_ref[rows, keys], grad_ref[rows, :])
+        back_ref[keys, values] = value_grad.astype(back_ref.dtype)
+
+    @pl.when(pl.program_id(0) == 0)
+    def _():
+        sum_ref[...] = jnp.zeros_like(sum_ref)
+
+    for i in range(blocks):
+        sum_ref[...] += eight_rows(back_ref[pl.ds(i * size, size), :].astype(jnp.float32))
+
+
+def attend(packed, context_grad, table, length):
+    tokens, columns = packed.shape
+    low = packed.dtype
+
+    def tile(size):
+        return pl.BlockSpec((length, size), lambda i: (i, 0))
+
+    pairs = tokens * (length + 256) // 2
+    return pl.pallas_call(
+        attention_kernel,
+        grid=(tokens // length,),
+        out_shape=(
+            jax.ShapeDtypeStruct((tokens, HEAD_DIM), low), jax.ShapeDtypeStruct((tokens, columns), low),
+            jax.ShapeDtypeStruct((8, columns), jnp.float32),
+        ),
+        in_specs=[tile(columns), tile(HEAD_DIM), pl.BlockSpec((1, *table.shape[1:]), lambda i: (i, 0, 0))],
+        out_specs=[tile(HEAD_DIM), tile(columns), pl.BlockSpec((8, columns), lambda i: (0, 0))],
+        scratch_shapes=[
+            pltpu.VMEM((length, HEAD_DIM), low), pltpu.VMEM((length, HEAD_DIM), low),
+            pltpu.VMEM((length, length), low), pltpu.VMEM((length, length), low),
+            pltpu.VMEM((length, table.shape[1]), jnp.float32),
+        ],
+        compiler_params=pltpu.CompilerParams(vmem_limit_bytes=48 * 1024 * 1024),
+        cost_estimate=pl.CostEstimate(
+            flops=14 * pairs * HEAD_DIM, transcendentals=pairs, bytes_accessed=tokens * (4 * columns + 4 * HEAD_DIM + 512)
+        ),
+        name="attend",
+    )(packed, context_grad, table)
+
+
+def output_kernel(context_ref, act_ref, dense_ref, down_ref, out_ref):
+    total = times_transposed(context_ref[...], dense_ref[...]) + times(act_ref[...], down_ref[...])
+    out_ref[...] = total.astype(out_ref.dtype)
+
+
+def input_kernel(packed_ref, hidden_ref, qkv_ref, up_ref, norm_ref, out_ref):
+    total = times(packed_ref[...], qkv_ref[...]) * norm_ref[0:1, :]
+    total = total + times(hidden_ref[...], up_ref[...]) * norm_ref[2:3, :]
+    out_ref[...] = total.astype(out_ref.dtype)
+
+
+def two_products(kernel, name, former, latter, weights, rows=256):
+    tokens = former.shape[0]
+    width = weights[1].shape[1]
+    depth = former.shape[1] + latter.shape[1]
+
+    def tile(size):
+        return pl.BlockSpec((rows, size), lambda i: (i, 0))
+
+    return pl.pallas_call(
+        kernel,
+        grid=(tokens // rows,),
+        out_shape=jax.ShapeDtypeStruct((tokens, width), former.dtype),
+        in_specs=[tile(former.shape[1]), tile(latter.shape[1])] + [whole_block(a) for a in weights],
+        out_specs=tile(width),
+        compiler_params=pltpu.CompilerParams(vmem_limit_bytes=48 * 1024 * 1024),
+        cost_estimate=pl.CostEstimate(
+            flops=2 * tokens * depth * width, transcendentals=0,
+            bytes_accessed=2 * (tokens * (depth + width) + depth * width),
+        ),
+        name=name,
+    )(former, latter, *weights)
+
+
+def gather_kernel(
+    x_ref, c_ref, seg_ref, up_ref, qkv_ref, b_up_ref, b_qkv_ref, norm_ref,
+    xg_ref, cg_ref, segs_ref, normed_out, normed_mlp_out, packed_out, act_out, slope_out,
+    held, tile, w_up, w_qkv, normed, normed_mlp, packed, act, slope,
+    seg_s, seg_r, seg_l, s1, r1, s2, r2, s3, r3, local, w_l, tile_l, keep_l,
+):
     f, s = lax.axis_index("fsdp"), lax.axis_index("sp")
     core, col, row = f % 2, (f // 2) % 2, f // 4
     f_x, f_y, f_c = f + 2 - 4 * col, f + 4 - 8 * row, f + 1 - 2 * core
@@ -187,6 +388,11 @@
         for copy in give_seg:
             copy.start()
 
+    weights = [
+        pltpu.make_async_copy(up_ref, w_up, w_l.at[0]), pltpu.make_async_copy(qkv_ref, w_qkv, w_l.at[1])
+    ]
+    for copy in weights:
+        copy.start()
     kept = []
     for a, (src, _) in enumerate(pairs):
         own = pltpu.make_async_copy(src.at[pl.ds(f * piece, piece)], held.at[a, f], local.at[a, 0])
@@ -248,6 +454,46 @@
         arrived(out.at[:, z, g_y], r3.at[a, 4, k])
         for half in range(2):
             arrived(out.at[half, z, g_d], r3.at[a, 7 + half, k])
+
+    results = ((normed, normed_out), (normed_mlp, normed_mlp_out), (packed, packed_out), (act, act_out), (slope, slope_out))
+    size = 8 * piece
+
+    def keep(b, z, n):
+        rows = pl.ds(pl.multiple_of((b * 4 + z) * size, size), size)
+        return pltpu.make_async_copy(results[n][0].at[b], results[n][1].at[rows], keep_l.at[b, n])
+
+    def work(k):
+        z = (s + 4 - k) % 4
+        loads = [pltpu.make_async_copy(xg_ref.at[b, z], tile.at[b], tile_l.at[b]) for b in range(2)]
+        for copy in loads:
+            copy.start()
+        if k == 0:
+            for copy in weights:
+                copy.wait()
+        for b in range(2):
+            loads[b].wait()
+            if k:
+                for n in range(5):
+                    keep(b, (s + 5 - k) % 4, n).wait()
+
+            @pl.loop(0, 8)
+            def _(i):
+                inputs = tile[b, i].astype(jnp.float32)
+                centred = inputs - jnp.mean(inputs, axis=-1, keepdims=True)
+                variance = jnp.mean(centred * centred, axis=-1, keepdims=True)
+                scaled = centred * lax.rsqrt(variance + EPSILON)
+                rows = pl.ds(pl.multiple_of(i * piece, piece), piece)
+                low = normed.dtype
+                normed[b, rows, :] = (scaled * norm_ref[0:1, :] + norm_ref[1:2, :]).astype(low)
+                normed_mlp[b, rows, :] = (scaled * norm_ref[2:3, :] + norm_ref[3:4, :]).astype(low)
+
+            hidden = times_transposed(normed_mlp[b], w_up[...]) + b_up_ref[...]
+            packed[b] = (times_transposed(normed[b], w_qkv[...]) + b_qkv_ref[...]).astype(packed.dtype)
+            activated, grown = gelu_pair(hidden)
+            act[b] = activated.astype(act.dtype)
+            slope[b] = grown
+            for n in range(5):
+                keep(b, z, n).start()
 
     own0 = to_planes(0)
     own1 = to_planes(1)
@@ -262,8 +508,14 @@
             pass_on(*steps[i - 1])
         if 0 <= i - 2 < len(steps):
             pass_corner(*steps[i - 2])
-    for a, k in steps:
-        from_core(a, k)
+        if 5 <= i < 9:
+            from_core(0, i - 5)
+            work(i - 5)
+    for k in range(4):
+        from_core(1, k)
+    for b in range(2):
+        for n in range(5):
+            keep(b, (s + 1) % 4, n).wait()
     for b in range(2):
 
         @pl.when(f != 2 * s + b)
@@ -280,24 +532,38 @@
         copy.wait_send()
 
 
-def gather_both(x, c, segments):
+def gather_both(x, c, segments, w_up, w_qkv, b_up, b_qkv, norms):
     rows, width = x.shape
     piece = rows // 8
+    tokens = 8 * rows
+    units, columns = w_up.shape[0], w_qkv.shape[0]
     shape = jax.ShapeDtypeStruct((2, 4, 8, piece, width), x.dtype)
     dma = pltpu.SemaphoreType.DMA
+    vmem = pltpu.VMEM
+    anywhere = pl.BlockSpec(memory_space=pl.ANY)
+    inside = pl.BlockSpec(memory_space=pltpu.VMEM)
+    sizes = ((width, x.dtype), (width, x.dtype), (columns, x.dtype), (units, x.dtype), (units, jnp.float32))
     return pl.pallas_call(
         gather_kernel,
-        out_shape=(shape, shape, jax.ShapeDtypeStruct((2, *segments.shape), segments.dtype)),
-        in_specs=[pl.BlockSpec(memory_space=pl.ANY)] * 3,
-        out_specs=[pl.BlockSpec(memory_space=pl.ANY)] * 3,
+        out_shape=(
+            shape, shape, jax.ShapeDtypeStruct((2, *segments.shape), segments.dtype),
+            *(jax.ShapeDtypeStruct((tokens, size), kind) for size, kind in sizes),
+        ),
+        in_specs=[anywhere] * 5 + [inside] * 3,
+        out_specs=[anywhere] * 8,
         scratch_shapes=[
-            pltpu.VMEM((2, 8, piece, width), x.dtype),
+            vmem((2, 8, piece, width), x.dtype), vmem((2, 8, piece, width), x.dtype),
+            vmem(w_up.shape, w_up.dtype), vmem(w_qkv.shape, w_qkv.dtype),
+            *(vmem((2, 8 * piece, size), kind) for size, kind in sizes),
             dma((8,)), dma((2,)), dma((1,)),
             dma((2, 8)), dma((2, 8)), dma((2, 4)), dma((2, 4)), dma((2, 9, 4)), dma((2, 9, 4)), dma((2, 2)),
+            dma((2,)), dma((2,)), dma((2, 5)),
         ],
-        compiler_params=pltpu.CompilerParams(collective_id=1, has_side_effects=True),
+        compiler_params=pltpu.CompilerParams(
+            collective_id=1, has_side_effects=True, vmem_limit_bytes=48 * 1024 * 1024
+        ),
         name="gather_tokens",
-    )(x, c, segments)
+    )(x, c, segments, w_up, w_qkv, b_up.reshape(1, units), b_qkv.reshape(1, columns), norms)
 
 
 def reduce_kernel(
@@ -666,7 +932,20 @@
     return [grad.astype(jnp.float32) for grad in grads], output, weighted, sums
 
 
-def per_device(
+def own_tokens(hidden_in, cotangent, output, weighted, shift):
+    inputs = hidden_in.astype(jnp.float32)
+    output = (inputs + (output.astype(jnp.float32) + shift)).astype(jnp.bfloat16)
+    scaled, inverse = norm_scaled(inputs)
+    weighted = weighted.astype(jnp.float32)
+    first_mean = jnp.mean(weighted, axis=-1, keepdims=True)
+    second_mean = jnp.mean(weighted * scaled, axis=-1, keepdims=True)
+    input_grad = (
+        cotangent.astype(jnp.float32) + inverse * (weighted - first_mean - scaled * second_mean)
+    ).astype(jnp.bfloat16)
+    return output, input_grad
+
+
+def by_collectives(
     hidden_in,
     segments,
     ln1_gain,
@@ -731,18 +1010,9 @@
         share = vector.shape[0] // nf
         return lax.dynamic_slice_in_dim(vector, f_place * share, share, 0)
 
-    fast = (nf, ns, seq_local, HEADS) == (8, 4, 1, 8)
-    if fast:
-        gathered, upstream, rows = gather_both(
-            hidden_in[0], cotangent[0], segments.reshape(8, seq_len // 8)
-        )
-        gathered, upstream = (array.reshape(tokens, width) for array in (gathered, upstream))
-        rows = rows.reshape(group, seq_len)
-        w_dense, gathered = lax.optimization_barrier((w_dense, gathered))
-    else:
-        gathered, upstream = gather_tokens(hidden_in), gather_tokens(cotangent)
-        rows = lax.all_gather(segments, "fsdp", axis=0, tiled=True)
-        rows = lax.dynamic_slice_in_dim(rows, s_place * group, group, 0)
+    gathered, upstream = gather_tokens(hidden_in), gather_tokens(cotangent)
+    rows = lax.all_gather(segments, "fsdp", axis=0, tiled=True)
+    rows = lax.dynamic_slice_in_dim(rows, s_place * group, group, 0)
 
     dense_in = lax.all_to_all(w_dense, "fsdp", split_axis=1, concat_axis=0, tiled=True)
     head_qkv = over_head(w_qkv, 0)
@@ -760,7 +1030,6 @@
     activated = activated.astype(jnp.bfloat16)
     down_term = contract_rows(activated, upstream).astype(jnp.bfloat16)
     grad_down_w = lax.psum(down_term, "sp").astype(jnp.float32)
-    normed, down_term = lax.optimization_barrier((normed, down_term))
     hidden_grad = (times_transposed(upstream, w_down) * slope).astype(jnp.bfloat16)
     up_term = contract_rows(hidden_grad, normed_mlp)
     mlp_norm_grad = times(hidden_grad, w_up)
@@ -810,44 +1079,16 @@
     bias_out = own_part(jnp.sum(upstream.astype(jnp.float32), axis=0))
     bias_qkv = jnp.sum(packed_grad.astype(jnp.float32), axis=0)
     bias_up = jnp.sum(hidden_grad.astype(jnp.float32), axis=0)
-    if fast:
-        share = width // nf
-        vectors = jnp.pad(vectors.reshape(4, nf, share).transpose(1, 0, 2), ((0, 0), (0, 4), (0, 0)))
-        biases = jnp.concatenate([bias_out, bias_qkv, bias_up]).reshape(8, share)
-        token_shape = (group, ns, 4, 2, piece, width)
-        grads, output, weighted, sums = reduce_tokens(
-            (up_term, qkv_term, dense_term),
-            partial_out.reshape(token_shape),
-            partial_back.reshape(token_shape),
-            vectors,
-            biases,
-        )
-        grad_up_w, grad_qkv_w, grad_dense_w = grads
-        output = output.reshape(hidden_in.shape)
-        weighted = weighted.reshape(hidden_in.shape)
-        vectors = sums[:4]
-        bias_out, bias_qkv, bias_up = sums[8], sums[9:12].reshape(-1), sums[12:16].reshape(-1)
-    else:
-        vectors = lax.psum_scatter(vectors, "fsdp", scatter_dimension=1, tiled=True)
-        vectors, bias_out, bias_qkv, bias_up = lax.psum((vectors, bias_out, bias_qkv, bias_up), "sp")
-        output = scatter_tokens(rounded(partial_out))
-        weighted = scatter_tokens(rounded(partial_back))
-        dense_term = lax.all_to_all(dense_term, "fsdp", split_axis=0, concat_axis=1, tiled=True)
-        grad_up_w, grad_qkv_w, grad_dense_w = (
-            lax.psum(term.astype(jnp.bfloat16), "sp").astype(jnp.float32)
-            for term in (up_term, qkv_term, dense_term)
-        )
-    inputs = hidden_in.astype(jnp.float32)
-    output = (inputs + (output.astype(jnp.float32) + (b_dense + b_down))).astype(jnp.bfloat16)
-    own_scaled, own_inverse = norm_scaled(inputs)
-    weighted = weighted.astype(jnp.float32)
-    first_mean = jnp.mean(weighted, axis=-1, keepdims=True)
-    second_mean = jnp.mean(weighted * own_scaled, axis=-1, keepdims=True)
-    input_grad = (
-        cotangent.astype(jnp.float32)
-        + own_inverse * (weighted - first_mean - own_scaled * second_mean)
-    ).astype(jnp.bfloat16)
-
+    vectors = lax.psum_scatter(vectors, "fsdp", scatter_dimension=1, tiled=True)
+    vectors, bias_out, bias_qkv, bias_up = lax.psum((vectors, bias_out, bias_qkv, bias_up), "sp")
+    output = scatter_tokens(rounded(partial_out))
+    weighted = scatter_tokens(rounded(partial_back))
+    dense_term = lax.all_to_all(dense_term, "fsdp", split_axis=0, concat_axis=1, tiled=True)
+    grad_up_w, grad_qkv_w, grad_dense_w = (
+        lax.psum(term.astype(jnp.bfloat16), "sp").astype(jnp.float32)
+        for term in (up_term, qkv_term, dense_term)
+    )
+    output, input_grad = own_tokens(hidden_in, cotangent, output, weighted, b_dense + b_down)
     return (
         output,
         input_grad,
@@ -864,6 +1105,123 @@
         grad_down_w,
         bias_out,
     )
+
+
+def norm_sums(weights, term, column_sums, gain, shift):
+    weights = weights.astype(jnp.float32)
+    column_sums = column_sums[:, None]
+    scaled = jnp.sum(weights * (term.astype(jnp.float32) - column_sums * shift), axis=0) / gain
+    return scaled, jnp.sum(weights * column_sums, axis=0)
+
+
+def by_kernels(
+    hidden_in,
+    segments,
+    ln1_gain,
+    ln1_bias,
+    ln2_gain,
+    ln2_bias,
+    w_qkv,
+    b_qkv,
+    w_dense,
+    b_dense,
+    w_up,
+    b_up,
+    w_down,
+    b_down,
+    cotangent,
+):
+    width = hidden_in.shape[2]
+    seq_len = segments.shape[1]
+    nf, ns = lax.axis_size("fsdp"), lax.axis_size("sp")
+    group = nf // ns
+    tokens = group * seq_len
+    share = width // nf
+    f_place = lax.axis_index("fsdp")
+
+    def own_part(vector):
+        size = vector.shape[0] // nf
+        return lax.dynamic_slice_in_dim(vector, f_place * size, size, 0)
+
+    norms = jnp.stack([ln1_gain, ln1_bias, ln2_gain, ln2_bias])
+    _, upstream, rows, normed, normed_mlp, packed, activated, slope = gather_both(
+        hidden_in[0],
+        cotangent[0],
+        segments.reshape(8, seq_len // 8),
+        w_up,
+        w_qkv,
+        own_part(b_up),
+        own_part(b_qkv),
+        norms,
+    )
+    upstream = upstream.reshape(tokens, width)
+    w_dense, upstream = lax.optimization_barrier((w_dense, upstream))
+    dense_in = lax.all_to_all(w_dense, "fsdp", split_axis=1, concat_axis=0, tiled=True)
+    down_term = contract_rows(activated, upstream).astype(jnp.bfloat16)
+    grad_down_w = lax.psum(down_term, "sp").astype(jnp.float32)
+    slope, down_term = lax.optimization_barrier((slope, down_term))
+    hidden_grad, context_grad, c_sums, h_sums = upstream_parts(upstream, slope, w_down, dense_in)
+    context, packed_grad, p_sums = attend(
+        packed, context_grad, head_tables(rows.reshape(group, seq_len)), seq_len
+    )
+    partial_out = two_products(
+        output_kernel, "partial_out", context, activated, (dense_in, w_down)
+    )
+    partial_back = two_products(
+        input_kernel, "partial_back", packed_grad, hidden_grad, (w_qkv, w_up, norms)
+    )
+    up_term = contract_rows(hidden_grad, normed_mlp).astype(jnp.bfloat16)
+    qkv_term = contract_rows(packed_grad, normed).astype(jnp.bfloat16)
+    dense_term = contract_rows(upstream, context).astype(jnp.bfloat16)
+    bias_up, bias_qkv = jnp.sum(h_sums, axis=0), jnp.sum(p_sums, axis=0)
+    bias_out = own_part(jnp.sum(c_sums, axis=0))
+    vectors = jnp.stack(
+        norm_sums(w_qkv, qkv_term, bias_qkv, ln1_gain, ln1_bias)
+        + norm_sums(w_up, up_term, bias_up, ln2_gain, ln2_bias)
+    )
+    vectors = jnp.pad(vectors.reshape(4, nf, share).transpose(1, 0, 2), ((0, 0), (0, 4), (0, 0)))
+    biases = jnp.concatenate([bias_out, bias_qkv, bias_up]).reshape(8, share)
+    token_shape = (group, ns, 4, 2, seq_len // (ns * nf), width)
+    grads, output, weighted, sums = reduce_tokens(
+        (up_term, qkv_term, dense_term),
+        partial_out.reshape(token_shape),
+        partial_back.reshape(token_shape),
+        vectors,
+        biases,
+    )
+    grad_up_w, grad_qkv_w, grad_dense_w = grads
+    bias_out = sums[8]
+    output, input_grad = own_tokens(
+        hidden_in,
+        cotangent,
+        output.reshape(hidden_in.shape),
+        weighted.reshape(hidden_in.shape),
+        b_dense + b_down,
+    )
+    return (
+        output,
+        input_grad,
+        sums[0],
+        sums[1],
+        sums[2],
+        sums[3],
+        grad_qkv_w,
+        sums[9:12].reshape(-1),
+        grad_dense_w,
+        bias_out,
+        grad_up_w,
+        sums[12:16].reshape(-1),
+        grad_down_w,
+        bias_out,
+    )
+
+
+def per_device(hidden_in, *rest):
+    sizes = (lax.axis_size("fsdp"), lax.axis_size("sp"), hidden_in.shape[0])
+    shapes = (hidden_in.shape[1] % 256, hidden_in.shape[2] % (8 * HEAD_DIM), rest[9].shape[0] % 256)
+    if sizes == (8, 4, 1) and HEADS == 8 and not any(shapes):
+        return by_kernels(hidden_in, *rest)
+    return by_collectives(hidden_in, *rest)
 
 
 def solution(mesh):

time: 696 us -> 638 us (0.917)
  Pallas kernels: 383 us -> 514 us
  matrix products: 168 us -> 48.2 us
  other arithmetic: 86.6 us -> 32.9 us
  local copies, waits for them, and re-layouts: 33.3 us -> 15.8 us
    dot_general x14 -> x0, matrix products: 125 us -> none  [the longest x4 52.1 us: times_transposed(): lax.dot_general(former, latter, (((1,), (1,)), ((), ())), preferred_eleme...]
    pallas_call x0 -> x4, Pallas kernels: none -> 67.5 us  [the longest x2 37 us: two_products(): pl.pallas_call(kernel, grid=(tokens // rows,), out_shape=jax.ShapeDtypeSt...]
    pallas_call x1, Pallas kernels: 281 us -> 322 us  [reduce_all(): pl.pallas_call(functools.partial(reduce_kernel, sizes, steps), out_shape=...]
    pallas_call x1, Pallas kernels: 102 us -> 124 us  [gather_both(): pl.pallas_call(gather_kernel, out_shape=(shape, shape, jax.ShapeDtypeStru...]
    convert_element_type x7 -> x5, other arithmetic: 27.5 us -> 10.6 us  [the longest x1 6.66 us: by_kernels(): grad_down_w = lax.psum(down_term, 'sp').astype(jnp.float32)]
    reduce_sum x5, other arithmetic: 12.7 us -> 1.97 us  [the longest x1 1.44 us: own_tokens(): first_mean = jnp.mean(weighted, axis=-1, keepdims=True)]
    concatenate x2 -> x0, local copies, waits for them, and re-layouts: 9.52 us -> none  [the longest x1 6.97 us: per_device(): jnp.concatenate([unrotate(query_grad, cos_table, sin_table), unrotate(key...]
  transfers between devices with their start and end apart: 2 -> 2, of which waited for: 0 -> 0; matrix products, arithmetic and copies ran while one was open for 40% -> 12% of each run, Pallas kernels for 41% -> 62%
where the time goes in v5:
time: 638 us; the launch traced here: 629 us
  Pallas kernels  514 us (81%)
  matrix products  48.2 us (8%)
  other arithmetic  32.9 us (5%)
  local copies, waits for them, and re-layouts  15.8 us (2%)
  between operations  14.8 us (2%)
    pallas_call x1, Pallas kernels, reduce_all(): pl.pallas_call(functools.partial(reduce_kernel, sizes, steps), out_shape=...  322 us
    pallas_call x1, Pallas kernels, gather_both(): pl.pallas_call(gather_kernel, out_shape=(shape, shape, jax.ShapeDtypeStru...  124 us
    dot_general x4, matrix products, contract_rows(): lax.dot_general(former, latter, (((0,), (0,)), ((), ())), preferred_eleme...  48.2 us
    pallas_call x2, Pallas kernels, two_products(): pl.pallas_call(kernel, grid=(tokens // rows,), out_shape=jax.ShapeDtypeSt...  37 us
    pallas_call x1, Pallas kernels, upstream_parts(): pl.pallas_call(upstream_kernel, grid=(tokens // rows,), out_shape=(jax.Sh...  17.4 us
    convert_element_type x3, other arithmetic, reduce_tokens(): grad.astype(jnp.float32)  15 us
    pallas_call x1, Pallas kernels, attend(): pl.pallas_call(attention_kernel, grid=(tokens // length,), out_shape=(jax...  13.1 us
  transfers between devices with their start and end apart: 2, of which 0 were waited for; matrix products, arithmetic and copies ran while one was open for 12% of the time, Pallas kernels for 62%

profile of v5, /device:TPU:0, one launch (start us, length us, event | category | flops | bytes accessed | tf_op | source)
XLA Modules:
  0.0 629.0 jit_solution(4405277791705504406)
XLA Ops:
  7.2 0.8 dynamic_slice.10
  8.0 0.7 dynamic_slice.9
  8.7 0.8 pad_maximum_fusion.1.norm_ref
  9.5 1.2 copy-done
  10.7 1.2 copy-done.2
  11.9 0.7 copy-done.4
  12.6 124.4 %gather_tokens.1 = (bf16[2,4,8,32,2048]{4,3,2,1,0:T(8,128)(2,1)}, bf16[2,4,8,32,2048]{4,3,2,1,0:T(8,128)(2,1)}, s32[2,8,128]{2,1,0:T(8,128)S(1)}, bf16[2048,2048...) custom-call(bf16[256,2048]{1,0:T(8,128)(2,1)S(1)} %bitcast.67, ...), custom_call_target="tpu_custom_call" | custom-call | tf_op jit(solution)/shard_map/gather_tokens/pallas_call | solution.py:546
  137.0 1.7 copy-done.5
  138.7 1.0 copy.41
  139.7 3.6 all-to-all-start
  143.3 14.5 %convolution_convert_fusion.1 = bf16[1024,2048]{1,0:T(8,128)(2,1)} fusion(bf16[2048,1024]{1,0:T(8,128)(2,1)} %get-tuple-element.40.act_ref, bf16[2048,2048]{1,0:T(8,128)(2,1)} %bitcast.98), kind=kOutput, calls=%fused_computation.9 | convolution fusion | flops 8592031744 | bytes 16777216 | tf_op jit(solution)/shard_map/dot_general | solution.py:30
  159.1 1.8 multiply_cosine_fusion
  161.0 1.0 pad_maximum_fusion.table_ref
  162.7 17.4 %upstream_parts.1 = (bf16[2048,1024]{1,0:T(8,128)(2,1)}, bf16[2048,256]{1,0:T(8,128)(2,1)S(1)}, f32[8,2048]{1,0:T(8,128)S(1)}, f32[8,1024]{1,0:T(8,128)S(1)}) custom-call(bf16[2048,2048]{1,0:T(8,128)(2,1)} %bitcast.99, f32[2048,1024]{1,0:T(8,128)} %get-tuple-element.41.slope_ref, bf16[1024,2048]{1,0:T(8,128)(2,1)} %down_ref.3, bf16[2048,256]{1,0:T(8,128)(2,1)S(1)} %bitcast.69), custom_call_target="tpu_custom_call" | custom-call | flops 10737418240 | bytes 27262976 | tf_op jit(solution)/shard_map/upstream_parts/pallas_call | solution.py:189
  180.1 1.0 copy-done.10
  181.1 1.2 copy-done.11
  182.4 13.1 %attend.1 = (bf16[2048,256]{1,0:T(8,128)(2,1)S(1)}, bf16[2048,768]{1,0:T(8,128)(2,1)}, f32[8,768]{1,0:T(8,128)S(1)}) custom-call(bf16[2048,768]{1,0:T(8,128)(2,1)} %copy-done.5, bf16[2048,256]{1,0:T(8,128)(2,1)S(1)} %copy-done.11, f32[2,128,1024]{2,1,0:T(8,128)S(1)} %pad_maximum_fusion.table_ref), custom_call_target="tpu_custom_call" | custom-call | flops 4697620480 | bytes 9437184 | tf_op jit(solution)/shard_map/attend/pallas_call | solution.py:285
  195.5 1.0 copy-done.8
  196.5 1.2 copy-done.9
  197.7 15.8 %partial_out.1 = bf16[2048,2048]{1,0:T(8,128)(2,1)} custom-call(bf16[2048,256]{1,0:T(8,128)(2,1)S(1)} %copy-done.9, bf16[2048,1024]{1,0:T(8,128)(2,1)} %get-tuple-element.40.act_ref, bf16[2048,256]{1,0:T(8,128)(2,1)S(1)} %bitcast.70, bf16[1024,2048]{1,0:T(8,128)(2,1)} %down_ref.3), custom_call_target="tpu_custom_call" | custom-call | flops 10737418240 | bytes 18874368 | tf_op jit(solution)/shard_map/partial_out/pallas_call | solution.py:326
  213.5 14.3 %fusion = (f32[2048]{0:T(1024)S(1)}, f32[2048]{0:T(1024)S(1)}, bf16[1024,2048]{1,0:T(8,128)(2,1)}) fusion(bf16[1024,2048]{1,0:T(8,128)(2,1)S(1)} %copy-done.12, f32[2048]{0:T(1024)S(1)} %copy-done.21, f32[1024]{0:T(1024)S(1)} %reduce_sum.102, bf16[2048,1024]{1,0:T(8,128)(2,1)S(1)} %copy-done.24, bf16[2048,2048]{1,0:T(8,128)(2,1)} %get-tuple-element.44), kind=kOutput, calls=%fused_computation.2 | convolution fusion | flops 8608804864 | bytes 21000192 | tf_op jit(solution)/shard_map/dot_general | solution.py:30
  227.9 11.8 %fusion.2 = (f32[2048]{0:T(1024)S(1)}, f32[2048]{0:T(1024)S(1)}, bf16[768,2048]{1,0:T(8,128)(2,1)}) fusion(bf16[768,2048]{1,0:T(8,128)(2,1)S(1)} %copy-done.13, f32[2048]{0:T(1024)S(1)} %copy-done.22, f32[768]{0:T(1024)S(1)} %reduce_sum.99, bf16[2048,768]{1,0:T(8,128)(2,1)S(1)} %copy-done.6, bf16[2048,2048]{1,0:T(8,128)(2,1)} %get-tuple-element.49), kind=kOutput, calls=%fused_computation.6 | convolution fusion | flops 6456602624 | bytes 17853440 | tf_op jit(solution)/shard_map/dot_general | solution.py:30
  241.1 7.6 %convolution_convert_fusion.3.dense_ref = bf16[2048,256]{1,0:T(8,128)(2,1)} fusion(bf16[2048,2048]{1,0:T(8,128)(2,1)} %bitcast.100, bf16[2048,256]{1,0:T(8,128)(2,1)S(1)} %copy-done.9), kind=kOutput, calls=%fused_computation.14 | convolution fusion | flops 2148007936 | bytes 10485760 | tf_op jit(solution)/shard_map/dot_general | solution.py:30
  248.7 21.2 %partial_back.1 = bf16[2048,2048]{1,0:T(8,128)(2,1)} custom-call(bf16[2048,768]{1,0:T(8,128)(2,1)S(1)} %copy-done.7, bf16[2048,1024]{1,0:T(8,128)(2,1)} %get-tuple-element.43.hidden_ref, bf16[768,2048]{1,0:T(8,128)(2,1)} %qkv_ref.3, bf16[1024,2048]{1,0:T(8,128)(2,1)} %up_ref.3, f32[4,2048]{1,0:T(4,128)S(1)} %pad_maximum_fusion.1.norm_ref), custom_call_target="tpu_custom_call" | custom-call | flops 15032385536 | bytes 23068672 | tf_op jit(solution)/shard_map/partial_back/pallas_call | solution.py:326
  269.9 321.8 %reduce_all.1 = (bf16[1024,2048]{1,0:T(8,128)(2,1)}, bf16[768,2048]{1,0:T(8,128)(2,1)}, bf16[256,2048]{1,0:T(8,128)(2,1)}, bf16[8,32,2048]{2,1,0:T(8,128)(2,1)},...) custom-call(bf16[1024,2048]{1,0:T(8,128)(2,1)} %get-tuple-element.73.up_ref, ...), custom_call_target="tpu_custom_call" | custom-call | tf_op jit(solution)/shard_map/reduce_all/pallas_call | solution.py:880
  591.7 1.5 convert_element_type.132
  593.1 1.4 convert_reduce_fusion.1
  594.7 5.5 convert_element_type.127
  600.7 2.8 convert_element_type.128
  603.5 6.8 %convert_element_type.129 = f32[1024,2048]{1,0:T(8,128)} convert(bf16[1024,2048]{1,0:T(8,128)(2,1)} %get-tuple-element.59) | non-fusion elementwise | flops 2097152 | bytes 12582912 | tf_op jit(solution)/shard_map/convert_element_type | solution.py:932
  612.0 2.4 fusion.12
  614.5 6.7 %convert_element_type.130 = f32[1024,2048]{1,0:T(8,128)} convert(bf16[1024,2048]{1,0:T(8,128)(2,1)} %all-reduce.4.cloned.1.call-done) | non-fusion elementwise | flops 2097152 | bytes 12582912 | tf_op jit(solution)/shard_map/convert_element_type | solution.py:1161
  (84 shorter events, 6.5 us)
Async XLA Ops:
  9.4 1.2 copy-start
  10.7 1.2 copy-start.2
  11.9 0.7 copy-start.4
  12.6 126.1 %copy-start.14 = (bf16[256,2048]{1,0:T(8,128)(2,1)S(1)}, bf16[256,2048]{1,0:T(8,128)(2,1)}, u32[]{:S(2)}) copy-start(bf16[256,2048]{1,0:T(8,128)(2,1)} %param.23) | copy-start | bytes 3145732
  137.0 1.7 copy-start.5
  139.7 23.0 %all-to-all-start = ((bf16[256,8,256]{2,0,1:T(8,128)(2,1)}), bf16[256,8,256]{2,0,1:T(8,128)(2,1)S(1)}, u32[]{:S(2)}, u32[]{:S(2)}) async-start(bf16[256,8,256]{2,0,1:T(8,128)(2,1)} %bitcast.61), calls=%async_computation | async-start | bytes 2097152 | tf_op jit(solution)/shard_map/all_to_all | solution.py:1159
  143.3 471.2 %all-reduce.4.cloned.1.call-start = ((), (), s32[]{:S(2)}) async-start(), calls=%async_computation.1 | async-start | bytes 8388608 | tf_op jit(solution)/shard_map/psum | solution.py:1161
  157.8 3.1 copy-start.19
  157.8 3.1 copy-start.20
  157.8 4.2 copy-start.1
  180.1 1.0 copy-start.10
  181.1 1.3 copy-start.11
  195.5 1.0 copy-start.8
  196.5 1.2 copy-start.9
  197.7 15.8 %copy-start.12 = (bf16[1024,2048]{1,0:T(8,128)(2,1)S(1)}, bf16[1024,2048]{1,0:T(8,128)(2,1)}, u32[]{:S(2)}) copy-start(bf16[1024,2048]{1,0:T(8,128)(2,1)} %up_ref.3) | copy-start | bytes 12582916
  197.7 15.8 %copy-start.21 = (f32[2048]{0:T(1024)S(1)}, f32[2048]{0:T(1024)}, u32[]{:S(2)}) copy-start(f32[2048]{0:T(1024)} %param.20) | copy-start | bytes 24580
  197.7 15.8 %copy-start.24 = (bf16[2048,1024]{1,0:T(8,128)(2,1)S(1)}, bf16[2048,1024]{1,0:T(8,128)(2,1)}, u32[]{:S(2)}) copy-start(bf16[2048,1024]{1,0:T(8,128)(2,1)} %get-tuple-element.43.hidden_ref) | copy-start | bytes 12582916
  213.5 14.4 %copy-start.16 = (f32[2048]{0:T(1024)S(1)}, f32[2048]{0:T(1024)}, u32[]{:S(2)}) copy-start(f32[2048]{0:T(1024)} %param.19) | copy-start | bytes 24580
  213.5 14.4 %copy-start.6 = (bf16[2048,768]{1,0:T(8,128)(2,1)S(1)}, bf16[2048,768]{1,0:T(8,128)(2,1)}, u32[]{:S(2)}) copy-start(bf16[2048,768]{1,0:T(8,128)(2,1)} %get-tuple-element.48.packed_ref) | copy-start | bytes 9437188
  213.5 14.4 %copy-start.13 = (bf16[768,2048]{1,0:T(8,128)(2,1)S(1)}, bf16[768,2048]{1,0:T(8,128)(2,1)}, u32[]{:S(2)}) copy-start(bf16[768,2048]{1,0:T(8,128)(2,1)} %qkv_ref.3) | copy-start | bytes 9437188
  213.5 14.4 %copy-start.22 = (f32[2048]{0:T(1024)S(1)}, f32[2048]{0:T(1024)}, u32[]{:S(2)}) copy-start(f32[2048]{0:T(1024)} %param.18) | copy-start | bytes 24580
  227.9 11.8 %copy-start.17 = (f32[2048]{0:T(1024)S(1)}, f32[2048]{0:T(1024)}, u32[]{:S(2)}) copy-start(f32[2048]{0:T(1024)} %param.17) | copy-start | bytes 24580
  241.1 7.6 %copy-start.7 = (bf16[2048,768]{1,0:T(8,128)(2,1)S(1)}, bf16[2048,768]{1,0:T(8,128)(2,1)}, u32[]{:S(2)}) copy-start(bf16[2048,768]{1,0:T(8,128)(2,1)} %get-tuple-element.48.packed_ref) | copy-start | bytes 9437188
  594.7 5.5 copy-start.18
  603.5 8.5 %copy-start.3 = (bf16[1,256,2048]{2,1,0:T(8,128)(2,1)S(1)}, bf16[1,256,2048]{2,1,0:T(8,128)(2,1)}, u32[]{:S(2)}) copy-start(bf16[1,256,2048]{2,1,0:T(8,128)(2,1)} %param.29) | copy-start | bytes 3145732
  603.5 8.5 %copy-start.15 = (bf16[8,32,2048]{2,1,0:T(8,128)(2,1)S(1)}, bf16[8,32,2048]{2,1,0:T(8,128)(2,1)}, u32[]{:S(2)}) copy-start(bf16[8,32,2048]{2,1,0:T(8,128)(2,1)} %get-tuple-element.54) | copy-start | bytes 3145732
  611.5 9.6 %copy-start.23 = (f32[1,256]{1,0:T(1,128)}, f32[1,256]{1,0:T(1,128)S(1)}, u32[]{:S(2)}) copy-start(f32[1,256]{1,0:T(1,128)S(1)} %get-tuple-element.66) | copy-start | bytes 3076
Sparse Core Ops, SparseCore 0:
  158.0 189.1 all-reduce.3

commit v6 on v2

v6 whole, which is shorter than its diff:
```python
import functools
import math

import jax
import jax.numpy as jnp
from jax import lax
from jax.experimental import pallas as pl
from jax.experimental.pallas import tpu as pltpu
from jax.sharding import PartitionSpec as P

MESH = pl.DeviceIdType.MESH

HEADS = 8
HEAD_DIM = 256
ROT = 64


EPSILON = 1e-05
NEGATIVE = -1e30
ROOT_HALF = 0.7071067811865476
ROOT_TWO_PI = 2.5066282746310002
SCALE = 1.0 / math.sqrt(HEAD_DIM)


def rounded(array):
    return lax.reduce_precision(array.astype(jnp.float32), 8, 7).astype(jnp.bfloat16)


def contract_rows(former, latter):
    return lax.dot_general(former, latter, (((0,), (0,)), ((), ())), preferred_element_type=jnp.float32)


def times_transposed(former, latter):
    return lax.dot_general(former, latter, (((1,), (1,)), ((), ())), preferred_element_type=jnp.float32)


def times(former, latter):
    return jnp.dot(former, latter, preferred_element_type=jnp.float32)


def norm_scaled(inputs):
    average = jnp.mean(inputs, axis=-1, keepdims=True)
    centred = inputs - average
    variance = jnp.mean(centred * centred, axis=-1, keepdims=True)
    inverse = lax.rsqrt(variance + EPSILON)
    return (centred * inverse, inverse)


def gelu_pair(hidden):
    cumulative = 0.5 * (1.0 + lax.erf(hidden * ROOT_HALF))
    return (hidden * cumulative, cumulative + hidden * (jnp.exp(-0.5 * hidden * hidden) * (1.0 / ROOT_TWO_PI)))


def document_starts(segment_rows):
    places = jnp.arange(segment_rows.shape[-1], dtype=jnp.int32)
    changes = jnp.concatenate([jnp.ones_like(segment_rows[..., :1]), (segment_rows[..., 1:] != segment_rows[..., :-1]).astype(jnp.int32)], axis=-1)
    return (places, lax.cummax(changes * places, axis=segment_rows.ndim - 1))


def frequencies():
    return 1.0 / jnp.power(10000.0, jnp.arange(0, ROT, 2).astype(jnp.float32) / ROT)


def rotary_tables(segment_rows):
    places, starts = document_starts(segment_rows)
    angles = (places - starts).astype(jnp.float32)[..., None] * frequencies()
    angles = jnp.concatenate([angles, angles], axis=-1)
    return (jnp.cos(angles), jnp.sin(angles))


def head_tables(segment_rows):
    places, starts = document_starts(segment_rows)
    angles = (places - starts).astype(jnp.float32)[:, None, :] * frequencies()[None, :, None]
    starts = jnp.broadcast_to(starts.astype(jnp.float32)[:, None, :], (starts.shape[0], ROT, starts.shape[1]))
    return jnp.concatenate([jnp.cos(angles), jnp.sin(angles), starts], axis=1)


def rotate(heads_part, cos_table, sin_table):
    half_rot = ROT // 2
    turned = heads_part[..., :ROT]
    swapped = jnp.concatenate([-turned[..., half_rot:], turned[..., :half_rot]], axis=-1)
    turned = turned * cos_table[..., None, :] + swapped * sin_table[..., None, :]
    return jnp.concatenate([turned, heads_part[..., ROT:]], axis=-1)


def unrotate(grads_part, cos_table, sin_table):
    half_rot = ROT // 2
    turned = grads_part[..., :ROT]
    along_sin = turned * sin_table[..., None, :]
    back_turn = jnp.concatenate([along_sin[..., half_rot:], -along_sin[..., :half_rot]], axis=-1)
    turned = turned * cos_table[..., None, :] + back_turn
    return jnp.concatenate([turned, grads_part[..., ROT:]], axis=-1)


def build_mask(segment_rows):
    places = jnp.arange(segment_rows.shape[-1], dtype=jnp.int32)
    return (segment_rows[:, :, None] == segment_rows[:, None, :]) & (places[None, :] <= places[:, None])


def attention_scores(queries, keys_rot):
    return jnp.einsum('bqhd,bkhd->bhqk', queries, keys_rot, preferred_element_type=jnp.float32) * SCALE


def attend_forward(queries, keys_rot, values, mask):
    scores = jnp.where(mask[:, None], attention_scores(queries, keys_rot), NEGATIVE)
    row_top = jnp.max(scores, axis=-1, keepdims=True)
    exponent = jnp.exp(scores - row_top)
    row_total = jnp.sum(exponent, axis=-1, keepdims=True)
    attention = (exponent / row_total).astype(jnp.bfloat16)
    context = jnp.einsum('bhqk,bkhd->bqhd', attention, values, preferred_element_type=jnp.float32)
    return (context.astype(jnp.bfloat16), row_top + jnp.log(row_total))


def attend_backward(queries, keys_rot, values, mask, log_total, context_grad):
    scores = attention_scores(queries, keys_rot)
    attention = jnp.where(mask[:, None], jnp.exp(scores - log_total), 0.0)
    value_grad = jnp.einsum('bhqk,bqhd->bkhd', attention.astype(jnp.bfloat16), context_grad, preferred_element_type=jnp.float32)
    attention_grad = jnp.einsum('bqhd,bkhd->bhqk', context_grad, values, preferred_element_type=jnp.float32)
    row_centre = jnp.sum(attention * attention_grad, axis=-1, keepdims=True)
    score_grad = (attention * (attention_grad - row_centre)).astype(jnp.bfloat16)
    query_grad = jnp.einsum('bhqk,bkhd->bqhd', score_grad, keys_rot, preferred_element_type=jnp.float32) * SCALE
    key_grad = jnp.einsum('bhqk,bqhd->bkhd', score_grad, queries, preferred_element_type=jnp.float32) * SCALE
    return (query_grad, key_grad, value_grad)


def whole_block(array):
    return pl.BlockSpec(array.shape, lambda *_: (0,) * array.ndim, pipeline_mode=pl.Buffered(1))


def eight_rows(array):
    return jnp.sum(array.reshape(array.shape[0] // 8, 8, array.shape[1]), axis=0)


def upstream_kernel(c_ref, slope_ref, down_ref, dense_ref, grad_ref, context_ref, c_sum_ref, h_sum_ref):
    @pl.when(pl.program_id(0) == 0)
    def _():
        c_sum_ref[...] = jnp.zeros_like(c_sum_ref)
        h_sum_ref[...] = jnp.zeros_like(h_sum_ref)
    hidden_grad = (times_transposed(c_ref[...], down_ref[...]) * slope_ref[...]).astype(grad_ref.dtype)
    grad_ref[...] = hidden_grad
    context_ref[...] = times(c_ref[...], dense_ref[...]).astype(context_ref.dtype)
    c_sum_ref[...] += eight_rows(c_ref[...].astype(jnp.float32))
    h_sum_ref[...] += eight_rows(hidden_grad.astype(jnp.float32))


def upstream_parts(c, slope, w_down, dense, rows=256):
    tokens, width = c.shape
    units, columns = (w_down.shape[0], dense.shape[1])

    def tile(size):
        return pl.BlockSpec((rows, size), lambda i: (i, 0))

    def total(size):
        return pl.BlockSpec((8, size), lambda i: (0, 0))
    return pl.pallas_call(upstream_kernel, grid=(tokens // rows,), out_shape=(jax.ShapeDtypeStruct((tokens, units), c.dtype),
        jax.ShapeDtypeStruct((tokens, columns), c.dtype), jax.ShapeDtypeStruct((8, width), jnp.float32), jax.ShapeDtypeStruct((8, units),
        jnp.float32)), in_specs=[tile(width), tile(units), whole_block(w_down), whole_block(dense)], out_specs=[tile(units), tile(columns),
        total(width), total(units)], compiler_params=pltpu.CompilerParams(vmem_limit_bytes=48 * 1024 * 1024),
        cost_estimate=pl.CostEstimate(flops=2 * tokens * width * (units + columns), transcendentals=0,
        bytes_accessed=2 * tokens * (width + 3 * units + columns) + 2 * width * (units + columns)), name='upstream_parts')(c, slope, w_down, dense)


def attention_kernel(packed_ref, grad_ref, table_ref, context_ref, back_ref, sum_ref, q_ref, k_ref, low_ref, score_ref, turned_ref):
    length = packed_ref.shape[0]
    size = 256
    lanes = 128
    lane = lax.broadcasted_iota(jnp.int32, (size, lanes), 1)
    half = ROT // 2

    def tables(rows):
        table = turned_ref[rows, :]
        cosine = jnp.where(lane < half, table, jnp.where(lane < ROT, pltpu.roll(table, half, 1), 1.0))
        sine = jnp.where(lane < half, pltpu.roll(table, lanes - half, 1), jnp.where(lane < ROT, table, 0.0))
        return (cosine, jnp.where(lane < half, -sine, sine))

    def swapped(array):
        return jnp.where(lane < half, pltpu.roll(array, lanes - half, 1), pltpu.roll(array, half, 1))

    def turn(array, cosine, sine):
        front = array[:, :lanes]
        return jnp.concatenate([front * cosine + swapped(front) * sine, array[:, lanes:]], axis=1)
    blocks = length // size
    for i in range(blocks):
        rows = pl.ds(i * size, size)
        turned_ref[rows, :] = jnp.transpose(table_ref[0, :, rows])
        cosine, sine = tables(rows)
        for part, ref in enumerate((q_ref, k_ref)):
            array = packed_ref[rows, part * HEAD_DIM:(part + 1) * HEAD_DIM].astype(jnp.float32)
            ref[rows, :] = turn(array, cosine, sine).astype(ref.dtype)
    values = pl.ds(2 * HEAD_DIM, HEAD_DIM)
    for i in range(blocks):
        rows = pl.ds(i * size, size)
        reach = (i + 1) * size
        keys = pl.ds(0, reach)
        scores = times_transposed(q_ref[rows, :], k_ref[keys, :]) * SCALE
        gradient = times_transposed(grad_ref[rows, :], packed_ref[keys, values])
        place = lax.broadcasted_iota(jnp.int32, (size, reach), 1)
        query = lax.broadcasted_iota(jnp.int32, (size, reach), 0) + i * size
        start = turned_ref[rows, ROT:ROT + 1].astype(jnp.int32)
        allowed = (place >= start) & (place <= query)
        scores = jnp.where(allowed, scores, NEGATIVE)
        exponent = jnp.exp(scores - jnp.max(scores, axis=-1, keepdims=True))
        attention = exponent / jnp.sum(exponent, axis=-1, keepdims=True)
        low = attention.astype(low_ref.dtype)
        low_ref[rows, keys] = low
        context_ref[rows, :] = times(low, packed_ref[keys, values]).astype(context_ref.dtype)
        centre = jnp.sum(attention * gradient, axis=-1, keepdims=True)
        score_grad = (attention * (gradient - centre)).astype(score_ref.dtype)
        score_ref[rows, keys] = score_grad
        query_grad = times(score_grad, k_ref[keys, :]) * SCALE
        cosine, sine = tables(rows)
        back_ref[rows, :HEAD_DIM] = turn(query_grad, cosine, -sine).astype(back_ref.dtype)
    for j in range(blocks):
        keys = pl.ds(j * size, size)
        rows = pl.ds(j * size, length - j * size)
        key_grad = contract_rows(score_ref[rows, keys], q_ref[rows, :]) * SCALE
        cosine, sine = tables(keys)
        back_ref[keys, HEAD_DIM:2 * HEAD_DIM] = turn(key_grad, cosine, -sine).astype(back_ref.dtype)
        value_grad = contract_rows(low_ref[rows, keys], grad_ref[rows, :])
        back_ref[keys, values] = value_grad.astype(back_ref.dtype)

    @pl.when(pl.program_id(0) == 0)
    def _():
        sum_ref[...] = jnp.zeros_like(sum_ref)
    for i in range(blocks):
        sum_ref[...] += eight_rows(back_ref[pl.ds(i * size, size), :].astype(jnp.float32))


def attend(packed, context_grad, table, length):
    tokens, columns = packed.shape
    low = packed.dtype

    def tile(size):
        return pl.BlockSpec((length, size), lambda i: (i, 0))
    pairs = tokens * (length + 256) // 2
    return pl.pallas_call(attention_kernel, grid=(tokens // length,), out_shape=(jax.ShapeDtypeStruct((tokens, HEAD_DIM), low),
        jax.ShapeDtypeStruct((tokens, columns), low), jax.ShapeDtypeStruct((8, columns), jnp.float32)), in_specs=[tile(columns), tile(HEAD_DIM),
        pl.BlockSpec((1, *table.shape[1:]), lambda i: (i, 0, 0))], out_specs=[tile(HEAD_DIM), tile(columns), pl.BlockSpec((8, columns), lambda i: (0,
        0))], scratch_shapes=[pltpu.VMEM((length, HEAD_DIM), low), pltpu.VMEM((length, HEAD_DIM), low), pltpu.VMEM((length, length), low),
        pltpu.VMEM((length, length), low), pltpu.VMEM((length, table.shape[1]), jnp.float32)],
        compiler_params=pltpu.CompilerParams(vmem_limit_bytes=48 * 1024 * 1024), cost_estimate=pl.CostEstimate(flops=14 * pairs * HEAD_DIM,
        transcendentals=pairs, bytes_accessed=tokens * (4 * columns + 4 * HEAD_DIM + 512)), name='attend')(packed, context_grad, table)


def remote(src, dst, send_sem, recv_sem, device):
    return pltpu.make_async_remote_copy(src_ref=src, dst_ref=dst, send_sem=send_sem, recv_sem=recv_sem, device_id=device, device_id_type=MESH)


def copied(src, dst, sem):
    copy = pltpu.make_async_copy(src, dst, sem)
    copy.start()
    return copy


def meet(f, s):
    barrier = pltpu.get_barrier_semaphore()
    for k in range(1, 8):
        pl.semaphore_signal(barrier, inc=1, device_id=((f + k) % 8, s), device_id_type=MESH)
    for k in range(1, 4):
        pl.semaphore_signal(barrier, inc=1, device_id=(f, (s + k) % 4), device_id_type=MESH)
    pl.semaphore_wait(barrier, 10)


def neighbours(f):
    f_x, f_y = (f + 2 - 4 * (f // 2 % 2), f + 4 - 8 * (f // 4))
    return (f_x, f_y, f + 1 - 2 * (f % 2), f_x + f_y - f)


def gather_kernel(x_ref, c_ref, seg_ref, up_ref, qkv_ref, b_up_ref, b_qkv_ref, norm_ref, xg_ref, cg_ref, segs_ref, normed_out, normed_mlp_out,
    packed_out, act_out, slope_out, held, tile, w_up, w_qkv, normed, normed_mlp, packed, act, slope, seg_s, seg_r, seg_l, s1, r1, s2, r2, s3, r3,
    local, w_l, tile_l, keep_l):
    f, s = (lax.axis_index('fsdp'), lax.axis_index('sp'))
    core = f % 2
    f_x, f_y, f_c, f_d = neighbours(f)
    piece = xg_ref.shape[3]
    meet(f, s)
    pairs = ((x_ref, xg_ref), (c_ref, cg_ref))
    sent = []

    def send(src, dst, send_sem, recv_sem, device):
        copy = remote(src, dst, send_sem, recv_sem, device)
        copy.start()
        sent.append(copy)

    def arrived(ref, recv_sem):
        remote(ref, ref, s1.at[0, 0], recv_sem, (f_c, s)).wait_recv()
    holds = f // 2 == s
    keep_seg = pltpu.make_async_copy(seg_ref, segs_ref.at[core], seg_l.at[0])
    give_seg = [remote(seg_ref, segs_ref.at[core], seg_s.at[k], seg_r.at[core], ((f + k) % 8, s)) for k in range(1, 8)]

    @pl.when(holds)
    def _():
        keep_seg.start()
        for copy in give_seg:
            copy.start()
    weights = [pltpu.make_async_copy(up_ref, w_up, w_l.at[0]), pltpu.make_async_copy(qkv_ref, w_qkv, w_l.at[1])]
    for copy in weights:
        copy.start()
    kept = []
    for a, (src, _) in enumerate(pairs):
        own = pltpu.make_async_copy(src.at[pl.ds(f * piece, piece)], held.at[a, f], local.at[a, 0])
        own.start()
        kept.append(own)
        for k in range(1, 8):
            j = (f + k) % 8
            send(src.at[pl.ds(j * piece, piece)], held.at[a, f], s1.at[a, k], r1.at[a, k], (j, s))

    def to_planes(a):
        out = pairs[a][1]
        kept[a].wait()
        for k in range(1, 8):
            arrived(held.at[a, (f + 8 - k) % 8], r1.at[a, k])
        for k in range(1, 4):
            plane = (s + k) % 4
            send(held.at[a, pl.ds(2 * plane, 2)], out.at[:, s, f], s2.at[a, k], r2.at[a, k], (f, plane))
        own = pltpu.make_async_copy(held.at[a, pl.ds(2 * s, 2)], out.at[:, s, f], local.at[a, 1])
        own.start()
        return own

    def spread(a, k):
        out = pairs[a][1]
        z = (s + 4 - k) % 4
        if k:
            arrived(out.at[:, z, f], r2.at[a, k])
        ref = out.at[:, z, f]
        send(ref, ref, s3.at[a, 0, k], r3.at[a, 0, k], (f_x, s))
        send(ref, ref, s3.at[a, 1, k], r3.at[a, 1, k], (f_y, s))
        send(ref, ref, s3.at[a, 2, k], r3.at[a, 2, k], (f_c, s))

    def pass_on(a, k):
        out = pairs[a][1]
        z = (s + 4 - k) % 4
        ref = out.at[:, z, f_x]
        arrived(ref, r3.at[a, 0, k])
        send(out.at[0, z, f_x], out.at[0, z, f_x], s3.at[a, 5, k], r3.at[a, 5, k], (f_y, s))
        send(ref, ref, s3.at[a, 3, k], r3.at[a, 3, k], (f_c, s))
        ref = out.at[:, z, f_y]
        arrived(ref, r3.at[a, 1, k])
        send(out.at[1, z, f_y], out.at[1, z, f_y], s3.at[a, 6, k], r3.at[a, 6, k], (f_x, s))
        send(ref, ref, s3.at[a, 4, k], r3.at[a, 4, k], (f_c, s))

    def pass_corner(a, k):
        out = pairs[a][1]
        z = (s + 4 - k) % 4
        for half in range(2):
            ref = out.at[half, z, f_d]
            arrived(ref, r3.at[a, 5 + half, k])
            send(ref, ref, s3.at[a, 7 + half, k], r3.at[a, 7 + half, k], (f_c, s))

    def from_core(a, k):
        out = pairs[a][1]
        z = (s + 4 - k) % 4
        g_x, g_y, _, g_d = neighbours(f_c)
        arrived(out.at[:, z, f_c], r3.at[a, 2, k])
        arrived(out.at[:, z, g_x], r3.at[a, 3, k])
        arrived(out.at[:, z, g_y], r3.at[a, 4, k])
        for half in range(2):
            arrived(out.at[half, z, g_d], r3.at[a, 7 + half, k])
    results = ((normed, normed_out), (normed_mlp, normed_mlp_out), (packed, packed_out), (act, act_out), (slope, slope_out))
    size = 8 * piece

    def keep(b, z, n):
        rows = pl.ds(pl.multiple_of((b * 4 + z) * size, size), size)
        return pltpu.make_async_copy(results[n][0].at[b], results[n][1].at[rows], keep_l.at[b, n])

    def work(k):
        z = (s + 4 - k) % 4
        loads = [pltpu.make_async_copy(xg_ref.at[b, z], tile.at[b], tile_l.at[b]) for b in range(2)]
        for copy in loads:
            copy.start()
        if k == 0:
            for copy in weights:
                copy.wait()
        for b in range(2):
            loads[b].wait()
            if k:
                for n in range(5):
                    keep(b, (s + 5 - k) % 4, n).wait()

            @pl.loop(0, 8)
            def _(i):
                inputs = tile[b, i].astype(jnp.float32)
                centred = inputs - jnp.mean(inputs, axis=-1, keepdims=True)
                variance = jnp.mean(centred * centred, axis=-1, keepdims=True)
                scaled = centred * lax.rsqrt(variance + EPSILON)
                rows = pl.ds(pl.multiple_of(i * piece, piece), piece)
                low = normed.dtype
                normed[b, rows, :] = (scaled * norm_ref[0:1, :] + norm_ref[1:2, :]).astype(low)
                normed_mlp[b, rows, :] = (scaled * norm_ref[2:3, :] + norm_ref[3:4, :]).astype(low)
            hidden = times_transposed(normed_mlp[b], w_up[...]) + b_up_ref[...]
            packed[b] = (times_transposed(normed[b], w_qkv[...]) + b_qkv_ref[...]).astype(packed.dtype)
            activated, grown = gelu_pair(hidden)
            act[b] = activated.astype(act.dtype)
            slope[b] = grown
            for n in range(5):
                keep(b, z, n).start()
    own0 = to_planes(0)
    own1 = to_planes(1)
    steps = [(a, k) for a in range(2) for k in range(4)]
    for i in range(len(steps) + 2):
        if i < len(steps):
            a, k = steps[i]
            if k == 0:
                (own0 if a == 0 else own1).wait()
            spread(a, k)
        if 0 <= i - 1 < len(steps):
            pass_on(*steps[i - 1])
        if 0 <= i - 2 < len(steps):
            pass_corner(*steps[i - 2])
        if 5 <= i < 9:
            from_core(0, i - 5)
            work(i - 5)
    for k in range(4):
        from_core(1, k)
    for b in range(2):
        for n in range(5):
            keep(b, (s + 1) % 4, n).wait()
    for b in range(2):

        @pl.when(f != 2 * s + b)
        def _():
            arrived(segs_ref.at[b], seg_r.at[b])

    @pl.when(holds)
    def _():
        keep_seg.wait()
        for copy in give_seg:
            copy.wait_send()
    for copy in sent:
        copy.wait_send()


def gather_both(x, c, segments, w_up, w_qkv, b_up, b_qkv, norms):
    rows, width = x.shape
    piece = rows // 8
    tokens = 8 * rows
    units, columns = (w_up.shape[0], w_qkv.shape[0])
    shape = jax.ShapeDtypeStruct((2, 4, 8, piece, width), x.dtype)
    dma = pltpu.SemaphoreType.DMA
    vmem = pltpu.VMEM
    anywhere = pl.BlockSpec(memory_space=pl.ANY)
    inside = pl.BlockSpec(memory_space=pltpu.VMEM)
    sizes = ((width, x.dtype), (width, x.dtype), (columns, x.dtype), (units, x.dtype), (units, jnp.float32))
    return pl.pallas_call(gather_kernel, out_shape=(shape, shape, jax.ShapeDtypeStruct((2, *segments.shape), segments.dtype),
        *(jax.ShapeDtypeStruct((tokens, size), kind) for size, kind in sizes)), in_specs=[anywhere] * 5 + [inside] * 3, out_specs=[anywhere] * 8,
        scratch_shapes=[vmem((2, 8, piece, width), x.dtype), vmem((2, 8, piece, width), x.dtype), vmem(w_up.shape, w_up.dtype), vmem(w_qkv.shape,
        w_qkv.dtype), *(vmem((2, 8 * piece, size), kind) for size, kind in sizes), dma((8,)), dma((2,)), dma((1,)), dma((2, 8)), dma((2, 8)), dma((2,
        4)), dma((2, 4)), dma((2, 9, 4)), dma((2, 9, 4)), dma((2, 2)), dma((2,)), dma((2,)), dma((2, 5))],
        compiler_params=pltpu.CompilerParams(collective_id=1, has_side_effects=True, vmem_limit_bytes=48 * 1024 * 1024), name='gather_tokens')(x, c,
        segments, w_up, w_qkv, b_up.reshape(1, units), b_qkv.reshape(1, columns), norms)


def finish_kernel(down_ref, dense_ref, hidden_ref, normed_mlp_ref, packed_ref, normed_ref, act_ref, context_ref, up_w_ref, down_w_ref, qkv_w_ref,
    dense_w_ref, norm_ref, h_col_ref, p_col_ref, bias_ref, g_down, g_up, g_qkv, g_dense, o_out, o_back, part, paired, kept, crossed, homed, o_small,
    line_a, line_b, turned, big, hidden, packed, weight, qkv_w, dense_w, context, act, total, made, own, right, vecs, vec_out, vec_in, small,
    small_in, load_l, act_l, part_l, tile_s, tile_r, tile_l, left_l, right_l, in_s, in_r, mid_s, mid_r, end_s, end_r, own_l, keep_l, turn_s, turn_r,
    cross_s, cross_r, home_s, home_r, back_s, back_r, local, vec_s, vec_r, small_s, small_r):
    f, s = (lax.axis_index('fsdp'), lax.axis_index('sp'))
    core = f % 2
    f_x, f_y, f_c, f_d = neighbours(f)
    is_end = (s == 0) | (s == 3)
    is_mid = (s == 1) | (s == 2)
    inner, outer, facing = (1 + s // 3, 3 * (s // 2), 3 - s)
    unit = made.shape[3]
    size = 8 * unit
    low = made.dtype
    meet(f, s)
    sent = []

    def send(src, dst, send_sem, recv_sem, device):
        copy = remote(src, dst, send_sem, recv_sem, device)
        copy.start()
        return copy

    def arrived(ref, recv_sem):
        remote(ref, ref, vec_s.at[0], recv_sem, (f_c, s)).wait_recv()
    chunks = []
    at = 0
    groups = {}
    for name, ref, first, result in (('down', down_ref, 0, g_down), ('up', part, 0, g_up), ('qkv', part, g_up.shape[0], g_qkv), ('dense', turned, 0,
        g_dense)):
        for g in range(result.shape[0]):
            cuts = (4,)
            if not chunks:
                cuts = (1, 1, 2)
            if name == 'dense':
                cuts = (2, 1, 1)
            start = 0
            for pairs_of in cuts:
                chunks.append((ref, first + g, result, g, start, pairs_of, at))
                groups[len(chunks) - 1] = (name, first + g)
                start += pairs_of
            at += 1
    count = len(chunks)
    ahead = 4

    def cut(ref, g, k):
        _, _, _, _, start, pairs_of, _ = chunks[k]
        return ref.at[g, pl.ds(start, pairs_of)]

    def source(k):
        return cut(chunks[k][0], chunks[k][1], k)

    def goal(k):
        return cut(chunks[k][2], chunks[k][3], k)

    def from_end(k):
        return remote(source(k), cut(line_a, chunks[k][6], k), in_s.at[k], in_r.at[k], (f, inner))

    def across(k):
        return remote(cut(line_a, chunks[k][6], k), cut(line_b, chunks[k][6], k), mid_s.at[k], mid_r.at[k], (f, facing))

    def to_end(k):
        return remote(cut(line_b, chunks[k][6], k), goal(k), end_s.at[k], end_r.at[k], (f, outer))

    def load_own(k):
        return pltpu.make_async_copy(source(k), cut(own, k % 2, k), own_l.at[k % 2])

    def keep(k):
        return pltpu.make_async_copy(cut(line_b, chunks[k][6], k), goal(k), keep_l.at[k])

    def add_units(target, others, number):
        @pl.loop(0, number)
        def _(i):
            for half in range(2):
                rows = pl.ds(half * (unit // 2), unit // 2)
                value = target[i // 2, i % 2, rows, :].astype(jnp.float32)
                for other in others:
                    value = value + other[i // 2, i % 2, rows, :].astype(jnp.float32)
                target[i // 2, i % 2, rows, :] = value.astype(low)

    def mid_in(k):
        load_own(k).wait()
        from_end(k).wait_recv()
        add_units(cut(line_a, chunks[k][6], k), [cut(own, k % 2, k)], 2 * chunks[k][5])
        across(k).start()
        if k + 2 < count:
            load_own(k + 2).start()

    def mid_out(k):
        across(k).wait_recv()
        add_units(cut(line_b, chunks[k][6], k), [cut(line_a, chunks[k][6], k)], 2 * chunks[k][5])
        to_end(k).start()
        keep(k).start()
    coming = {'big': copied(normed_mlp_ref, big, load_l.at[0]), 'hidden': copied(hidden_ref, hidden, load_l.at[1]), 'weight': copied(up_w_ref,
        weight, load_l.at[2]), 'packed': copied(packed_ref, packed, load_l.at[3]), 'qkv': copied(qkv_w_ref, qkv_w, load_l.at[4]),
        'dense': copied(dense_w_ref, dense_w, load_l.at[5]), 'context': copied(context_ref, context, load_l.at[6])}

    def ready(*names):
        for name in names:
            if coming[name] is not None:
                coming[name].wait()
                coming[name] = None
    span = dense_ref.shape[4]
    columns = pl.ds(pl.multiple_of(f * span, span), span)
    turn_own = copied(dense_ref.at[f], turned.at[0, :, :, :, columns], local.at[0])
    bias_own = copied(bias_ref, small.at[pl.ds(8, 8)], local.at[1])
    vecs[...] = jnp.zeros_like(vecs)
    vec_out[...] = jnp.zeros_like(vec_out)
    busy = {0: [], 1: []}
    turns = [0]

    def next_made():
        slot = turns[0] % 2
        turns[0] += 1
        for wait in busy[slot]:
            wait()
        busy[slot] = []
        return slot
    stores = {}

    def finish_group(g, weights, first, column_ref, which):
        slot = next_made()

        @pl.loop(0, 8)
        def _(i):
            rows = pl.ds(pl.multiple_of(i * unit, unit), unit)
            wide = pl.ds(pl.multiple_of(first + i * unit, unit), unit)
            value = total[rows, :]
            made[slot, i // 2, i % 2] = value.astype(low)
            line = weights[wide, :].astype(jnp.float32)
            sums = column_ref[wide, 0:1]
            scaled = line * (value - sums * norm_ref[2 * which + 1:2 * which + 2, :])
            vecs[2 * which] += eight_rows(scaled)
            vecs[2 * which + 1] += eight_rows(line * sums)
        stores[g] = copied(made.at[slot], part.at[g], part_l.at[g])
        busy[slot] = [functools.partial(stored, g)]

    def stored(g):
        if stores[g] is not None:
            stores[g].wait()
            stores[g] = None

    def up_group(g):
        ready('big', 'hidden', 'weight')
        total[...] = contract_rows(hidden[:, g * size:(g + 1) * size], big[...])
        finish_group(g, weight, g * size, h_col_ref, 1)
        if g == g_up.shape[0] - 1:
            coming['big'] = copied(normed_ref, big, load_l.at[7])
            coming['weight'] = copied(down_w_ref, weight, load_l.at[8])
            load_act(0)

    def qkv_group(g):
        ready('big', 'packed', 'qkv')
        total[...] = contract_rows(packed[:, g * size:(g + 1) * size], big[...])
        finish_group(g_up.shape[0] + g, qkv_w, g * size, p_col_ref, 0)

    def load_act(t):
        coming['act', t] = copied(act_ref.at[pl.ds(t * size, size)], act.at[t % 2], act_l.at[t % 2])

    def give_tile(a, t, value):
        b, z = (t // 4, t % 4)
        slot = next_made()
        made[slot] = value.astype(low).reshape(4, 2, unit, value.shape[1])
        give = send(made.at[slot, :, 1 - core], paired.at[a, :, z, b], tile_s.at[a, t], tile_r.at[a, t], (f_c, s))
        hold = copied(made.at[slot, :, core], kept.at[a, :, z, b], tile_l.at[a, t])
        busy[slot] = [give.wait_send, hold.wait]

    def out_tile(t):
        ready('weight', 'context', 'dense', ('act', t))
        if t < 7:
            load_act(t + 1)
        rows = slice(t * size, (t + 1) * size)
        value = times_transposed(context[rows, :], dense_w[...]) + times(act[t % 2], weight[...])
        give_tile(0, t, value)
        if t == 7:
            coming['weight'] = copied(up_w_ref, weight, load_l.at[9])

    def back_tile(t):
        ready('weight', 'packed', 'qkv', 'hidden')
        rows = slice(t * size, (t + 1) * size)
        value = times(packed[rows, :], qkv_w[...]) * norm_ref[0:1, :]
        value = value + times(hidden[rows, :], weight[...]) * norm_ref[2:3, :]
        give_tile(1, t, value)
    results = (o_out, o_back)
    order = (f_d // 2, f_x // 2, f_y // 2, f // 2)
    def free(slot):
        for wait in busy[slot]:
            wait()
        busy[slot] = []

    def tiles_here(a):
        for slot in range(2):
            free(slot)
        for t in range(8):
            arrived(paired.at[a, :, t % 4, t // 4], tile_r.at[a, t])

    def add_pair(a, n):
        if n == 0:
            tiles_here(a)
        slot = next_made()
        first = copied(paired.at[a, order[n]], made.at[slot], left_l.at[slot])
        second = copied(kept.at[a, order[n]], right.at[slot], right_l.at[slot])
        first.wait()
        second.wait()
        add_units(made.at[slot], [right.at[slot]], 8)
        give = send(made.at[slot], crossed.at[a, n], cross_s.at[a, n], cross_r.at[a, n], ((f_d, f_x, f_y)[n], s))
        busy[slot] = [give.wait_send]

    def add_chips(a):
        one, two = next_made(), next_made()
        first = copied(paired.at[a, order[3]], made.at[one], left_l.at[one])
        second = copied(kept.at[a, order[3]], right.at[0], right_l.at[0])
        arrived(crossed.at[a, 0], cross_r.at[a, 0])
        third = copied(crossed.at[a, 0], made.at[two], left_l.at[two])
        arrived(crossed.at[a, 1], cross_r.at[a, 1])
        fourth = copied(crossed.at[a, 1], right.at[1], right_l.at[1])
        first.wait()
        second.wait()
        add_units(made.at[one], [right.at[0]], 8)
        arrived(crossed.at[a, 2], cross_r.at[a, 2])
        fifth = copied(crossed.at[a, 2], right.at[0], right_l.at[0])
        third.wait()
        fourth.wait()
        fifth.wait()
        add_units(made.at[one], [made.at[two], right.at[1], right.at[0]], 8)
        for k in range(1, 4):
            z = (s + k) % 4
            give = send(made.at[one, z], homed.at[a, s], home_s.at[a, k], home_r.at[a, k], (f, z))
            busy[one].append(give.wait_send)
        hold = copied(made.at[one, s], homed.at[a, s], local.at[2 + a])
        busy[one].append(hold.wait)
        home_slot[a] = one
    homes, home_slot = {}, {}

    def go_home(a):
        free(home_slot[a])
        for k in range(1, 4):
            arrived(homed.at[a, (s + 4 - k) % 4], home_r.at[a, k])
        for k in range(1, 8):
            j = (f + k) % 8
            sent.append(send(homed.at[a, j // 2, j % 2], results[a].at[f], back_s.at[a, k], back_r.at[a, k], (j, s)))
        homes[a] = copied(homed.at[a, f // 2, core], results[a].at[f], local.at[4 + a])

    def give_vectors():
        for which in range(2):
            gain = norm_ref[2 * which:2 * which + 1, :]
            scaled = jnp.sum(vecs[2 * which], axis=0, keepdims=True) / gain
            plain = jnp.sum(vecs[2 * which + 1], axis=0, keepdims=True)
            for j in range(8):
                part_of = slice(j * span, (j + 1) * span)
                vec_out[j, 2 * which:2 * which + 1, :] = scaled[:, part_of]
                vec_out[j, 2 * which + 1:2 * which + 2, :] = plain[:, part_of]
        for k in range(1, 8):
            j = (f + k) % 8
            sent.append(send(vec_out.at[j], vec_in.at[f], vec_s.at[k], vec_r.at[k], (j, s)))
        homes['vec'] = copied(vec_out.at[f], vec_in.at[f], local.at[6])

    def add_vectors():
        homes['vec'].wait()
        bias_own.wait()
        for k in range(1, 8):
            arrived(vec_in.at[(f + 8 - k) % 8], vec_r.at[k])
        value = vec_in[0]
        for j in range(1, 8):
            value = value + vec_in[j]
        small[0:8, :] = value
        for k in range(1, 4):
            sent.append(send(small, small_in.at[s], small_s.at[k], small_r.at[k], (f, (s + k) % 4)))
        homes['small'] = copied(small, small_in.at[s], local.at[7])

    def add_small():
        homes['small'].wait()
        for k in range(1, 4):
            arrived(small_in.at[(s + 4 - k) % 4], small_r.at[k])
        value = small_in[0]
        for z in range(1, 4):
            value = value + small_in[z]
        o_small[...] = value

    def turn_start():
        for k in range(1, 8):
            j = (f + k) % 8
            sent.append(send(dense_ref.at[j], turned.at[0, :, :, :, columns], turn_s.at[k], turn_r.at[k], (j, s)))

    def turn_done():
        turn_own.wait()
        for k in range(1, 8):
            j = (f + 8 - k) % 8
            there = pl.ds(pl.multiple_of(j * span, span), span)
            arrived(turned.at[0, :, :, :, there], turn_r.at[k])

    def task(name, i):
        if name == 'turn':
            turn_start()
        elif name == 'turned':
            turn_done()
        elif name == 'up':
            up_group(i)
        elif name == 'qkv':
            qkv_group(i)
        elif name == 'out':
            out_tile(i)
        elif name == 'back':
            back_tile(i)
        elif name == 'pair':
            add_pair(i // 3, i % 3)
        elif name == 'chips':
            add_chips(i)
        elif name == 'home':
            go_home(i)
        elif name == 'vectors':
            give_vectors()
        elif name == 'sums':
            add_vectors()
        else:
            add_small()

    @pl.when(is_end)
    def _():
        for k in range(ahead):
            from_end(k).start()

    @pl.when(is_mid)
    def _():
        for k in range(2):
            load_own(k).start()
    for k in range(count + 2):
        for name, first, last in FINISH_STEPS[k] if k in FINISH_STEPS else ():
            for i in range(first, last):
                task(name, i)
        if k + ahead - 1 in groups and groups[k + ahead - 1][0] in ('up', 'qkv'):
            stored(groups[k + ahead - 1][1])

        @pl.when(is_mid)
        def _():
            if k < count:
                mid_in(k)
            if 1 <= k <= count:
                mid_out(k - 1)

        @pl.when(is_end)
        def _():
            if 1 <= k <= count:
                to_end(k - 1).wait_recv()
                if k - 1 + ahead < count:
                    from_end(k - 1 + ahead).start()
    for a in range(2):
        homes[a].wait()
        for k in range(1, 8):
            arrived(results[a].at[(f + 8 - k) % 8], back_r.at[a, k])
    for slot in range(2):
        free(slot)
    for copy in sent:
        copy.wait_send()

    @pl.when(is_end)
    def _():
        for k in range(count):
            from_end(k).wait_send()

    @pl.when(is_mid)
    def _():
        for k in range(count):
            across(k).wait_send()
            to_end(k).wait_send()
            keep(k).wait()


FINISH_STEPS = {
    0: (("turn", 0, 1), ("up", 0, 2)),
    1: (("up", 2, 3),),
    2: (("up", 3, 4),),
    3: (("qkv", 0, 3), ("out", 0, 2)),
    4: (("out", 2, 8),),
    5: (("back", 0, 4), ("pair", 0, 3)),
    6: (("back", 4, 8), ("vectors", 0, 1)),
    7: (("pair", 3, 6), ("turned", 0, 1)),
    8: (("chips", 0, 1), ("sums", 0, 1)),
    9: (("home", 0, 1),),
    10: (("chips", 1, 2), ("small", 0, 1)),
    12: (("home", 1, 2),),
}


def finish(down, dense, hidden_grad, normed_mlp, packed_grad, normed, act, context, w_up, w_down, w_qkv, dense_in, norms, h_sums, p_sums, bias):
    width = down.shape[1]
    tokens = hidden_grad.shape[0]
    low = down.dtype
    unit = tokens // 64
    size = 8 * unit
    span = width // 8

    def grouped(rows):
        return (rows // size, 4, 2, unit, width)

    def columns(sums):
        return jnp.broadcast_to(sums[:, None], (sums.shape[0], 128))
    sets = [w.shape[0] // size for w in (down, w_up, w_qkv)]
    number = sum(sets) + 1
    count = sum(sets) + 5
    sums = [jax.ShapeDtypeStruct(grouped(n * size), low) for n in (*sets, 1)]
    token = jax.ShapeDtypeStruct((8, unit, width), low)
    halves = jax.ShapeDtypeStruct((2, 4, 4, 2, unit, width), low)
    others = [jax.ShapeDtypeStruct(grouped((sets[1] + sets[2]) * size), low), halves, halves, jax.ShapeDtypeStruct((2, 3, 4, 2, unit, width), low),
        jax.ShapeDtypeStruct((2, 4, 2, unit, width), low)]
    dma = pltpu.SemaphoreType.DMA
    vmem = pltpu.VMEM
    anywhere = pl.BlockSpec(memory_space=pl.ANY)
    inside = pl.BlockSpec(memory_space=pltpu.VMEM)
    result = pl.pallas_call(finish_kernel, out_shape=(*sums, token, token, *others, jax.ShapeDtypeStruct((16, span), jnp.float32)),
        in_specs=[anywhere] * 12 + [inside] * 3 + [anywhere], out_specs=[anywhere] * 11 + [inside], scratch_shapes=[vmem((number, 4, 2, unit, width),
        low), vmem((number, 4, 2, unit, width), low), vmem((1, 4, 2, unit, width), low), vmem((tokens, width), low), vmem(hidden_grad.shape, low),
        vmem(packed_grad.shape, low), vmem(w_up.shape, low), vmem(w_qkv.shape, low), vmem(dense_in.shape, low), vmem(context.shape, low), vmem((2,
        size, act.shape[1]), low), vmem((size, width), jnp.float32), *(vmem((2, 4, 2, unit, width), low) for _ in range(3)), vmem((4, 8, width),
        jnp.float32), vmem((8, 8, span), jnp.float32), vmem((8, 8, span), jnp.float32), vmem((16, span), jnp.float32), vmem((4, 16, span),
        jnp.float32), dma((10,)), dma((2,)), dma((sets[1] + sets[2],)), dma((2, 8)), dma((2, 8)), dma((2, 8)), dma((2,)), dma((2,)), dma((count,)),
        dma((count,)), dma((count,)), dma((count,)), dma((count,)), dma((count,)), dma((2,)), dma((count,)), dma((8,)), dma((8,)), dma((2, 3)),
        dma((2, 3)), dma((2, 4)), dma((2, 4)), dma((2, 8)), dma((2, 8)), dma((8,)), dma((8,)), dma((8,)), dma((4,)), dma((4,))],
        compiler_params=pltpu.CompilerParams(collective_id=2, has_side_effects=True, vmem_limit_bytes=60 * 1024 * 1024),
        name='finish')(down.reshape(grouped(down.shape[0])), dense.reshape(8, 4, 2, unit, span), hidden_grad, normed_mlp, packed_grad, normed, act,
        context, w_up, w_down, w_qkv, dense_in, norms, columns(h_sums), columns(p_sums), bias)
    grads = [grad.reshape(-1, width) for grad in result[:4]]
    return (grads, result[4], result[5], result[11])


def own_tokens(hidden_in, cotangent, output, weighted, shift):
    inputs = hidden_in.astype(jnp.float32)
    output = (inputs + (output.astype(jnp.float32) + shift)).astype(jnp.bfloat16)
    scaled, inverse = norm_scaled(inputs)
    weighted = weighted.astype(jnp.float32)
    first_mean = jnp.mean(weighted, axis=-1, keepdims=True)
    second_mean = jnp.mean(weighted * scaled, axis=-1, keepdims=True)
    input_grad = (cotangent.astype(jnp.float32) + inverse * (weighted - first_mean - scaled * second_mean)).astype(jnp.bfloat16)
    return (output, input_grad)


def by_collectives(hidden_in, segments, ln1_gain, ln1_bias, ln2_gain, ln2_bias, w_qkv, b_qkv, w_dense, b_dense, w_up, b_up, w_down, b_down,
    cotangent):
    seq_local, shard_len, width = hidden_in.shape
    seq_len = segments.shape[1]
    nf, ns = (lax.axis_size('fsdp'), lax.axis_size('sp'))
    f_place, s_place = (lax.axis_index('fsdp'), lax.axis_index('sp'))
    seqs = seq_local * nf
    group = seqs // ns
    piece = shard_len // nf
    tokens = group * seq_len
    per_head = max(1, nf // HEADS)
    head_count = max(1, HEADS // nf)
    head_sets = [[head * per_head + k for k in range(per_head)] for head in range(nf // per_head)]

    def gather_tokens(block):
        part = lax.all_to_all(block, 'fsdp', split_axis=1, concat_axis=0, tiled=True)
        part = lax.all_to_all(part, 'sp', split_axis=0, concat_axis=1, tiled=True)
        return in_order(lax.all_gather(part, 'fsdp', axis=0, tiled=True)).reshape(tokens, width)

    def scatter_tokens(partial):
        part = out_of_order(partial).reshape(nf * group, ns * piece, width)
        part = lax.psum_scatter(part, 'fsdp', scatter_dimension=0, tiled=True)
        part = lax.all_to_all(part, 'sp', split_axis=1, concat_axis=0, tiled=True)
        return lax.all_to_all(part, 'fsdp', split_axis=0, concat_axis=1, tiled=True)

    def in_order(array):
        array = array.reshape(nf, group, ns, piece, -1)
        return array.transpose(1, 2, 0, 3, 4).reshape(group, seq_len, -1)

    def out_of_order(array):
        array = array.reshape(group, ns, nf, piece, -1)
        return array.transpose(2, 0, 1, 3, 4).reshape(tokens, -1)

    def over_head(array, axis):
        if per_head == 1:
            return array
        return lax.all_gather(array, 'fsdp', axis=axis, tiled=True, axis_index_groups=head_sets)

    def own_columns(array):
        if per_head == 1:
            return array
        share = array.shape[-1] // per_head
        return lax.dynamic_slice_in_dim(array, f_place % per_head * share, share, array.ndim - 1)

    def own_part(vector):
        share = vector.shape[0] // nf
        return lax.dynamic_slice_in_dim(vector, f_place * share, share, 0)
    gathered, upstream = (gather_tokens(hidden_in), gather_tokens(cotangent))
    rows = lax.all_gather(segments, 'fsdp', axis=0, tiled=True)
    rows = lax.dynamic_slice_in_dim(rows, s_place * group, group, 0)
    dense_in = lax.all_to_all(w_dense, 'fsdp', split_axis=1, concat_axis=0, tiled=True)
    head_qkv = over_head(w_qkv, 0)
    head_dense = over_head(dense_in, 1)
    head_bias = lax.dynamic_slice_in_dim(b_qkv, f_place // per_head * head_qkv.shape[0], head_qkv.shape[0], 0)
    scaled, _ = norm_scaled(gathered.astype(jnp.float32))
    normed = (scaled * ln1_gain + ln1_bias).astype(jnp.bfloat16)
    normed_mlp = (scaled * ln2_gain + ln2_bias).astype(jnp.bfloat16)
    hidden = times_transposed(normed_mlp, w_up) + own_part(b_up)
    activated, slope = gelu_pair(hidden)
    activated = activated.astype(jnp.bfloat16)
    down_term = contract_rows(activated, upstream).astype(jnp.bfloat16)
    grad_down_w = lax.psum(down_term, 'sp').astype(jnp.float32)
    hidden_grad = (times_transposed(upstream, w_down) * slope).astype(jnp.bfloat16)
    up_term = contract_rows(hidden_grad, normed_mlp)
    mlp_norm_grad = times(hidden_grad, w_up)
    packed = (times_transposed(normed, head_qkv) + head_bias).astype(jnp.bfloat16)
    packed = packed.reshape(group, seq_len, head_count, 3 * HEAD_DIM)
    cos_table, sin_table = rotary_tables(rows)
    queries = rotate(packed[..., :HEAD_DIM].astype(jnp.float32), cos_table, sin_table).astype(jnp.bfloat16)
    keys_rot = rotate(packed[..., HEAD_DIM:2 * HEAD_DIM].astype(jnp.float32), cos_table, sin_table).astype(jnp.bfloat16)
    values = packed[..., 2 * HEAD_DIM:]
    mask = build_mask(rows)
    context, log_total = attend_forward(queries, keys_rot, values, mask)
    context = own_columns(context.reshape(tokens, -1))
    partial_out = times_transposed(context, dense_in) + times(activated, w_down)
    context_grad = times(upstream, head_dense).astype(jnp.bfloat16).reshape(group, seq_len, head_count, HEAD_DIM)
    query_grad, key_grad, value_grad = attend_backward(queries, keys_rot, values, mask, log_total, context_grad)
    packed_grad = jnp.concatenate([unrotate(query_grad, cos_table, sin_table), unrotate(key_grad, cos_table, sin_table), value_grad],
        axis=-1).astype(jnp.bfloat16)
    packed_grad = own_columns(packed_grad.reshape(tokens, -1))
    attn_norm_grad = times(packed_grad, w_qkv)
    qkv_term = contract_rows(packed_grad, normed)
    dense_term = contract_rows(upstream, context).astype(jnp.bfloat16)
    partial_back = attn_norm_grad * ln1_gain + mlp_norm_grad * ln2_gain
    vectors = jnp.stack([jnp.sum(attn_norm_grad * scaled, axis=0), jnp.sum(attn_norm_grad, axis=0), jnp.sum(mlp_norm_grad * scaled, axis=0),
        jnp.sum(mlp_norm_grad, axis=0)])
    bias_out = own_part(jnp.sum(upstream.astype(jnp.float32), axis=0))
    bias_qkv = jnp.sum(packed_grad.astype(jnp.float32), axis=0)
    bias_up = jnp.sum(hidden_grad.astype(jnp.float32), axis=0)
    vectors = lax.psum_scatter(vectors, 'fsdp', scatter_dimension=1, tiled=True)
    vectors, bias_out, bias_qkv, bias_up = lax.psum((vectors, bias_out, bias_qkv, bias_up), 'sp')
    output = scatter_tokens(rounded(partial_out))
    weighted = scatter_tokens(rounded(partial_back))
    dense_term = lax.all_to_all(dense_term, 'fsdp', split_axis=0, concat_axis=1, tiled=True)
    grad_up_w, grad_qkv_w, grad_dense_w = (lax.psum(term.astype(jnp.bfloat16), 'sp').astype(jnp.float32) for term in (up_term, qkv_term, dense_term))
    output, input_grad = own_tokens(hidden_in, cotangent, output, weighted, b_dense + b_down)
    return (output, input_grad, vectors[0], vectors[1], vectors[2], vectors[3], grad_qkv_w, bias_qkv, grad_dense_w, bias_out, grad_up_w, bias_up,
        grad_down_w, bias_out)


def by_kernels(hidden_in, segments, ln1_gain, ln1_bias, ln2_gain, ln2_bias, w_qkv, b_qkv, w_dense, b_dense, w_up, b_up, w_down, b_down, cotangent):
    width = hidden_in.shape[2]
    seq_len = segments.shape[1]
    nf, ns = (lax.axis_size('fsdp'), lax.axis_size('sp'))
    group = nf // ns
    tokens = group * seq_len
    share = width // nf
    f_place = lax.axis_index('fsdp')

    def own_part(vector):
        size = vector.shape[0] // nf
        return lax.dynamic_slice_in_dim(vector, f_place * size, size, 0)
    norms = jnp.stack([ln1_gain, ln1_bias, ln2_gain, ln2_bias])
    _, upstream, rows, normed, normed_mlp, packed, activated, slope = gather_both(hidden_in[0], cotangent[0], segments.reshape(8, seq_len // 8),
        w_up, w_qkv, own_part(b_up), own_part(b_qkv), norms)
    upstream = upstream.reshape(tokens, width)
    w_dense, upstream = lax.optimization_barrier((w_dense, upstream))
    dense_in = lax.all_to_all(w_dense, 'fsdp', split_axis=1, concat_axis=0, tiled=True)
    early = activated.shape[1] // 2
    down_term = contract_rows(activated[:, :early], upstream).astype(jnp.bfloat16)
    early_down_w = lax.psum(down_term, 'sp').astype(jnp.float32)
    slope, activated, down_term = lax.optimization_barrier((slope, activated, down_term))
    hidden_grad, context_grad, c_sums, h_sums = upstream_parts(upstream, slope, w_down, dense_in)
    context, packed_grad, p_sums = attend(packed, context_grad, head_tables(rows.reshape(group, seq_len)), seq_len)
    late_down_term = contract_rows(activated[:, early:], upstream).astype(jnp.bfloat16)
    dense_term = contract_rows(upstream, context).astype(jnp.bfloat16)
    bias_up, bias_qkv = (jnp.sum(h_sums, axis=0), jnp.sum(p_sums, axis=0))
    bias_out = own_part(jnp.sum(c_sums, axis=0))
    grads, output, weighted, sums = finish(late_down_term, dense_term, hidden_grad, normed_mlp, packed_grad, normed, activated, context, w_up,
        w_down, w_qkv, dense_in, norms, bias_up, bias_qkv, jnp.concatenate([bias_out, bias_qkv, bias_up]).reshape(8, share))
    late_down_w, grad_up_w, grad_qkv_w, grad_dense_w = (grad.astype(jnp.float32) for grad in grads)
    grad_down_w = jnp.concatenate([early_down_w, late_down_w])
    bias_out = sums[8]
    output, input_grad = own_tokens(hidden_in, cotangent, output.reshape(hidden_in.shape), weighted.reshape(hidden_in.shape), b_dense + b_down)
    return (output, input_grad, sums[0], sums[1], sums[2], sums[3], grad_qkv_w, sums[9:12].reshape(-1), grad_dense_w, bias_out, grad_up_w,
        sums[12:16].reshape(-1), grad_down_w, bias_out)


def per_device(hidden_in, *rest):
    sizes = (lax.axis_size('fsdp'), lax.axis_size('sp'), hidden_in.shape[0])
    shapes = (hidden_in.shape[1] % 256, hidden_in.shape[2] % (8 * HEAD_DIM), rest[9].shape[0] % 256)
    if sizes == (8, 4, 1) and HEADS == 8 and (not any(shapes)):
        return by_kernels(hidden_in, *rest)
    return by_collectives(hidden_in, *rest)


def solution(mesh):
    rows = P('fsdp', 'sp', None)
    first = P('fsdp', None)
    return jax.shard_map(per_device, mesh=mesh, in_specs=(rows, first, P(), P(), P(), P(), first, P(), first, P(), first, P(), first, P(), rows),
        out_specs=(rows, rows, P('fsdp'), P('fsdp'), P('fsdp'), P('fsdp'), first, P('fsdp'), first, P('fsdp'), first, P('fsdp'), first, P('fsdp')),
        check_vma=False)
```

time: 1000 us -> 634 us (0.63)
  Pallas kernels: 107 us -> 539 us
  waiting for transfers between devices: 291 us -> 0.02 us
  matrix products: 169 us -> 27.1 us
  starting transfers between devices: 118 us -> 3.77 us
  other arithmetic: 133 us -> 27.9 us
  blocking collectives: 100 us -> 0 us
  local copies, waits for them, and re-layouts: 58.4 us -> 13 us
    pallas_call x1 -> x4, Pallas kernels: 107 us -> 539 us  [the longest x1 383 us: finish(): pl.pallas_call(finish_kernel, out_shape=(*sums, token, token, *others, ja...]
    ppermute x12 -> x0, waiting for transfers between devices: 157 us -> none  [the longest x4 157 us: sum_over_line(): inward = lax.ppermute(partial, 'sp', [(0, 1), (3, 2)])]
    dot_general x14 -> x0, matrix products: 126 us -> none  [the longest x4 51.9 us: times(): return jnp.dot(former, latter, preferred_element_type=jnp.float32)]
    all_to_all x6 -> x1, waiting for transfers between devices: 97.4 us -> 0.01 us  [by_kernels(): lax.all_to_all(w_dense, 'fsdp', split_axis=1, concat_axis=0, tiled=True)]
    psum x1 -> x0, blocking collectives: 91.1 us -> none  [per_device(): lax.psum((vectors, bias_out, bias_qkv, bias_up), 'sp')]
    all_to_all x6 -> x1, starting transfers between devices: 84.5 us -> 3.56 us  [by_kernels(): lax.all_to_all(w_dense, 'fsdp', split_axis=1, concat_axis=0, tiled=True)]
    convert_element_type x18 -> x7, other arithmetic: 86.5 us -> 16 us  [the longest x3 10.1 us: by_kernels(): grad.astype(jnp.float32)]
    unnamed x4 -> x1, waiting for transfers between devices: 36.7 us -> 0.02 us
  transfers between devices with their start and end apart: 21 -> 2, of which waited for: 8 -> 0; matrix products, arithmetic and copies ran while one was open for 27% -> 9% of each run, Pallas kernels for 11% -> 66%
where the time goes in v6:
time: 634 us; the launch traced here: 626 us
  Pallas kernels  539 us (85%)
  other arithmetic  27.9 us (4%)
  matrix products  27.1 us (4%)
  between operations  14.8 us (2%)
  local copies, waits for them, and re-layouts  13 us (2%)
    pallas_call x1, Pallas kernels, finish(): pl.pallas_call(finish_kernel, out_shape=(*sums, token, token, *others, ja...  383 us
    pallas_call x1, Pallas kernels, gather_both(): pl.pallas_call(gather_kernel, out_shape=(shape, shape, jax.ShapeDtypeStru...  125 us
    dot_general x3, matrix products, contract_rows(): lax.dot_general(former, latter, (((0,), (0,)), ((), ())), preferred_eleme...  27.1 us
    pallas_call x1, Pallas kernels, upstream_parts(): pl.pallas_call(upstream_kernel, grid=(tokens // rows,), out_shape=(jax.Sh...  17.8 us
    pallas_call x1, Pallas kernels, attend(): pl.pallas_call(attention_kernel, grid=(tokens // length,), out_shape=(jax...  13.2 us
  transfers between devices with their start and end apart: 2, of which 0 were waited for; matrix products, arithmetic and copies ran while one was open for 9% of the time, Pallas kernels for 66%

profile of v6, /device:TPU:0, one launch (start us, length us, event | category | flops | bytes accessed | tf_op | source)
XLA Modules:
  0.0 625.5 jit_solution(16452580949683336165)
XLA Ops:
  7.2 0.8 dynamic_slice.10
  8.0 0.7 dynamic_slice.9
  8.7 0.8 pad_maximum_fusion.1.norm_ref
  9.5 1.2 copy-done
  10.7 1.2 copy-done.3
  11.9 0.7 copy-done.7
  12.6 124.7 %gather_tokens.1 = (bf16[2,4,8,32,2048]{4,3,2,1,0:T(8,128)(2,1)}, bf16[2,4,8,32,2048]{4,3,2,1,0:T(8,128)(2,1)}, s32[2,8,128]{2,1,0:T(8,128)S(1)}, bf16[2048,2048...) custom-call(bf16[256,2048]{1,0:T(8,128)(2,1)S(1)} %bitcast.67, ...), custom_call_target="tpu_custom_call" | custom-call | tf_op jit(solution)/shard_map/gather_tokens/pallas_call | solution.py:444
  137.3 1.7 copy-done.8
  139.0 1.0 copy.41
  140.0 3.6 all-to-all-start
  143.8 9.9 %convolution_convert_fusion.1 = bf16[512,2048]{1,0:T(8,128)(2,1)} fusion(bf16[2048,2048]{1,0:T(8,128)(2,1)} %bitcast.95, bf16[2048,1024]{1,0:T(8,128)(2,1)} %get-tuple-element.43.act_ref), kind=kOutput, calls=%fused_computation.7 | convolution fusion | flops 4296015872 | bytes 12582912 | tf_op jit(solution)/shard_map/dot_general | solution.py:30
  153.9 0.6 reduce-window.6
  155.7 1.8 multiply_cosine_fusion
  157.5 1.0 pad_maximum_fusion.table_ref
  158.6 10.3 %convolution_convert_fusion = bf16[512,2048]{1,0:T(8,128)(2,1)} fusion(bf16[2048,2048]{1,0:T(8,128)(2,1)} %bitcast.96, bf16[2048,1024]{1,0:T(8,128)(2,1)} %get-tuple-element.43.act_ref), kind=kOutput, calls=%fused_computation.6 | convolution fusion | flops 4296015872 | bytes 12582912 | tf_op jit(solution)/shard_map/dot_general | solution.py:30
  168.9 17.8 %upstream_parts.1 = (bf16[2048,1024]{1,0:T(8,128)(2,1)}, bf16[2048,256]{1,0:T(8,128)(2,1)S(1)}, f32[8,2048]{1,0:T(8,128)S(1)}, f32[8,1024]{1,0:T(8,128)S(1)}) custom-call(bf16[2048,2048]{1,0:T(8,128)(2,1)} %bitcast.97, f32[2048,1024]{1,0:T(8,128)} %get-tuple-element.45.slope_ref, bf16[1024,2048]{1,0:T(8,128)(2,1)} %down_w_ref.1, bf16[2048,256]{1,0:T(8,128)(2,1)S(1)} %bitcast.68), custom_call_target="tpu_custom_call" | custom-call | flops 10737418240 | bytes 27262976 | tf_op jit(solution)/shard_map/upstream_parts/pallas_call | solution.py:155
  186.6 13.2 %attend.1 = (bf16[2048,256]{1,0:T(8,128)(2,1)S(1)}, bf16[2048,768]{1,0:T(8,128)(2,1)}, f32[8,768]{1,0:T(8,128)S(1)}) custom-call(bf16[2048,768]{1,0:T(8,128)(2,1)} %copy-done.8, bf16[2048,256]{1,0:T(8,128)(2,1)S(1)} %get-tuple-element.47.grad_ref, f32[2,128,1024]{2,1,0:T(8,128)S(1)} %pad_maximum_fusion.table_ref), custom_call_target="tpu_custom_call" | custom-call | flops 4697620480 | bytes 9437184 | tf_op jit(solution)/shard_map/attend/pallas_call | solution.py:236
  200.0 0.7 reshape.254.bias_ref
  200.7 6.9 %convolution_convert_fusion.2 = bf16[2048,256]{1,0:T(8,128)(2,1)} fusion(bf16[2048,2048]{1,0:T(8,128)(2,1)} %bitcast.98, bf16[2048,256]{1,0:T(8,128)(2,1)S(1)} %get-tuple-element.49.context_ref), kind=kOutput, calls=%fused_computation.8 | convolution fusion | flops 2148007936 | bytes 10485760 | tf_op jit(solution)/shard_map/dot_general | solution.py:30
  207.6 0.9 broadcast_in_dim.8.p_col_ref
  208.5 1.0 broadcast_in_dim.7.h_col_ref
  209.5 383.3 %finish.1 = (bf16[2,4,2,32,2048]{4,3,2,1,0:T(8,128)(2,1)}, bf16[4,4,2,32,2048]{4,3,2,1,0:T(8,128)(2,1)}, bf16[3,4,2,32,2048]{4,3,2,1,0:T(8,128)(2,1)}, bf16[1,4,...) custom-call(bf16[2,4,2,32,2048]{4,3,2,1,0:T(8,128)(2,1)} %bitcast.76, ...), custom_call_target="tpu_custom_call" | custom-call | tf_op jit(solution)/shard_map/finish/pallas_call | solution.py:861
  592.9 1.6 convert_element_type.124
  594.8 0.8 fusion.15
  595.6 1.6 bitcast_convert_fusion.2
  597.8 0.6 copy.35
  598.4 0.6 reshape.255
  599.0 4.2 fusion.8
  603.2 3.8 bitcast_convert_fusion.1
  607.0 4.7 bitcast_convert_fusion
  611.7 5.9 maximum_convert_fusion
  617.6 0.6 copy.46
  (71 shorter events, 2.6 us)
Async XLA Ops:
  9.4 127.9 %copy-start.6 = (f32[4,2048]{1,0:T(4,128)}, f32[4,2048]{1,0:T(4,128)S(1)}, u32[]{:S(2)}) copy-start(f32[4,2048]{1,0:T(4,128)S(1)} %pad_maximum_fusion.1.norm_ref) | copy-start | bytes 98308
  9.4 1.2 copy-start
  10.7 1.2 copy-start.3
  11.9 0.7 copy-start.7
  12.6 126.4 %copy-start.15 = (bf16[256,2048]{1,0:T(8,128)(2,1)S(1)}, bf16[256,2048]{1,0:T(8,128)(2,1)}, u32[]{:S(2)}) copy-start(bf16[256,2048]{1,0:T(8,128)(2,1)} %param.23) | copy-start | bytes 3145732
  137.3 1.7 copy-start.8
  140.0 28.8 %all-to-all-start = ((bf16[256,8,256]{2,0,1:T(8,128)(2,1)}), bf16[256,8,256]{2,0,1:T(8,128)(2,1)S(1)}, u32[]{:S(2)}, u32[]{:S(2)}) async-start(bf16[256,8,256]{2,0,1:T(8,128)(2,1)} %bitcast.61), calls=%async_computation | async-start | bytes 2097152 | tf_op jit(solution)/shard_map/all_to_all | solution.py:1005
  143.6 468.1 %all-reduce.3.cloned.1.call-start = ((), (), s32[]{:S(2)}) async-start(), calls=%async_computation.1 | async-start | bytes 4194304 | tf_op jit(solution)/shard_map/psum | solution.py:1008
  153.7 1.3 copy-start.1
  153.7 3.8 copy-start.18
  153.7 3.8 copy-start.19
  168.9 17.8 %copy-start.2 = (bf16[256,8,256]{2,0,1:T(8,128)(2,1)}, bf16[256,8,256]{2,0,1:T(8,128)(2,1)S(1)}, u32[]{:S(2)}) copy-start(bf16[256,8,256]{2,0,1:T(8,128)(2,1)S(1)} %all-to-all-done) | copy-start | bytes 3145732
  199.8 7.8 %copy-start.5 = (bf16[2048,256]{1,0:T(8,128)(2,1)}, bf16[2048,256]{1,0:T(8,128)(2,1)S(1)}, u32[]{:S(2)}) copy-start(bf16[2048,256]{1,0:T(8,128)(2,1)S(1)} %get-tuple-element.49.context_ref) | copy-start | bytes 3145732
  592.9 1.6 copy-start.11
  592.9 1.9 copy-start.17
  592.9 2.7 copy-start.14
  594.5 2.7 copy-start.9
  595.6 22.0 %copy-start.20 = (f32[1,256]{1,0:T(1,128)}, f32[1,256]{1,0:T(1,128)S(1)}, u32[]{:S(2)}) copy-start(f32[1,256]{1,0:T(1,128)S(1)} %get-tuple-element.66) | copy-start | bytes 3076
  597.2 1.8 copy-start.4
  597.2 1.8 copy-start.16
  599.0 4.2 copy-start.12
  603.2 3.8 copy-start.10
  607.0 4.8 copy-start.13
Sparse Core Ops, SparseCore 0:
  153.9 108.4 all-reduce.2

commit v7 on v6

--- a/solution.py
+++ b/solution.py
@@ -593,7 +593,7 @@
 
     def up_group(g):
         ready('big', 'hidden', 'weight')
-        total[...] = contract_rows(hidden[:, g * size:(g + 1) * size], big[...])
+        total[...] = contract_rows(hidden[:, g * size:(g + 1) * size], big[...].reshape(hidden.shape[0], -1))
         finish_group(g, weight, g * size, h_col_ref, 1)
         if g == g_up.shape[0] - 1:
             coming['big'] = copied(normed_ref, big, load_l.at[7])
@@ -602,7 +602,7 @@
 
     def qkv_group(g):
         ready('big', 'packed', 'qkv')
-        total[...] = contract_rows(packed[:, g * size:(g + 1) * size], big[...])
+        total[...] = contract_rows(packed[:, g * size:(g + 1) * size], big[...].reshape(hidden.shape[0], -1))
         finish_group(g_up.shape[0] + g, qkv_w, g * size, p_col_ref, 0)
 
     def load_act(t):
@@ -634,6 +634,8 @@
         give_tile(1, t, value)
     results = (o_out, o_back)
     order = (f_d // 2, f_x // 2, f_y // 2, f // 2)
+    homes = {}
+
     def free(slot):
         for wait in busy[slot]:
             wait()
@@ -648,43 +650,36 @@
     def add_pair(a, n):
         if n == 0:
             tiles_here(a)
-        slot = next_made()
-        first = copied(paired.at[a, order[n]], made.at[slot], left_l.at[slot])
+        left = big.at[3 * a + n]
+        slot = n % 2
+        first = copied(paired.at[a, order[n]], left, left_l.at[slot])
         second = copied(kept.at[a, order[n]], right.at[slot], right_l.at[slot])
         first.wait()
         second.wait()
-        add_units(made.at[slot], [right.at[slot]], 8)
-        give = send(made.at[slot], crossed.at[a, n], cross_s.at[a, n], cross_r.at[a, n], ((f_d, f_x, f_y)[n], s))
-        busy[slot] = [give.wait_send]
+        add_units(left, [right.at[slot]], 8)
+        sent.append(send(left, crossed.at[a, n], cross_s.at[a, n], cross_r.at[a, n], ((f_d, f_x, f_y)[n], s)))
 
     def add_chips(a):
-        one, two = next_made(), next_made()
-        first = copied(paired.at[a, order[3]], made.at[one], left_l.at[one])
-        second = copied(kept.at[a, order[3]], right.at[0], right_l.at[0])
-        arrived(crossed.at[a, 0], cross_r.at[a, 0])
-        third = copied(crossed.at[a, 0], made.at[two], left_l.at[two])
-        arrived(crossed.at[a, 1], cross_r.at[a, 1])
-        fourth = copied(crossed.at[a, 1], right.at[1], right_l.at[1])
-        first.wait()
-        second.wait()
-        add_units(made.at[one], [right.at[0]], 8)
-        arrived(crossed.at[a, 2], cross_r.at[a, 2])
-        fifth = copied(crossed.at[a, 2], right.at[0], right_l.at[0])
-        third.wait()
-        fourth.wait()
-        fifth.wait()
-        add_units(made.at[one], [made.at[two], right.at[1], right.at[0]], 8)
+        left = big.at[6 + a]
+        copies = [copied(paired.at[a, order[3]], left, left_l.at[0]), copied(kept.at[a, order[3]], right.at[0], right_l.at[0])]
+        for n in range(3):
+            arrived(crossed.at[a, n], cross_r.at[a, n])
+            slot = (n + 1) % 2
+            more = copied(crossed.at[a, n], right.at[slot], right_l.at[slot])
+            for copy in copies:
+                copy.wait()
+            add_units(left, [right.at[1 - slot]], 8)
+            copies = [more]
+        copies[0].wait()
+        add_units(left, [right.at[1]], 8)
         for k in range(1, 4):
             z = (s + k) % 4
-            give = send(made.at[one, z], homed.at[a, s], home_s.at[a, k], home_r.at[a, k], (f, z))
-            busy[one].append(give.wait_send)
-        hold = copied(made.at[one, s], homed.at[a, s], local.at[2 + a])
-        busy[one].append(hold.wait)
-        home_slot[a] = one
-    homes, home_slot = {}, {}
+            sent.append(send(left.at[z], homed.at[a, s], home_s.at[a, k], home_r.at[a, k], (f, z)))
+        homes['own', a] = copied(left.at[s], homed.at[a, s], local.at[2 + a])
+
 
     def go_home(a):
-        free(home_slot[a])
+        homes['own', a].wait()
         for k in range(1, 4):
             arrived(homed.at[a, (s + 4 - k) % 4], home_r.at[a, k])
         for k in range(1, 8):
@@ -818,18 +813,20 @@
 
 
 FINISH_STEPS = {
-    0: (("turn", 0, 1), ("up", 0, 2)),
-    1: (("up", 2, 3),),
-    2: (("up", 3, 4),),
-    3: (("qkv", 0, 3), ("out", 0, 2)),
-    4: (("out", 2, 8),),
-    5: (("back", 0, 4), ("pair", 0, 3)),
-    6: (("back", 4, 8), ("vectors", 0, 1)),
-    7: (("pair", 3, 6), ("turned", 0, 1)),
-    8: (("chips", 0, 1), ("sums", 0, 1)),
-    9: (("home", 0, 1),),
-    10: (("chips", 1, 2), ("small", 0, 1)),
-    12: (("home", 1, 2),),
+    0: (("turn", 0, 1),),
+    1: (("up", 0, 1),),
+    2: (("up", 1, 2),),
+    3: (("up", 2, 4),),
+    4: (("qkv", 0, 3),),
+    5: (("out", 0, 6),),
+    6: (("out", 6, 8), ("back", 0, 3)),
+    7: (("pair", 0, 3), ("turned", 0, 1), ("back", 3, 5)),
+    8: (("back", 5, 8), ("vectors", 0, 1)),
+    9: (("pair", 3, 6), ("chips", 0, 1)),
+    10: (("home", 0, 1), ("sums", 0, 1)),
+    12: (("chips", 1, 2),),
+    13: (("small", 0, 1),),
+    14: (("home", 1, 2),),
 }
 
 
@@ -860,7 +857,7 @@
     inside = pl.BlockSpec(memory_space=pltpu.VMEM)
     result = pl.pallas_call(finish_kernel, out_shape=(*sums, token, token, *others, jax.ShapeDtypeStruct((16, span), jnp.float32)),
         in_specs=[anywhere] * 12 + [inside] * 3 + [anywhere], out_specs=[anywhere] * 11 + [inside], scratch_shapes=[vmem((number, 4, 2, unit, width),
-        low), vmem((number, 4, 2, unit, width), low), vmem((1, 4, 2, unit, width), low), vmem((tokens, width), low), vmem(hidden_grad.shape, low),
+        low), vmem((number, 4, 2, unit, width), low), vmem((1, 4, 2, unit, width), low), vmem(grouped(tokens), low), vmem(hidden_grad.shape, low),
         vmem(packed_grad.shape, low), vmem(w_up.shape, low), vmem(w_qkv.shape, low), vmem(dense_in.shape, low), vmem(context.shape, low), vmem((2,
         size, act.shape[1]), low), vmem((size, width), jnp.float32), *(vmem((2, 4, 2, unit, width), low) for _ in range(3)), vmem((4, 8, width),
         jnp.float32), vmem((8, 8, span), jnp.float32), vmem((8, 8, span), jnp.float32), vmem((16, span), jnp.float32), vmem((4, 16, span),
@@ -868,7 +865,7 @@
         dma((count,)), dma((count,)), dma((count,)), dma((count,)), dma((count,)), dma((2,)), dma((count,)), dma((8,)), dma((8,)), dma((2, 3)),
         dma((2, 3)), dma((2, 4)), dma((2, 4)), dma((2, 8)), dma((2, 8)), dma((8,)), dma((8,)), dma((8,)), dma((4,)), dma((4,))],
         compiler_params=pltpu.CompilerParams(collective_id=2, has_side_effects=True, vmem_limit_bytes=60 * 1024 * 1024),
-        name='finish')(down.reshape(grouped(down.shape[0])), dense.reshape(8, 4, 2, unit, span), hidden_grad, normed_mlp, packed_grad, normed, act,
+        name='finish')(down.reshape(grouped(down.shape[0])), dense.reshape(8, 4, 2, unit, span), hidden_grad, normed_mlp.reshape(grouped(tokens)), packed_grad, normed.reshape(grouped(tokens)), act,
         context, w_up, w_down, w_qkv, dense_in, norms, columns(h_sums), columns(p_sums), bias)
     grads = [grad.reshape(-1, width) for grad in result[:4]]
     return (grads, result[4], result[5], result[11])

time: 634 us -> 611 us (0.964)
  Pallas kernels: 539 us -> 516 us
    pallas_call x1, Pallas kernels: 383 us -> 360 us  [finish(): pl.pallas_call(finish_kernel, out_shape=(*sums, token, token, *others, ja...]
  transfers between devices with their start and end apart: 2 -> 2, of which waited for: 0 -> 0; matrix products, arithmetic and copies ran while one was open for 9% -> 9% of each run, Pallas kernels for 66% -> 65%
where the time goes in v7:
time: 611 us; the launch traced here: 602 us
  Pallas kernels  516 us (84%)
  other arithmetic  27.9 us (5%)
  matrix products  27.1 us (4%)
  between operations  14.5 us (2%)
  local copies, waits for them, and re-layouts  13 us (2%)
    pallas_call x1, Pallas kernels, finish(): pl.pallas_call(finish_kernel, out_shape=(*sums, token, token, *others, ja...  360 us
    pallas_call x1, Pallas kernels, gather_both(): pl.pallas_call(gather_kernel, out_shape=(shape, shape, jax.ShapeDtypeStru...  125 us
    dot_general x3, matrix products, contract_rows(): lax.dot_general(former, latter, (((0,), (0,)), ((), ())), preferred_eleme...  27.1 us
    pallas_call x1, Pallas kernels, upstream_parts(): pl.pallas_call(upstream_kernel, grid=(tokens // rows,), out_shape=(jax.Sh...  17.8 us
    pallas_call x1, Pallas kernels, attend(): pl.pallas_call(attention_kernel, grid=(tokens // length,), out_shape=(jax...  13.4 us
  transfers between devices with their start and end apart: 2, of which 0 were waited for; matrix products, arithmetic and copies ran while one was open for 9% of the time, Pallas kernels for 65%

profile of v7, /device:TPU:0, one launch (start us, length us, event | category | flops | bytes accessed | tf_op | source)
XLA Modules:
  0.0 601.9 jit_solution(17334419704306485222)
XLA Ops:
  7.2 0.8 dynamic_slice.10
  8.0 0.7 dynamic_slice.9
  8.7 0.8 pad_maximum_fusion.1.norm_ref
  9.5 1.2 copy-done
  10.7 1.2 copy-done.3
  11.9 0.7 copy-done.7
  12.6 124.7 %gather_tokens.1 = (bf16[2,4,8,32,2048]{4,3,2,1,0:T(8,128)(2,1)}, bf16[2,4,8,32,2048]{4,3,2,1,0:T(8,128)(2,1)}, s32[2,8,128]{2,1,0:T(8,128)S(1)}, bf16[2048,2048...) custom-call(bf16[256,2048]{1,0:T(8,128)(2,1)S(1)} %bitcast.69, ...), custom_call_target="tpu_custom_call" | custom-call | tf_op jit(solution)/shard_map/gather_tokens/pallas_call | solution.py:444
  137.3 1.7 copy-done.8
  139.0 1.0 copy.41
  140.0 3.6 all-to-all-start
  143.8 9.9 %convolution_convert_fusion.1 = bf16[512,2048]{1,0:T(8,128)(2,1)} fusion(bf16[2048,2048]{1,0:T(8,128)(2,1)} %bitcast.99, bf16[2048,1024]{1,0:T(8,128)(2,1)} %get-tuple-element.43.act_ref), kind=kOutput, calls=%fused_computation.7 | convolution fusion | flops 4296015872 | bytes 12582912 | tf_op jit(solution)/shard_map/dot_general | solution.py:30
  153.9 0.6 reduce-window.6
  155.7 1.8 multiply_cosine_fusion
  157.5 1.0 pad_maximum_fusion.table_ref
  158.6 10.3 %convolution_convert_fusion = bf16[512,2048]{1,0:T(8,128)(2,1)} fusion(bf16[2048,2048]{1,0:T(8,128)(2,1)} %bitcast.100, bf16[2048,1024]{1,0:T(8,128)(2,1)} %get-tuple-element.43.act_ref), kind=kOutput, calls=%fused_computation.6 | convolution fusion | flops 4296015872 | bytes 12582912 | tf_op jit(solution)/shard_map/dot_general | solution.py:30
  168.9 17.8 %upstream_parts.1 = (bf16[2048,1024]{1,0:T(8,128)(2,1)}, bf16[2048,256]{1,0:T(8,128)(2,1)S(1)}, f32[8,2048]{1,0:T(8,128)S(1)}, f32[8,1024]{1,0:T(8,128)S(1)}) custom-call(bf16[2048,2048]{1,0:T(8,128)(2,1)} %bitcast.101, f32[2048,1024]{1,0:T(8,128)} %get-tuple-element.45.slope_ref, bf16[1024,2048]{1,0:T(8,128)(2,1)} %down_w_ref.1, bf16[2048,256]{1,0:T(8,128)(2,1)S(1)} %bitcast.70), custom_call_target="tpu_custom_call" | custom-call | flops 10737418240 | bytes 27262976 | tf_op jit(solution)/shard_map/upstream_parts/pallas_call | solution.py:155
  186.6 13.4 %attend.1 = (bf16[2048,256]{1,0:T(8,128)(2,1)S(1)}, bf16[2048,768]{1,0:T(8,128)(2,1)}, f32[8,768]{1,0:T(8,128)S(1)}) custom-call(bf16[2048,768]{1,0:T(8,128)(2,1)} %copy-done.8, bf16[2048,256]{1,0:T(8,128)(2,1)S(1)} %get-tuple-element.47.grad_ref, f32[2,128,1024]{2,1,0:T(8,128)S(1)} %pad_maximum_fusion.table_ref), custom_call_target="tpu_custom_call" | custom-call | flops 4697620480 | bytes 9437184 | tf_op jit(solution)/shard_map/attend/pallas_call | solution.py:236
  200.2 0.7 reshape.262.bias_ref
  200.9 6.9 %convolution_convert_fusion.2 = bf16[2048,256]{1,0:T(8,128)(2,1)} fusion(bf16[2048,2048]{1,0:T(8,128)(2,1)} %bitcast.102, bf16[2048,256]{1,0:T(8,128)(2,1)S(1)} %get-tuple-element.49.context_ref), kind=kOutput, calls=%fused_computation.8 | convolution fusion | flops 2148007936 | bytes 10485760 | tf_op jit(solution)/shard_map/dot_general | solution.py:30
  207.8 0.9 broadcast_in_dim.8.p_col_ref
  208.7 1.0 broadcast_in_dim.7.h_col_ref
  209.7 359.8 %finish.1 = (bf16[2,4,2,32,2048]{4,3,2,1,0:T(8,128)(2,1)}, bf16[4,4,2,32,2048]{4,3,2,1,0:T(8,128)(2,1)}, bf16[3,4,2,32,2048]{4,3,2,1,0:T(8,128)(2,1)}, bf16[1,4,...) custom-call(bf16[2,4,2,32,2048]{4,3,2,1,0:T(8,128)(2,1)} %bitcast.80, ...), custom_call_target="tpu_custom_call" | custom-call | tf_op jit(solution)/shard_map/finish/pallas_call | solution.py:858
  569.6 1.6 convert_element_type.124
  571.5 0.8 fusion.15
  572.3 1.6 bitcast_convert_fusion.2
  574.5 0.6 copy.35
  575.1 0.6 reshape.263
  575.7 4.2 fusion.8
  579.9 3.8 bitcast_convert_fusion.1
  583.7 4.7 bitcast_convert_fusion
  588.4 5.9 maximum_convert_fusion
  594.3 0.6 copy.46
  (71 shorter events, 2.6 us)
Async XLA Ops:
  9.4 127.9 %copy-start.6 = (f32[4,2048]{1,0:T(4,128)}, f32[4,2048]{1,0:T(4,128)S(1)}, u32[]{:S(2)}) copy-start(f32[4,2048]{1,0:T(4,128)S(1)} %pad_maximum_fusion.1.norm_ref) | copy-start | bytes 98308
  9.4 1.2 copy-start
  10.7 1.2 copy-start.3
  11.9 0.7 copy-start.7
  12.6 126.4 %copy-start.15 = (bf16[256,2048]{1,0:T(8,128)(2,1)S(1)}, bf16[256,2048]{1,0:T(8,128)(2,1)}, u32[]{:S(2)}) copy-start(bf16[256,2048]{1,0:T(8,128)(2,1)} %param.23) | copy-start | bytes 3145732
  137.3 1.7 copy-start.8
  140.0 28.8 %all-to-all-start = ((bf16[256,8,256]{2,0,1:T(8,128)(2,1)}), bf16[256,8,256]{2,0,1:T(8,128)(2,1)S(1)}, u32[]{:S(2)}, u32[]{:S(2)}) async-start(bf16[256,8,256]{2,0,1:T(8,128)(2,1)} %bitcast.63), calls=%async_computation | async-start | bytes 2097152 | tf_op jit(solution)/shard_map/all_to_all | solution.py:1002
  143.6 444.8 %all-reduce.3.cloned.1.call-start = ((), (), s32[]{:S(2)}) async-start(), calls=%async_computation.1 | async-start | bytes 4194304 | tf_op jit(solution)/shard_map/psum | solution.py:1005
  153.7 1.3 copy-start.1
  153.7 3.8 copy-start.18
  153.7 3.8 copy-start.19
  168.9 17.8 %copy-start.2 = (bf16[256,8,256]{2,0,1:T(8,128)(2,1)}, bf16[256,8,256]{2,0,1:T(8,128)(2,1)S(1)}, u32[]{:S(2)}) copy-start(bf16[256,8,256]{2,0,1:T(8,128)(2,1)S(1)} %all-to-all-done) | copy-start | bytes 3145732
  200.0 7.8 %copy-start.5 = (bf16[2048,256]{1,0:T(8,128)(2,1)}, bf16[2048,256]{1,0:T(8,128)(2,1)S(1)}, u32[]{:S(2)}) copy-start(bf16[2048,256]{1,0:T(8,128)(2,1)S(1)} %get-tuple-element.49.context_ref) | copy-start | bytes 3145732
  569.6 1.6 copy-start.11
  569.6 1.9 copy-start.17
  569.6 2.7 copy-start.14
  571.2 2.7 copy-start.9
  572.3 22.0 %copy-start.20 = (f32[1,256]{1,0:T(1,128)}, f32[1,256]{1,0:T(1,128)S(1)}, u32[]{:S(2)}) copy-start(f32[1,256]{1,0:T(1,128)S(1)} %get-tuple-element.66) | copy-start | bytes 3076
  573.9 1.8 copy-start.4
  573.9 1.8 copy-start.16
  575.7 4.2 copy-start.12
  579.9 3.8 copy-start.10
  583.7 4.8 copy-start.13
Sparse Core Ops, SparseCore 0:
  153.9 108.2 all-reduce.2

commit v8 on v7

--- a/solution.py
+++ b/solution.py
@@ -266,9 +266,9 @@
     return (f_x, f_y, f + 1 - 2 * (f % 2), f_x + f_y - f)
 
 
-def gather_kernel(x_ref, c_ref, seg_ref, up_ref, qkv_ref, b_up_ref, b_qkv_ref, norm_ref, xg_ref, cg_ref, segs_ref, normed_out, normed_mlp_out,
+def gather_kernel(x_ref, c_ref, seg_ref, up_ref, qkv_ref, b_up_in, b_qkv_in, norm_in, xg_ref, cg_ref, segs_ref, normed_out, normed_mlp_out,
     packed_out, act_out, slope_out, held, tile, w_up, w_qkv, normed, normed_mlp, packed, act, slope, seg_s, seg_r, seg_l, s1, r1, s2, r2, s3, r3,
-    local, w_l, tile_l, keep_l):
+    local, w_l, tile_l, keep_l, b_up_ref, b_qkv_ref, norm_ref):
     f, s = (lax.axis_index('fsdp'), lax.axis_index('sp'))
     core = f % 2
     f_x, f_y, f_c, f_d = neighbours(f)
@@ -293,7 +293,12 @@
         keep_seg.start()
         for copy in give_seg:
             copy.start()
-    weights = [pltpu.make_async_copy(up_ref, w_up, w_l.at[0]), pltpu.make_async_copy(qkv_ref, w_qkv, w_l.at[1])]
+    weights = [
+        pltpu.make_async_copy(ref, held_ref, w_l.at[n])
+        for n, (ref, held_ref) in enumerate(
+            ((up_ref, w_up), (qkv_ref, w_qkv), (b_up_in, b_up_ref), (b_qkv_in, b_qkv_ref), (norm_in, norm_ref))
+        )
+    ]
     for copy in weights:
         copy.start()
     kept = []
@@ -363,37 +368,38 @@
         rows = pl.ds(pl.multiple_of((b * 4 + z) * size, size), size)
         return pltpu.make_async_copy(results[n][0].at[b], results[n][1].at[rows], keep_l.at[b, n])
 
-    def work(k):
+    tiles = {}
+
+    def work(k, b):
         z = (s + 4 - k) % 4
-        loads = [pltpu.make_async_copy(xg_ref.at[b, z], tile.at[b], tile_l.at[b]) for b in range(2)]
-        for copy in loads:
-            copy.start()
-        if k == 0:
-            for copy in weights:
-                copy.wait()
-        for b in range(2):
-            loads[b].wait()
-            if k:
-                for n in range(5):
-                    keep(b, (s + 5 - k) % 4, n).wait()
-
-            @pl.loop(0, 8)
-            def _(i):
-                inputs = tile[b, i].astype(jnp.float32)
-                centred = inputs - jnp.mean(inputs, axis=-1, keepdims=True)
-                variance = jnp.mean(centred * centred, axis=-1, keepdims=True)
-                scaled = centred * lax.rsqrt(variance + EPSILON)
-                rows = pl.ds(pl.multiple_of(i * piece, piece), piece)
-                low = normed.dtype
-                normed[b, rows, :] = (scaled * norm_ref[0:1, :] + norm_ref[1:2, :]).astype(low)
-                normed_mlp[b, rows, :] = (scaled * norm_ref[2:3, :] + norm_ref[3:4, :]).astype(low)
-            hidden = times_transposed(normed_mlp[b], w_up[...]) + b_up_ref[...]
-            packed[b] = (times_transposed(normed[b], w_qkv[...]) + b_qkv_ref[...]).astype(packed.dtype)
-            activated, grown = gelu_pair(hidden)
-            act[b] = activated.astype(act.dtype)
-            slope[b] = grown
+        if b == 0:
+            for half in range(2):
+                tiles[half] = copied(xg_ref.at[half, z], tile.at[half], tile_l.at[half])
+            if k == 0:
+                for copy in weights:
+                    copy.wait()
+        tiles[b].wait()
+        if k:
             for n in range(5):
-                keep(b, z, n).start()
+                keep(b, (s + 5 - k) % 4, n).wait()
+
+        @pl.loop(0, 8)
+        def _(i):
+            inputs = tile[b, i].astype(jnp.float32)
+            centred = inputs - jnp.mean(inputs, axis=-1, keepdims=True)
+            variance = jnp.mean(centred * centred, axis=-1, keepdims=True)
+            scaled = centred * lax.rsqrt(variance + EPSILON)
+            rows = pl.ds(pl.multiple_of(i * piece, piece), piece)
+            low = normed.dtype
+            normed[b, rows, :] = (scaled * norm_ref[0:1, :] + norm_ref[1:2, :]).astype(low)
+            normed_mlp[b, rows, :] = (scaled * norm_ref[2:3, :] + norm_ref[3:4, :]).astype(low)
+        hidden = times_transposed(normed_mlp[b], w_up[...]) + b_up_ref[...]
+        packed[b] = (times_transposed(normed[b], w_qkv[...]) + b_qkv_ref[...]).astype(packed.dtype)
+        activated, grown = gelu_pair(hidden)
+        act[b] = activated.astype(act.dtype)
+        slope[b] = grown
+        for n in range(5):
+            keep(b, z, n).start()
     own0 = to_planes(0)
     own1 = to_planes(1)
     steps = [(a, k) for a in range(2) for k in range(4)]
@@ -403,13 +409,15 @@
             if k == 0:
                 (own0 if a == 0 else own1).wait()
             spread(a, k)
+        if 3 <= i < 7:
+            from_core(0, i - 3)
+            work(i - 3, 0)
         if 0 <= i - 1 < len(steps):
             pass_on(*steps[i - 1])
         if 0 <= i - 2 < len(steps):
             pass_corner(*steps[i - 2])
-        if 5 <= i < 9:
-            from_core(0, i - 5)
-            work(i - 5)
+        if 3 <= i < 7:
+            work(i - 3, 1)
     for k in range(4):
         from_core(1, k)
     for b in range(2):
@@ -439,13 +447,13 @@
     dma = pltpu.SemaphoreType.DMA
     vmem = pltpu.VMEM
     anywhere = pl.BlockSpec(memory_space=pl.ANY)
-    inside = pl.BlockSpec(memory_space=pltpu.VMEM)
     sizes = ((width, x.dtype), (width, x.dtype), (columns, x.dtype), (units, x.dtype), (units, jnp.float32))
     return pl.pallas_call(gather_kernel, out_shape=(shape, shape, jax.ShapeDtypeStruct((2, *segments.shape), segments.dtype),
-        *(jax.ShapeDtypeStruct((tokens, size), kind) for size, kind in sizes)), in_specs=[anywhere] * 5 + [inside] * 3, out_specs=[anywhere] * 8,
+        *(jax.ShapeDtypeStruct((tokens, size), kind) for size, kind in sizes)), in_specs=[anywhere] * 8, out_specs=[anywhere] * 8,
         scratch_shapes=[vmem((2, 8, piece, width), x.dtype), vmem((2, 8, piece, width), x.dtype), vmem(w_up.shape, w_up.dtype), vmem(w_qkv.shape,
         w_qkv.dtype), *(vmem((2, 8 * piece, size), kind) for size, kind in sizes), dma((8,)), dma((2,)), dma((1,)), dma((2, 8)), dma((2, 8)), dma((2,
-        4)), dma((2, 4)), dma((2, 9, 4)), dma((2, 9, 4)), dma((2, 2)), dma((2,)), dma((2,)), dma((2, 5))],
+        4)), dma((2, 4)), dma((2, 9, 4)), dma((2, 9, 4)), dma((2, 2)), dma((5,)), dma((2,)), dma((2, 5)),
+        vmem((1, units), jnp.float32), vmem((1, columns), jnp.float32), vmem(norms.shape, jnp.float32)],
         compiler_params=pltpu.CompilerParams(collective_id=1, has_side_effects=True, vmem_limit_bytes=48 * 1024 * 1024), name='gather_tokens')(x, c,
         segments, w_up, w_qkv, b_up.reshape(1, units), b_qkv.reshape(1, columns), norms)
 
@@ -818,14 +826,14 @@
     2: (("up", 1, 2),),
     3: (("up", 2, 4),),
     4: (("qkv", 0, 3),),
-    5: (("out", 0, 6),),
-    6: (("out", 6, 8), ("back", 0, 3)),
-    7: (("pair", 0, 3), ("turned", 0, 1), ("back", 3, 5)),
-    8: (("back", 5, 8), ("vectors", 0, 1)),
-    9: (("pair", 3, 6), ("chips", 0, 1)),
-    10: (("home", 0, 1), ("sums", 0, 1)),
-    12: (("chips", 1, 2),),
-    13: (("small", 0, 1),),
+    5: (("out", 0, 8),),
+    6: (("pair", 0, 3), ("back", 0, 3)),
+    7: (("back", 3, 6), ("turned", 0, 1)),
+    8: (("back", 6, 8), ("vectors", 0, 1), ("pair", 3, 6)),
+    9: (("chips", 0, 1),),
+    10: (("sums", 0, 1),),
+    11: (("home", 0, 1), ("chips", 1, 2)),
+    12: (("small", 0, 1),),
     14: (("home", 1, 2),),
 }
 
@@ -869,6 +877,35 @@
         context, w_up, w_down, w_qkv, dense_in, norms, columns(h_sums), columns(p_sums), bias)
     grads = [grad.reshape(-1, width) for grad in result[:4]]
     return (grads, result[4], result[5], result[11])
+
+
+def widen_kernel(early_ref, late_ref, up_ref, qkv_ref, dense_ref, down_out, up_out, qkv_out, dense_out):
+    down_out[0] = early_ref[...].astype(jnp.float32)
+    down_out[1] = late_ref[...].astype(jnp.float32)
+    for ref, out in ((up_ref, up_out), (qkv_ref, qkv_out), (dense_ref, dense_out)):
+        out[...] = ref[...].astype(jnp.float32)
+
+
+def widen(early, late, up, qkv, dense, steps=8):
+    width = up.shape[1]
+
+    def tile(array):
+        return pl.BlockSpec((array.shape[0] // steps, width), lambda i: (i, 0))
+
+    arrays = (early, late, up, qkv, dense)
+    wide = jax.ShapeDtypeStruct((2, early.shape[0], width), jnp.float32)
+    number = 2 * early.size + up.size + qkv.size + dense.size
+    down, up, qkv, dense = pl.pallas_call(
+        widen_kernel,
+        grid=(steps,),
+        out_shape=(wide, *(jax.ShapeDtypeStruct(array.shape, jnp.float32) for array in arrays[2:])),
+        in_specs=[tile(array) for array in arrays],
+        out_specs=[pl.BlockSpec((2, early.shape[0] // steps, width), lambda i: (0, i, 0)), *(tile(array) for array in arrays[2:])],
+        compiler_params=pltpu.CompilerParams(vmem_limit_bytes=60 * 1024 * 1024),
+        cost_estimate=pl.CostEstimate(flops=0, transcendentals=0, bytes_accessed=6 * number),
+        name="widen",
+    )(*arrays)
+    return down.reshape(-1, width), up, qkv, dense
 
 
 def own_tokens(hidden_in, cotangent, output, weighted, shift):
@@ -1002,7 +1039,7 @@
     dense_in = lax.all_to_all(w_dense, 'fsdp', split_axis=1, concat_axis=0, tiled=True)
     early = activated.shape[1] // 2
     down_term = contract_rows(activated[:, :early], upstream).astype(jnp.bfloat16)
-    early_down_w = lax.psum(down_term, 'sp').astype(jnp.float32)
+    early_down_w = lax.psum(down_term, 'sp')
     slope, activated, down_term = lax.optimization_barrier((slope, activated, down_term))
     hidden_grad, context_grad, c_sums, h_sums = upstream_parts(upstream, slope, w_down, dense_in)
     context, packed_grad, p_sums = attend(packed, context_grad, head_tables(rows.reshape(group, seq_len)), seq_len)
@@ -1012,8 +1049,7 @@
     bias_out = own_part(jnp.sum(c_sums, axis=0))
     grads, output, weighted, sums = finish(late_down_term, dense_term, hidden_grad, normed_mlp, packed_grad, normed, activated, context, w_up,
         w_down, w_qkv, dense_in, norms, bias_up, bias_qkv, jnp.concatenate([bias_out, bias_qkv, bias_up]).reshape(8, share))
-    late_down_w, grad_up_w, grad_qkv_w, grad_dense_w = (grad.astype(jnp.float32) for grad in grads)
-    grad_down_w = jnp.concatenate([early_down_w, late_down_w])
+    grad_down_w, grad_up_w, grad_qkv_w, grad_dense_w = widen(early_down_w, *grads)
     bias_out = sums[8]
     output, input_grad = own_tokens(hidden_in, cotangent, output.reshape(hidden_in.shape), weighted.reshape(hidden_in.shape), b_dense + b_down)
     return (output, input_grad, sums[0], sums[1], sums[2], sums[3], grad_qkv_w, sums[9:12].reshape(-1), grad_dense_w, bias_out, grad_up_w,

time: 611 us -> 599 us (0.980)
  other arithmetic: 27.9 us -> 13 us
    pallas_call x0 -> x1, Pallas kernels: none -> 14.1 us  [widen(): pl.pallas_call(widen_kernel, grid=(steps,), out_shape=(wide, *(jax.ShapeD...]
    pallas_call x1, Pallas kernels: 125 us -> 114 us  [gather_both(): pl.pallas_call(gather_kernel, out_shape=(shape, shape, jax.ShapeDtypeStru...]
    convert_element_type x3 -> x0, other arithmetic: 10.1 us -> none  [by_kernels(): grad.astype(jnp.float32)]
  transfers between devices with their start and end apart: 2 -> 2, of which waited for: 0 -> 0; matrix products, arithmetic and copies ran while one was open for 9% -> 7% of each run, Pallas kernels for 65% -> 66%
where the time goes in v8:
time: 599 us; the launch traced here: 589 us
  Pallas kernels  518 us (86%)
  matrix products  27.1 us (5%)
  between operations  14.7 us (2%)
  other arithmetic  13 us (2%)
  local copies, waits for them, and re-layouts  12.6 us (2%)
    pallas_call x1, Pallas kernels, finish(): pl.pallas_call(finish_kernel, out_shape=(*sums, token, token, *others, ja...  359 us
    pallas_call x1, Pallas kernels, gather_both(): pl.pallas_call(gather_kernel, out_shape=(shape, shape, jax.ShapeDtypeStru...  114 us
    dot_general x3, matrix products, contract_rows(): lax.dot_general(former, latter, (((0,), (0,)), ((), ())), preferred_eleme...  27.1 us
    pallas_call x1, Pallas kernels, upstream_parts(): pl.pallas_call(upstream_kernel, grid=(tokens // rows,), out_shape=(jax.Sh...  17.8 us
    pallas_call x1, Pallas kernels, widen(): pl.pallas_call(widen_kernel, grid=(steps,), out_shape=(wide, *(jax.ShapeD...  14.1 us
    pallas_call x1, Pallas kernels, attend(): pl.pallas_call(attention_kernel, grid=(tokens // length,), out_shape=(jax...  13.2 us
  transfers between devices with their start and end apart: 2, of which 0 were waited for; matrix products, arithmetic and copies ran while one was open for 7% of the time, Pallas kernels for 66%

profile of v8, /device:TPU:0, one launch (start us, length us, event | category | flops | bytes accessed | tf_op | source)
XLA Modules:
  0.0 589.5 jit_solution(8885517286036616872)
XLA Ops:
  7.2 0.8 dynamic_slice.10
  8.0 0.7 dynamic_slice.9
  8.7 0.8 pad_maximum_fusion.1.norm_in.norm_ref
  9.5 1.2 copy-done
  10.7 1.2 copy-done.3
  11.9 0.7 copy-done.7
  12.6 113.9 %gather_tokens.1 = (bf16[2,4,8,32,2048]{4,3,2,1,0:T(8,128)(2,1)}, bf16[2,4,8,32,2048]{4,3,2,1,0:T(8,128)(2,1)}, s32[2,8,128]{2,1,0:T(8,128)S(1)}, bf16[2048,2048...) custom-call(bf16[256,2048]{1,0:T(8,128)(2,1)S(1)} %bitcast.64, ...), custom_call_target="tpu_custom_call" | custom-call | tf_op jit(solution)/shard_map/gather_tokens/pallas_call | solution.py:451
  126.5 1.7 copy-done.8
  128.2 1.0 copy.41
  129.2 3.6 all-to-all-start
  133.0 9.9 %convolution_convert_fusion.1 = bf16[512,2048]{1,0:T(8,128)(2,1)} fusion(bf16[2048,2048]{1,0:T(8,128)(2,1)} %bitcast.97, bf16[2048,1024]{1,0:T(8,128)(2,1)} %get-tuple-element.47.act_ref), kind=kOutput, calls=%fused_computation.4 | convolution fusion | flops 4296015872 | bytes 12582912 | tf_op jit(solution)/shard_map/dot_general | solution.py:30
  143.1 0.6 reduce-window.6
  144.2 0.2 convert_reduce_fusion
  144.5 0.4 fusion.9
  144.9 1.8 multiply_cosine_fusion
  146.7 1.0 pad_maximum_fusion.table_ref
  147.8 9.9 %convolution_convert_fusion = bf16[512,2048]{1,0:T(8,128)(2,1)} fusion(bf16[2048,2048]{1,0:T(8,128)(2,1)} %bitcast.98, bf16[2048,1024]{1,0:T(8,128)(2,1)} %get-tuple-element.47.act_ref), kind=kOutput, calls=%fused_computation.3 | convolution fusion | flops 4296015872 | bytes 12582912 | tf_op jit(solution)/shard_map/dot_general | solution.py:30
  157.7 17.8 %upstream_parts.1 = (bf16[2048,1024]{1,0:T(8,128)(2,1)}, bf16[2048,256]{1,0:T(8,128)(2,1)S(1)}, f32[8,2048]{1,0:T(8,128)S(1)}, f32[8,1024]{1,0:T(8,128)S(1)}) custom-call(bf16[2048,2048]{1,0:T(8,128)(2,1)} %bitcast.99, f32[2048,1024]{1,0:T(8,128)} %get-tuple-element.49.slope_ref, bf16[1024,2048]{1,0:T(8,128)(2,1)} %down_w_ref.1, bf16[2048,256]{1,0:T(8,128)(2,1)S(1)} %bitcast.65), custom_call_target="tpu_custom_call" | custom-call | flops 10737418240 | bytes 27262976 | tf_op jit(solution)/shard_map/upstream_parts/pallas_call | solution.py:155
  175.4 13.2 %attend.1 = (bf16[2048,256]{1,0:T(8,128)(2,1)S(1)}, bf16[2048,768]{1,0:T(8,128)(2,1)}, f32[8,768]{1,0:T(8,128)S(1)}) custom-call(bf16[2048,768]{1,0:T(8,128)(2,1)} %copy-done.8, bf16[2048,256]{1,0:T(8,128)(2,1)S(1)} %get-tuple-element.51.grad_ref, f32[2,128,1024]{2,1,0:T(8,128)S(1)} %pad_maximum_fusion.table_ref), custom_call_target="tpu_custom_call" | custom-call | flops 4697620480 | bytes 9437184 | tf_op jit(solution)/shard_map/attend/pallas_call | solution.py:236
  188.6 7.3 %convolution_convert_fusion.2 = bf16[2048,256]{1,0:T(8,128)(2,1)} fusion(bf16[2048,2048]{1,0:T(8,128)(2,1)} %bitcast.100, bf16[2048,256]{1,0:T(8,128)(2,1)S(1)} %get-tuple-element.53.context_ref), kind=kOutput, calls=%fused_computation.5 | convolution fusion | flops 2148007936 | bytes 10485760 | tf_op jit(solution)/shard_map/dot_general | solution.py:30
  196.1 0.6 reshape.265.bias_ref
  196.7 0.9 broadcast_in_dim.8.p_col_ref
  197.6 1.0 broadcast_in_dim.7.h_col_ref
  198.6 359.3 %finish.1 = (bf16[2,4,2,32,2048]{4,3,2,1,0:T(8,128)(2,1)}, bf16[4,4,2,32,2048]{4,3,2,1,0:T(8,128)(2,1)}, bf16[3,4,2,32,2048]{4,3,2,1,0:T(8,128)(2,1)}, bf16[1,4,...) custom-call(bf16[2,4,2,32,2048]{4,3,2,1,0:T(8,128)(2,1)} %bitcast.77, ...), custom_call_target="tpu_custom_call" | custom-call | tf_op jit(solution)/shard_map/finish/pallas_call | solution.py:866
  557.9 2.9 convert_element_type.94
  561.1 0.6 copy.35
  561.7 0.6 reshape.270
  562.3 0.6 fusion.15
  562.9 2.1 fusion.4
  565.1 2.5 fusion.8
  567.5 14.1 %widen.1 = (f32[2,512,2048]{2,1,0:T(8,128)}, f32[1024,2048]{1,0:T(8,128)}, f32[768,2048]{1,0:T(8,128)}, f32[256,2048]{1,0:T(8,128)}) custom-call(bf16[512,2048]{1,0:T(8,128)(2,1)} %all-reduce.3.cloned.1.call-done.early_ref, bf16[512,2048]{1,0:T(8,128)(2,1)} %bitcast.78, bf16[1024,2048]{1,0:T(8,128)(2,1)} %bitcast.75, bf16[768,2048]{1,0:T(8,128)(2,1)} %bitcast.76, ...), custom_call_target="tpu_custom_call" | custom-call | bytes 37748736 | tf_op jit(solution)/shard_map/widen/pallas_call | solution.py:898
  581.6 0.6 copy.46
  (60 shorter events, 1.5 us)
Async XLA Ops:
  9.4 117.1 %copy-start.6 = (f32[4,2048]{1,0:T(4,128)}, f32[4,2048]{1,0:T(4,128)S(1)}, u32[]{:S(2)}) copy-start(f32[4,2048]{1,0:T(4,128)S(1)} %pad_maximum_fusion.1.norm_in.norm_ref) | copy-start | bytes 98308
  9.4 1.2 copy-start
  10.7 1.2 copy-start.3
  11.9 0.7 copy-start.7
  12.6 115.6 %copy-start.11 = (bf16[256,2048]{1,0:T(8,128)(2,1)S(1)}, bf16[256,2048]{1,0:T(8,128)(2,1)}, u32[]{:S(2)}) copy-start(bf16[256,2048]{1,0:T(8,128)(2,1)} %param.23) | copy-start | bytes 3145732
  126.5 1.7 copy-start.8
  129.2 28.4 %all-to-all-start = ((bf16[256,8,256]{2,0,1:T(8,128)(2,1)}), bf16[256,8,256]{2,0,1:T(8,128)(2,1)S(1)}, u32[]{:S(2)}, u32[]{:S(2)}) async-start(bf16[256,8,256]{2,0,1:T(8,128)(2,1)} %bitcast.58), calls=%async_computation | async-start | bytes 2097152 | tf_op jit(solution)/shard_map/all_to_all | solution.py:1039
  132.8 434.7 %all-reduce.3.cloned.1.call-start = ((), (), s32[]{:S(2)}) async-start(), calls=%async_computation.1 | async-start | bytes 4194304 | tf_op jit(solution)/shard_map/psum | solution.py:1042
  142.9 1.3 copy-start.1
  142.9 3.8 copy-start.14
  142.9 3.8 copy-start.15
  157.7 17.8 %copy-start.2 = (bf16[256,8,256]{2,0,1:T(8,128)(2,1)}, bf16[256,8,256]{2,0,1:T(8,128)(2,1)S(1)}, u32[]{:S(2)}) copy-start(bf16[256,8,256]{2,0,1:T(8,128)(2,1)S(1)} %all-to-all-done) | copy-start | bytes 3145732
  188.6 7.3 %copy-start.5 = (bf16[2048,256]{1,0:T(8,128)(2,1)}, bf16[2048,256]{1,0:T(8,128)(2,1)S(1)}, u32[]{:S(2)}) copy-start(bf16[2048,256]{1,0:T(8,128)(2,1)S(1)} %get-tuple-element.53.context_ref) | copy-start | bytes 3145732
  557.9 2.9 copy-start.10
  557.9 3.2 copy-start.13
  560.8 4.2 copy-start.4
  560.8 4.2 copy-start.12
  562.3 2.7 copy-start.9
  562.9 18.7 %copy-start.16 = (f32[1,256]{1,0:T(1,128)}, f32[1,256]{1,0:T(1,128)S(1)}, u32[]{:S(2)}) copy-start(f32[1,256]{1,0:T(1,128)S(1)} %get-tuple-element.74) | copy-start | bytes 3076
Sparse Core Ops, SparseCore 0:
  143.1 113.4 all-reduce.2

commit v9 on v8

--- a/solution.py
+++ b/solution.py
@@ -454,7 +454,7 @@
         w_qkv.dtype), *(vmem((2, 8 * piece, size), kind) for size, kind in sizes), dma((8,)), dma((2,)), dma((1,)), dma((2, 8)), dma((2, 8)), dma((2,
         4)), dma((2, 4)), dma((2, 9, 4)), dma((2, 9, 4)), dma((2, 2)), dma((5,)), dma((2,)), dma((2, 5)),
         vmem((1, units), jnp.float32), vmem((1, columns), jnp.float32), vmem(norms.shape, jnp.float32)],
-        compiler_params=pltpu.CompilerParams(collective_id=1, has_side_effects=True, vmem_limit_bytes=48 * 1024 * 1024), name='gather_tokens')(x, c,
+        compiler_params=pltpu.CompilerParams(collective_id=1, has_side_effects=True, vmem_limit_bytes=60 * 1024 * 1024), name='gather_tokens')(x, c,
         segments, w_up, w_qkv, b_up.reshape(1, units), b_qkv.reshape(1, columns), norms)
 
 
@@ -879,33 +879,52 @@
     return (grads, result[4], result[5], result[11])
 
 
-def widen_kernel(early_ref, late_ref, up_ref, qkv_ref, dense_ref, down_out, up_out, qkv_out, dense_out):
+def last_kernel(
+    x_ref, c_ref, out_ref, back_ref, shift_ref, early_ref, late_ref, up_ref, qkv_ref, dense_ref,
+    output, input_grad, down_out, up_out, qkv_out, dense_out,
+):
+    inputs = x_ref[...].astype(jnp.float32)
+    output[...] = (inputs + (out_ref[...].astype(jnp.float32) + shift_ref[...])).astype(output.dtype)
+    centred = inputs - jnp.mean(inputs, axis=-1, keepdims=True)
+    inverse = lax.rsqrt(jnp.mean(centred * centred, axis=-1, keepdims=True) + EPSILON)
+    scaled = centred * inverse
+    weighted = back_ref[...].astype(jnp.float32)
+    first_mean = jnp.mean(weighted, axis=-1, keepdims=True)
+    second_mean = jnp.mean(weighted * scaled, axis=-1, keepdims=True)
+    change = inverse * (weighted - first_mean - scaled * second_mean)
+    input_grad[...] = (c_ref[...].astype(jnp.float32) + change).astype(input_grad.dtype)
     down_out[0] = early_ref[...].astype(jnp.float32)
     down_out[1] = late_ref[...].astype(jnp.float32)
     for ref, out in ((up_ref, up_out), (qkv_ref, qkv_out), (dense_ref, dense_out)):
         out[...] = ref[...].astype(jnp.float32)
 
 
-def widen(early, late, up, qkv, dense, steps=8):
+def last(x, c, out, back, shift, early, late, up, qkv, dense, steps=8):
     width = up.shape[1]
 
     def tile(array):
         return pl.BlockSpec((array.shape[0] // steps, width), lambda i: (i, 0))
 
-    arrays = (early, late, up, qkv, dense)
+    tokens, sums = (x, c, out, back), (early, late, up, qkv, dense)
     wide = jax.ShapeDtypeStruct((2, early.shape[0], width), jnp.float32)
     number = 2 * early.size + up.size + qkv.size + dense.size
-    down, up, qkv, dense = pl.pallas_call(
-        widen_kernel,
+    output, input_grad, down, up, qkv, dense = pl.pallas_call(
+        last_kernel,
         grid=(steps,),
-        out_shape=(wide, *(jax.ShapeDtypeStruct(array.shape, jnp.float32) for array in arrays[2:])),
-        in_specs=[tile(array) for array in arrays],
-        out_specs=[pl.BlockSpec((2, early.shape[0] // steps, width), lambda i: (0, i, 0)), *(tile(array) for array in arrays[2:])],
+        out_shape=(
+            jax.ShapeDtypeStruct(x.shape, x.dtype), jax.ShapeDtypeStruct(x.shape, x.dtype), wide,
+            *(jax.ShapeDtypeStruct(array.shape, jnp.float32) for array in sums[2:]),
+        ),
+        in_specs=[tile(array) for array in tokens] + [pl.BlockSpec((1, width), lambda i: (0, 0))] + [tile(array) for array in sums],
+        out_specs=[
+            tile(x), tile(x), pl.BlockSpec((2, early.shape[0] // steps, width), lambda i: (0, i, 0)),
+            *(tile(array) for array in sums[2:]),
+        ],
         compiler_params=pltpu.CompilerParams(vmem_limit_bytes=60 * 1024 * 1024),
-        cost_estimate=pl.CostEstimate(flops=0, transcendentals=0, bytes_accessed=6 * number),
-        name="widen",
-    )(*arrays)
-    return down.reshape(-1, width), up, qkv, dense
+        cost_estimate=pl.CostEstimate(flops=20 * x.size, transcendentals=0, bytes_accessed=6 * number + 12 * x.size),
+        name="last",
+    )(*tokens, shift.reshape(1, width), *sums)
+    return output, input_grad, down.reshape(-1, width), up, qkv, dense
 
 
 def own_tokens(hidden_in, cotangent, output, weighted, shift):
@@ -1049,9 +1068,11 @@
     bias_out = own_part(jnp.sum(c_sums, axis=0))
     grads, output, weighted, sums = finish(late_down_term, dense_term, hidden_grad, normed_mlp, packed_grad, normed, activated, context, w_up,
         w_down, w_qkv, dense_in, norms, bias_up, bias_qkv, jnp.concatenate([bias_out, bias_qkv, bias_up]).reshape(8, share))
-    grad_down_w, grad_up_w, grad_qkv_w, grad_dense_w = widen(early_down_w, *grads)
+    output, input_grad, grad_down_w, grad_up_w, grad_qkv_w, grad_dense_w = last(
+        hidden_in[0], cotangent[0], output.reshape(-1, width), weighted.reshape(-1, width), b_dense + b_down, early_down_w, *grads
+    )
+    output, input_grad = output[None], input_grad[None]
     bias_out = sums[8]
-    output, input_grad = own_tokens(hidden_in, cotangent, output.reshape(hidden_in.shape), weighted.reshape(hidden_in.shape), b_dense + b_down)
     return (output, input_grad, sums[0], sums[1], sums[2], sums[3], grad_qkv_w, sums[9:12].reshape(-1), grad_dense_w, bias_out, grad_up_w,
         sums[12:16].reshape(-1), grad_down_w, bias_out)
 

time: 599 us -> 591 us (0.987)
  Pallas kernels: 518 us -> 511 us
    another operation x2, other arithmetic: 0.77 us -> 9.51 us
    pallas_call x1, Pallas kernels: 359 us -> 351 us  [finish(): pl.pallas_call(finish_kernel, out_shape=(*sums, token, token, *others, ja...]
  transfers between devices with their start and end apart: 2 -> 2, of which waited for: 0 -> 0; matrix products, arithmetic and copies ran while one was open for 7% -> 8% of each run, Pallas kernels for 66% -> 66%
where the time goes in v9:
time: 591 us; the launch traced here: 581 us
  Pallas kernels  511 us (86%)
  matrix products  27.4 us (5%)
  between operations  14.7 us (2%)
  other arithmetic  12.9 us (2%)
  local copies, waits for them, and re-layouts  11.3 us (2%)
    pallas_call x1, Pallas kernels, finish(): pl.pallas_call(finish_kernel, out_shape=(*sums, token, token, *others, ja...  351 us
    pallas_call x1, Pallas kernels, gather_both(): pl.pallas_call(gather_kernel, out_shape=(shape, shape, jax.ShapeDtypeStru...  112 us
    dot_general x3, matrix products, contract_rows(): lax.dot_general(former, latter, (((0,), (0,)), ((), ())), preferred_eleme...  27.4 us
    pallas_call x1, Pallas kernels, upstream_parts(): pl.pallas_call(upstream_kernel, grid=(tokens // rows,), out_shape=(jax.Sh...  17.8 us
    pallas_call x1, Pallas kernels, last(): pl.pallas_call(last_kernel, grid=(steps,), out_shape=(jax.ShapeDtypeStruc...  16.5 us
    pallas_call x1, Pallas kernels, attend(): pl.pallas_call(attention_kernel, grid=(tokens // length,), out_shape=(jax...  13.4 us
  transfers between devices with their start and end apart: 2, of which 0 were waited for; matrix products, arithmetic and copies ran while one was open for 8% of the time, Pallas kernels for 66%

profile of v9, /device:TPU:0, one launch (start us, length us, event | category | flops | bytes accessed | tf_op | source)
XLA Modules:
  0.0 581.3 jit_solution(1635735438750925728)
XLA Ops:
  7.2 0.8 dynamic_slice.10
  8.0 0.6 reshape.136.b_qkv_in
  8.5 1.3 dynamic_slice.9
  9.8 1.4 pad_maximum_fusion.1.norm_in.norm_ref
  11.2 112.4 %gather_tokens.1 = (bf16[2,4,8,32,2048]{4,3,2,1,0:T(8,128)(2,1)}, bf16[2,4,8,32,2048]{4,3,2,1,0:T(8,128)(2,1)}, s32[2,8,128]{2,1,0:T(8,128)}, bf16[2048,2048]{1,...) custom-call(bf16[256,2048]{1,0:T(8,128)(2,1)} %bitcast.64, ...), custom_call_target="tpu_custom_call" | custom-call | tf_op jit(solution)/shard_map/gather_tokens/pallas_call | solution.py:451
  123.6 1.0 copy.41
  124.6 3.6 all-to-all-start
  128.3 9.9 %convolution_convert_fusion.1 = bf16[512,2048]{1,0:T(8,128)(2,1)} fusion(bf16[2048,2048]{1,0:T(8,128)(2,1)} %bitcast.94, bf16[2048,1024]{1,0:T(8,128)(2,1)} %get-tuple-element.49.act_ref), kind=kOutput, calls=%fused_computation.1 | convolution fusion | flops 4296015872 | bytes 12582912 | tf_op jit(solution)/shard_map/dot_general | solution.py:30
  138.2 0.1 slice_compare_fusion
  138.3 0.1 fusion.2
  138.4 9.3 %reduce-window.6 = s32[2,8,128]{2,1,0:T(8,128)S(1)} reduce-window(s32[2,8,128]{2,1,0:T(8,128)S(1)} %bitcast.78, s32[]{:T(128)} %constant.13.clone.1), window={size=1x1x128 pad=0_0x0_0x127_0}, to_apply=%region_0.0 | reduce-window | flops 260096 | bytes 16388 | tf_op jit(solution)/shard_map/reduce-window
  147.7 0.2 slice_reduce_fusion
  148.0 0.2 reduce-window.9
  148.2 1.0 multiply_cosine_fusion
  149.3 0.6 add.17
  149.9 0.1 pad_maximum_fusion.table_ref
  150.0 10.3 %convolution_convert_fusion = bf16[512,2048]{1,0:T(8,128)(2,1)} fusion(bf16[2048,2048]{1,0:T(8,128)(2,1)} %bitcast.95, bf16[2048,1024]{1,0:T(8,128)(2,1)} %get-tuple-element.49.act_ref), kind=kOutput, calls=%fused_computation | convolution fusion | flops 4296015872 | bytes 12582912 | tf_op jit(solution)/shard_map/dot_general | solution.py:30
  160.3 17.8 %upstream_parts.1 = (bf16[2048,1024]{1,0:T(8,128)(2,1)}, bf16[2048,256]{1,0:T(8,128)(2,1)S(1)}, f32[8,2048]{1,0:T(8,128)S(1)}, f32[8,1024]{1,0:T(8,128)S(1)}) custom-call(bf16[2048,2048]{1,0:T(8,128)(2,1)} %bitcast.96, f32[2048,1024]{1,0:T(8,128)} %get-tuple-element.51.slope_ref, bf16[1024,2048]{1,0:T(8,128)(2,1)} %down_w_ref.1, bf16[2048,256]{1,0:T(8,128)(2,1)S(1)} %bitcast.59), custom_call_target="tpu_custom_call" | custom-call | flops 10737418240 | bytes 27262976 | tf_op jit(solution)/shard_map/upstream_parts/pallas_call | solution.py:155
  178.1 13.4 %attend.1 = (bf16[2048,256]{1,0:T(8,128)(2,1)S(1)}, bf16[2048,768]{1,0:T(8,128)(2,1)}, f32[8,768]{1,0:T(8,128)S(1)}) custom-call(bf16[2048,768]{1,0:T(8,128)(2,1)} %get-tuple-element.50.packed_ref, bf16[2048,256]{1,0:T(8,128)(2,1)S(1)} %get-tuple-element.53.grad_ref, f32[2,128,1024]{2,1,0:T(8,128)S(1)} %pad_maximum_fusion.table_ref), custom_call_target="tpu_custom_call" | custom-call | flops 4697620480 | bytes 9437184 | tf_op jit(solution)/shard_map/attend/pallas_call | solution.py:236
  191.5 0.1 dynamic_slice.11
  191.6 0.8 reshape.145.bias_ref
  192.4 7.2 %convolution_convert_fusion.2 = bf16[2048,256]{1,0:T(8,128)(2,1)} fusion(bf16[2048,2048]{1,0:T(8,128)(2,1)} %bitcast.97, bf16[2048,256]{1,0:T(8,128)(2,1)S(1)} %get-tuple-element.55.context_ref), kind=kOutput, calls=%fused_computation.2 | convolution fusion | flops 2148007936 | bytes 10485760 | tf_op jit(solution)/shard_map/dot_general | solution.py:30
  199.6 0.9 broadcast_in_dim.12.p_col_ref
  200.5 1.0 broadcast_in_dim.11.h_col_ref
  201.5 351.4 %finish.1 = (bf16[2,4,2,32,2048]{4,3,2,1,0:T(8,128)(2,1)}, bf16[4,4,2,32,2048]{4,3,2,1,0:T(8,128)(2,1)}, bf16[3,4,2,32,2048]{4,3,2,1,0:T(8,128)(2,1)}, bf16[1,4,...) custom-call(bf16[2,4,2,32,2048]{4,3,2,1,0:T(8,128)(2,1)} %bitcast.69, ...), custom_call_target="tpu_custom_call" | custom-call | tf_op jit(solution)/shard_map/finish/pallas_call | solution.py:866
  552.9 0.7 slice.49
  553.6 0.7 slice_bitcast_fusion
  554.3 0.6 copy.35
  554.9 0.6 reshape.153
  555.5 1.4 fusion.4
  557.0 16.5 %last.1 = (bf16[256,2048]{1,0:T(8,128)(2,1)}, bf16[256,2048]{1,0:T(8,128)(2,1)}, f32[2,512,2048]{2,1,0:T(8,128)}, f32[1024,2048]{1,0:T(8,128)}, f32[768,2048]{1,0:T(8,128)}, /*index=5*/f32[256,2048]{1,0:T(8,128)}) custom-call(bf16[256,2048]{1,0:T(8,128)(2,1)} %bitcast.65, bf16[256,2048]{1,0:T(8,128)(2,1)} %bitcast.67, bf16[256,2048]{1,0:T(8,128)(2,1)} %bitcast.74, ...), custom_call_target="tpu_custom_call" | custom-call | flops 10485760 | bytes 44040192 | tf_op jit(solution)/shard_map/last/pallas_call | solution.py:911
  573.5 0.6 copy.46
  (29 shorter events, 0.3 us)
Async XLA Ops:
  11.2 112.4 %copy-start.2 = (bf16[256,2048]{1,0:T(8,128)(2,1)S(1)}, bf16[256,2048]{1,0:T(8,128)(2,1)}, u32[]{:S(2)}) copy-start(bf16[256,2048]{1,0:T(8,128)(2,1)} %param.23) | copy-start | bytes 3145732
  124.6 35.7 %all-to-all-start = ((bf16[256,8,256]{2,0,1:T(8,128)(2,1)}), bf16[256,8,256]{2,0,1:T(8,128)(2,1)S(1)}, u32[]{:S(2)}, u32[]{:S(2)}) async-start(bf16[256,8,256]{2,0,1:T(8,128)(2,1)} %bitcast.55), calls=%async_computation | async-start | bytes 2097152 | tf_op jit(solution)/shard_map/all_to_all | solution.py:1058
  128.2 428.8 %all-reduce.3.cloned.1.call-start = ((), (), s32[]{:S(2)}) async-start(), calls=%async_computation.1 | async-start | bytes 4194304 | tf_op jit(solution)/shard_map/psum | solution.py:1061
  128.2 10.0 %copy-start.5 = (s32[2,8,128]{2,1,0:T(8,128)S(1)}, s32[2,8,128]{2,1,0:T(8,128)}, u32[]{:S(2)}) copy-start(s32[2,8,128]{2,1,0:T(8,128)} %get-tuple-element.54) | copy-start | bytes 24580
  128.2 21.0 %copy-start.3 = (f32[2048]{0:T(1024)S(1)}, f32[2048]{0:T(1024)}, u32[]{:S(2)}) copy-start(f32[2048]{0:T(1024)} %param.24) | copy-start | bytes 24580
  128.3 21.0 %copy-start.4 = (f32[2048]{0:T(1024)S(1)}, f32[2048]{0:T(1024)}, u32[]{:S(2)}) copy-start(f32[2048]{0:T(1024)} %param.28) | copy-start | bytes 24580
  160.3 17.8 %copy-start = (bf16[256,8,256]{2,0,1:T(8,128)(2,1)}, bf16[256,8,256]{2,0,1:T(8,128)(2,1)S(1)}, u32[]{:S(2)}) copy-start(bf16[256,8,256]{2,0,1:T(8,128)(2,1)S(1)} %all-to-all-done) | copy-start | bytes 3145732
  191.5 8.1 %copy-start.1 = (bf16[2048,256]{1,0:T(8,128)(2,1)}, bf16[2048,256]{1,0:T(8,128)(2,1)S(1)}, u32[]{:S(2)}) copy-start(bf16[2048,256]{1,0:T(8,128)(2,1)S(1)} %get-tuple-element.55.context_ref) | copy-start | bytes 3145732
  557.0 16.5 %copy-start.6 = (f32[1,256]{1,0:T(1,128)}, f32[1,256]{1,0:T(1,128)S(1)}, u32[]{:S(2)}) copy-start(f32[1,256]{1,0:T(1,128)S(1)} %get-tuple-element.76) | copy-start | bytes 3076
Sparse Core Ops, SparseCore 0:
  138.3 106.7 all-reduce.2

commit v10 on v9

--- a/solution.py
+++ b/solution.py
@@ -69,9 +69,11 @@
 
 
 def head_tables(segment_rows):
-    places, starts = document_starts(segment_rows)
-    angles = (places - starts).astype(jnp.float32)[:, None, :] * frequencies()[None, :, None]
-    starts = jnp.broadcast_to(starts.astype(jnp.float32)[:, None, :], (starts.shape[0], ROT, starts.shape[1]))
+    smaller = segment_rows[:, :, None] < segment_rows[:, None, :]
+    starts = jnp.sum(smaller.astype(jnp.float32), axis=1)
+    places = jnp.arange(segment_rows.shape[-1], dtype=jnp.float32)
+    angles = (places - starts)[:, None, :] * frequencies()[None, :, None]
+    starts = jnp.broadcast_to(starts[:, None, :], (starts.shape[0], ROT, starts.shape[1]))
     return jnp.concatenate([jnp.cos(angles), jnp.sin(angles), starts], axis=1)
 
 

time: 591 us -> 591 us (level)
  Pallas kernels: 511 us -> 521 us
  other arithmetic: 12.9 us -> 4.15 us
    pallas_call x1, Pallas kernels: 351 us -> 361 us  [finish(): pl.pallas_call(finish_kernel, out_shape=(*sums, token, token, *others, ja...]
    another operation x2 -> x0, other arithmetic: 9.51 us -> none
  transfers between devices with their start and end apart: 2 -> 2, of which waited for: 0 -> 0; matrix products, arithmetic and copies ran while one was open for 8% -> 6% of each run, Pallas kernels for 66% -> 67%
where the time goes in v10:
time: 591 us; the launch traced here: 581 us
  Pallas kernels  521 us (88%)
  matrix products  26.7 us (5%)
  between operations  14.4 us (2%)
  local copies, waits for them, and re-layouts  11.1 us (2%)
    pallas_call x1, Pallas kernels, finish(): pl.pallas_call(finish_kernel, out_shape=(*sums, token, token, *others, ja...  361 us
    pallas_call x1, Pallas kernels, gather_both(): pl.pallas_call(gather_kernel, out_shape=(shape, shape, jax.ShapeDtypeStru...  112 us
    dot_general x3, matrix products, contract_rows(): lax.dot_general(former, latter, (((0,), (0,)), ((), ())), preferred_eleme...  26.7 us
    pallas_call x1, Pallas kernels, upstream_parts(): pl.pallas_call(upstream_kernel, grid=(tokens // rows,), out_shape=(jax.Sh...  17.8 us
    pallas_call x1, Pallas kernels, last(): pl.pallas_call(last_kernel, grid=(steps,), out_shape=(jax.ShapeDtypeStruc...  16.5 us
    pallas_call x1, Pallas kernels, attend(): pl.pallas_call(attention_kernel, grid=(tokens // length,), out_shape=(jax...  13.2 us
  transfers between devices with their start and end apart: 2, of which 0 were waited for; matrix products, arithmetic and copies ran while one was open for 6% of the time, Pallas kernels for 67%

profile of v10, /device:TPU:0, one launch (start us, length us, event | category | flops | bytes accessed | tf_op | source)
XLA Modules:
  0.0 581.5 jit_solution(14091593691917416734)
XLA Ops:
  7.2 0.8 dynamic_slice.10
  8.0 0.6 reshape.111.b_qkv_in
  8.5 1.3 dynamic_slice.9
  9.8 1.4 pad_maximum_fusion.1.norm_in.norm_ref
  11.2 112.3 %gather_tokens.1 = (bf16[2,4,8,32,2048]{4,3,2,1,0:T(8,128)(2,1)}, bf16[2,4,8,32,2048]{4,3,2,1,0:T(8,128)(2,1)}, s32[2,8,128]{2,1,0:T(8,128)}, bf16[2048,2048]{1,...) custom-call(bf16[256,2048]{1,0:T(8,128)(2,1)} %bitcast.51, ...), custom_call_target="tpu_custom_call" | custom-call | tf_op jit(solution)/shard_map/gather_tokens/pallas_call | solution.py:453
  123.6 1.0 copy.36
  124.6 3.6 all-to-all-start
  128.2 0.4 all-reduce.2.cloned.1.call-start
  128.6 0.0 copy-start.3
  128.6 9.9 %convolution_convert_fusion.1 = bf16[512,2048]{1,0:T(8,128)(2,1)} fusion(bf16[2048,2048]{1,0:T(8,128)(2,1)} %bitcast.79, bf16[2048,1024]{1,0:T(8,128)(2,1)} %get-tuple-element.49.act_ref), kind=kOutput, calls=%fused_computation.2 | convolution fusion | flops 4296015872 | bytes 12582912 | tf_op jit(solution)/shard_map/dot_general | solution.py:30
  138.6 0.0 all-reduce.2.cloned.1.call-update
  138.6 1.0 convert_reduce_fusion
  139.6 1.0 multiply_cosine_fusion
  140.7 0.6 add.17
  141.3 0.1 pad_maximum_fusion.table_ref
  141.4 9.9 %convolution_convert_fusion = bf16[512,2048]{1,0:T(8,128)(2,1)} fusion(bf16[2048,2048]{1,0:T(8,128)(2,1)} %bitcast.80, bf16[2048,1024]{1,0:T(8,128)(2,1)} %get-tuple-element.49.act_ref), kind=kOutput, calls=%fused_computation.1 | convolution fusion | flops 4296015872 | bytes 12582912 | tf_op jit(solution)/shard_map/dot_general | solution.py:30
  151.3 17.8 %upstream_parts.1 = (bf16[2048,1024]{1,0:T(8,128)(2,1)}, bf16[2048,256]{1,0:T(8,128)(2,1)S(1)}, f32[8,2048]{1,0:T(8,128)S(1)}, f32[8,1024]{1,0:T(8,128)S(1)}) custom-call(bf16[2048,2048]{1,0:T(8,128)(2,1)} %bitcast.81, f32[2048,1024]{1,0:T(8,128)} %get-tuple-element.51.slope_ref, bf16[1024,2048]{1,0:T(8,128)(2,1)} %down_w_ref.1, bf16[2048,256]{1,0:T(8,128)(2,1)S(1)} %bitcast.46), custom_call_target="tpu_custom_call" | custom-call | flops 10737418240 | bytes 27262976 | tf_op jit(solution)/shard_map/upstream_parts/pallas_call | solution.py:157
  169.1 13.2 %attend.1 = (bf16[2048,256]{1,0:T(8,128)(2,1)S(1)}, bf16[2048,768]{1,0:T(8,128)(2,1)}, f32[8,768]{1,0:T(8,128)S(1)}) custom-call(bf16[2048,768]{1,0:T(8,128)(2,1)} %get-tuple-element.50.packed_ref, bf16[2048,256]{1,0:T(8,128)(2,1)S(1)} %get-tuple-element.53.grad_ref, f32[2,128,1024]{2,1,0:T(8,128)S(1)} %pad_maximum_fusion.table_ref), custom_call_target="tpu_custom_call" | custom-call | flops 4697620480 | bytes 9437184 | tf_op jit(solution)/shard_map/attend/pallas_call | solution.py:238
  182.3 0.1 dynamic_slice.11
  182.4 0.7 reshape.117.bias_ref
  183.1 6.9 %convolution_convert_fusion.2 = bf16[2048,256]{1,0:T(8,128)(2,1)} fusion(bf16[2048,2048]{1,0:T(8,128)(2,1)} %bitcast.82, bf16[2048,256]{1,0:T(8,128)(2,1)S(1)} %get-tuple-element.55.context_ref), kind=kOutput, calls=%fused_computation.3 | convolution fusion | flops 2148007936 | bytes 10485760 | tf_op jit(solution)/shard_map/dot_general | solution.py:30
  190.1 0.9 broadcast_in_dim.12.p_col_ref
  191.0 1.0 broadcast_in_dim.11.h_col_ref
  192.0 361.3 %finish.1 = (bf16[2,4,2,32,2048]{4,3,2,1,0:T(8,128)(2,1)}, bf16[4,4,2,32,2048]{4,3,2,1,0:T(8,128)(2,1)}, bf16[3,4,2,32,2048]{4,3,2,1,0:T(8,128)(2,1)}, bf16[1,4,...) custom-call(bf16[2,4,2,32,2048]{4,3,2,1,0:T(8,128)(2,1)} %bitcast.56, ...), custom_call_target="tpu_custom_call" | custom-call | tf_op jit(solution)/shard_map/finish/pallas_call | solution.py:868
  553.3 0.7 slice.33
  554.0 0.7 slice_bitcast_fusion
  554.7 0.6 copy.33
  555.3 0.6 reshape.125
  555.9 1.4 fusion.2
  557.3 0.0 all-reduce.2.cloned.1.call-done.early_ref
  557.4 16.5 %last.1 = (bf16[256,2048]{1,0:T(8,128)(2,1)}, bf16[256,2048]{1,0:T(8,128)(2,1)}, f32[2,512,2048]{2,1,0:T(8,128)}, f32[1024,2048]{1,0:T(8,128)}, f32[768,2048]{1,0:T(8,128)}, /*index=5*/f32[256,2048]{1,0:T(8,128)}) custom-call(bf16[256,2048]{1,0:T(8,128)(2,1)} %bitcast.52, bf16[256,2048]{1,0:T(8,128)(2,1)} %bitcast.54, bf16[256,2048]{1,0:T(8,128)(2,1)} %bitcast.61, ...), custom_call_target="tpu_custom_call" | custom-call | flops 10485760 | bytes 44040192 | tf_op jit(solution)/shard_map/last/pallas_call | solution.py:913
  573.8 0.6 copy.40
  (22 shorter events, 0.2 us)
Async XLA Ops:
  11.2 112.3 %copy-start.2 = (bf16[256,2048]{1,0:T(8,128)(2,1)S(1)}, bf16[256,2048]{1,0:T(8,128)(2,1)}, u32[]{:S(2)}) copy-start(bf16[256,2048]{1,0:T(8,128)(2,1)} %param.23) | copy-start | bytes 3145732
  124.6 26.7 %all-to-all-start = ((bf16[256,8,256]{2,0,1:T(8,128)(2,1)}), bf16[256,8,256]{2,0,1:T(8,128)(2,1)S(1)}, u32[]{:S(2)}, u32[]{:S(2)}) async-start(bf16[256,8,256]{2,0,1:T(8,128)(2,1)} %bitcast.44), calls=%async_computation | async-start | bytes 2097152 | tf_op jit(solution)/shard_map/all_to_all | solution.py:1060
  128.2 429.2 %all-reduce.2.cloned.1.call-start = ((), (), s32[]{:S(2)}) async-start(), calls=%async_computation.1 | async-start | bytes 4194304 | tf_op jit(solution)/shard_map/psum | solution.py:1063
  128.6 10.0 %copy-start.5 = (s32[2,8,128]{2,1,0:T(8,128)S(1)}, s32[2,8,128]{2,1,0:T(8,128)}, u32[]{:S(2)}) copy-start(s32[2,8,128]{2,1,0:T(8,128)} %get-tuple-element.54) | copy-start | bytes 24580
  128.6 12.0 %copy-start.3 = (f32[2048]{0:T(1024)S(1)}, f32[2048]{0:T(1024)}, u32[]{:S(2)}) copy-start(f32[2048]{0:T(1024)} %param.24) | copy-start | bytes 24580
  128.6 12.0 %copy-start.4 = (f32[2048]{0:T(1024)S(1)}, f32[2048]{0:T(1024)}, u32[]{:S(2)}) copy-start(f32[2048]{0:T(1024)} %param.28) | copy-start | bytes 24580
  151.3 17.8 %copy-start = (bf16[256,8,256]{2,0,1:T(8,128)(2,1)}, bf16[256,8,256]{2,0,1:T(8,128)(2,1)S(1)}, u32[]{:S(2)}) copy-start(bf16[256,8,256]{2,0,1:T(8,128)(2,1)S(1)} %all-to-all-done) | copy-start | bytes 3145732
  182.3 7.8 %copy-start.1 = (bf16[2048,256]{1,0:T(8,128)(2,1)}, bf16[2048,256]{1,0:T(8,128)(2,1)S(1)}, u32[]{:S(2)}) copy-start(bf16[2048,256]{1,0:T(8,128)(2,1)S(1)} %get-tuple-element.55.context_ref) | copy-start | bytes 3145732
  557.3 16.5 %copy-start.6 = (f32[1,256]{1,0:T(1,128)}, f32[1,256]{1,0:T(1,128)S(1)}, u32[]{:S(2)}) copy-start(f32[1,256]{1,0:T(1,128)S(1)} %get-tuple-element.76) | copy-start | bytes 3076
Sparse Core Ops, SparseCore 0:
  138.7 115.7 all-reduce.1

commit v11 on v10

--- a/solution.py
+++ b/solution.py
@@ -502,7 +502,7 @@
                 start += pairs_of
             at += 1
     count = len(chunks)
-    ahead = 4
+    ahead = 3
 
     def cut(ref, g, k):
         _, _, _, _, start, pairs_of, _ = chunks[k]

time: 591 us -> 591 us (level)
  no operation moved by 1% of the time
where the time goes in v11:
time: 591 us; the launch traced here: 581 us
  Pallas kernels  521 us (88%)
  matrix products  26.7 us (5%)
  between operations  14.4 us (2%)
  local copies, waits for them, and re-layouts  11.1 us (2%)
    pallas_call x1, Pallas kernels, finish(): pl.pallas_call(finish_kernel, out_shape=(*sums, token, token, *others, ja...  361 us
    pallas_call x1, Pallas kernels, gather_both(): pl.pallas_call(gather_kernel, out_shape=(shape, shape, jax.ShapeDtypeStru...  112 us
    dot_general x3, matrix products, contract_rows(): lax.dot_general(former, latter, (((0,), (0,)), ((), ())), preferred_eleme...  26.7 us
    pallas_call x1, Pallas kernels, upstream_parts(): pl.pallas_call(upstream_kernel, grid=(tokens // rows,), out_shape=(jax.Sh...  17.8 us
    pallas_call x1, Pallas kernels, last(): pl.pallas_call(last_kernel, grid=(steps,), out_shape=(jax.ShapeDtypeStruc...  16.5 us
    pallas_call x1, Pallas kernels, attend(): pl.pallas_call(attention_kernel, grid=(tokens // length,), out_shape=(jax...  13.2 us
  transfers between devices with their start and end apart: 2, of which 0 were waited for; matrix products, arithmetic and copies ran while one was open for 6% of the time, Pallas kernels for 67%

profile of v11, /device:TPU:0, one launch (start us, length us, event | category | flops | bytes accessed | tf_op | source)
XLA Modules:
  0.0 581.2 jit_solution(4881130538322317511)
XLA Ops:
  7.2 0.8 dynamic_slice.10
  8.0 0.6 reshape.111.b_qkv_in
  8.5 1.3 dynamic_slice.9
  9.8 1.4 pad_maximum_fusion.1.norm_in.norm_ref
  11.2 112.3 %gather_tokens.1 = (bf16[2,4,8,32,2048]{4,3,2,1,0:T(8,128)(2,1)}, bf16[2,4,8,32,2048]{4,3,2,1,0:T(8,128)(2,1)}, s32[2,8,128]{2,1,0:T(8,128)}, bf16[2048,2048]{1,...) custom-call(bf16[256,2048]{1,0:T(8,128)(2,1)} %bitcast.51, ...), custom_call_target="tpu_custom_call" | custom-call | tf_op jit(solution)/shard_map/gather_tokens/pallas_call | solution.py:453
  123.6 1.0 copy.36
  124.6 3.6 all-to-all-start
  128.2 0.4 all-reduce.2.cloned.1.call-start
  128.6 0.0 copy-start.3
  128.6 9.9 %convolution_convert_fusion.1 = bf16[512,2048]{1,0:T(8,128)(2,1)} fusion(bf16[2048,2048]{1,0:T(8,128)(2,1)} %bitcast.79, bf16[2048,1024]{1,0:T(8,128)(2,1)} %get-tuple-element.49.act_ref), kind=kOutput, calls=%fused_computation.2 | convolution fusion | flops 4296015872 | bytes 12582912 | tf_op jit(solution)/shard_map/dot_general | solution.py:30
  138.6 0.0 all-reduce.2.cloned.1.call-update
  138.6 1.0 convert_reduce_fusion
  139.6 1.0 multiply_cosine_fusion
  140.7 0.6 add.17
  141.3 0.1 pad_maximum_fusion.table_ref
  141.4 9.9 %convolution_convert_fusion = bf16[512,2048]{1,0:T(8,128)(2,1)} fusion(bf16[2048,2048]{1,0:T(8,128)(2,1)} %bitcast.80, bf16[2048,1024]{1,0:T(8,128)(2,1)} %get-tuple-element.49.act_ref), kind=kOutput, calls=%fused_computation.1 | convolution fusion | flops 4296015872 | bytes 12582912 | tf_op jit(solution)/shard_map/dot_general | solution.py:30
  151.3 17.8 %upstream_parts.1 = (bf16[2048,1024]{1,0:T(8,128)(2,1)}, bf16[2048,256]{1,0:T(8,128)(2,1)S(1)}, f32[8,2048]{1,0:T(8,128)S(1)}, f32[8,1024]{1,0:T(8,128)S(1)}) custom-call(bf16[2048,2048]{1,0:T(8,128)(2,1)} %bitcast.81, f32[2048,1024]{1,0:T(8,128)} %get-tuple-element.51.slope_ref, bf16[1024,2048]{1,0:T(8,128)(2,1)} %down_w_ref.1, bf16[2048,256]{1,0:T(8,128)(2,1)S(1)} %bitcast.46), custom_call_target="tpu_custom_call" | custom-call | flops 10737418240 | bytes 27262976 | tf_op jit(solution)/shard_map/upstream_parts/pallas_call | solution.py:157
  169.1 13.2 %attend.1 = (bf16[2048,256]{1,0:T(8,128)(2,1)S(1)}, bf16[2048,768]{1,0:T(8,128)(2,1)}, f32[8,768]{1,0:T(8,128)S(1)}) custom-call(bf16[2048,768]{1,0:T(8,128)(2,1)} %get-tuple-element.50.packed_ref, bf16[2048,256]{1,0:T(8,128)(2,1)S(1)} %get-tuple-element.53.grad_ref, f32[2,128,1024]{2,1,0:T(8,128)S(1)} %pad_maximum_fusion.table_ref), custom_call_target="tpu_custom_call" | custom-call | flops 4697620480 | bytes 9437184 | tf_op jit(solution)/shard_map/attend/pallas_call | solution.py:238
  182.3 0.1 dynamic_slice.11
  182.4 0.7 reshape.117.bias_ref
  183.1 6.9 %convolution_convert_fusion.2 = bf16[2048,256]{1,0:T(8,128)(2,1)} fusion(bf16[2048,2048]{1,0:T(8,128)(2,1)} %bitcast.82, bf16[2048,256]{1,0:T(8,128)(2,1)S(1)} %get-tuple-element.55.context_ref), kind=kOutput, calls=%fused_computation.3 | convolution fusion | flops 2148007936 | bytes 10485760 | tf_op jit(solution)/shard_map/dot_general | solution.py:30
  190.1 0.9 broadcast_in_dim.12.p_col_ref
  191.0 1.0 broadcast_in_dim.11.h_col_ref
  192.0 361.0 %finish.1 = (bf16[2,4,2,32,2048]{4,3,2,1,0:T(8,128)(2,1)}, bf16[4,4,2,32,2048]{4,3,2,1,0:T(8,128)(2,1)}, bf16[3,4,2,32,2048]{4,3,2,1,0:T(8,128)(2,1)}, bf16[1,4,...) custom-call(bf16[2,4,2,32,2048]{4,3,2,1,0:T(8,128)(2,1)} %bitcast.56, ...), custom_call_target="tpu_custom_call" | custom-call | tf_op jit(solution)/shard_map/finish/pallas_call | solution.py:868
  553.0 0.7 slice.33
  553.7 0.7 slice_bitcast_fusion
  554.4 0.6 copy.33
  555.0 0.6 reshape.125
  555.6 1.4 fusion.2
  557.0 0.0 all-reduce.2.cloned.1.call-done.early_ref
  557.0 16.5 %last.1 = (bf16[256,2048]{1,0:T(8,128)(2,1)}, bf16[256,2048]{1,0:T(8,128)(2,1)}, f32[2,512,2048]{2,1,0:T(8,128)}, f32[1024,2048]{1,0:T(8,128)}, f32[768,2048]{1,0:T(8,128)}, /*index=5*/f32[256,2048]{1,0:T(8,128)}) custom-call(bf16[256,2048]{1,0:T(8,128)(2,1)} %bitcast.52, bf16[256,2048]{1,0:T(8,128)(2,1)} %bitcast.54, bf16[256,2048]{1,0:T(8,128)(2,1)} %bitcast.61, ...), custom_call_target="tpu_custom_call" | custom-call | flops 10485760 | bytes 44040192 | tf_op jit(solution)/shard_map/last/pallas_call | solution.py:913
  573.5 0.6 copy.40
  (22 shorter events, 0.2 us)
Async XLA Ops:
  11.2 112.3 %copy-start.2 = (bf16[256,2048]{1,0:T(8,128)(2,1)S(1)}, bf16[256,2048]{1,0:T(8,128)(2,1)}, u32[]{:S(2)}) copy-start(bf16[256,2048]{1,0:T(8,128)(2,1)} %param.23) | copy-start | bytes 3145732
  124.6 26.7 %all-to-all-start = ((bf16[256,8,256]{2,0,1:T(8,128)(2,1)}), bf16[256,8,256]{2,0,1:T(8,128)(2,1)S(1)}, u32[]{:S(2)}, u32[]{:S(2)}) async-start(bf16[256,8,256]{2,0,1:T(8,128)(2,1)} %bitcast.44), calls=%async_computation | async-start | bytes 2097152 | tf_op jit(solution)/shard_map/all_to_all | solution.py:1060
  128.2 428.9 %all-reduce.2.cloned.1.call-start = ((), (), s32[]{:S(2)}) async-start(), calls=%async_computation.1 | async-start | bytes 4194304 | tf_op jit(solution)/shard_map/psum | solution.py:1063
  128.6 10.0 %copy-start.5 = (s32[2,8,128]{2,1,0:T(8,128)S(1)}, s32[2,8,128]{2,1,0:T(8,128)}, u32[]{:S(2)}) copy-start(s32[2,8,128]{2,1,0:T(8,128)} %get-tuple-element.54) | copy-start | bytes 24580
  128.6 12.0 %copy-start.3 = (f32[2048]{0:T(1024)S(1)}, f32[2048]{0:T(1024)}, u32[]{:S(2)}) copy-start(f32[2048]{0:T(1024)} %param.24) | copy-start | bytes 24580
  128.6 12.0 %copy-start.4 = (f32[2048]{0:T(1024)S(1)}, f32[2048]{0:T(1024)}, u32[]{:S(2)}) copy-start(f32[2048]{0:T(1024)} %param.28) | copy-start | bytes 24580
  151.3 17.8 %copy-start = (bf16[256,8,256]{2,0,1:T(8,128)(2,1)}, bf16[256,8,256]{2,0,1:T(8,128)(2,1)S(1)}, u32[]{:S(2)}) copy-start(bf16[256,8,256]{2,0,1:T(8,128)(2,1)S(1)} %all-to-all-done) | copy-start | bytes 3145732
  182.3 7.8 %copy-start.1 = (bf16[2048,256]{1,0:T(8,128)(2,1)}, bf16[2048,256]{1,0:T(8,128)(2,1)S(1)}, u32[]{:S(2)}) copy-start(bf16[2048,256]{1,0:T(8,128)(2,1)S(1)} %get-tuple-element.55.context_ref) | copy-start | bytes 3145732
  557.0 16.5 %copy-start.6 = (f32[1,256]{1,0:T(1,128)}, f32[1,256]{1,0:T(1,128)S(1)}, u32[]{:S(2)}) copy-start(f32[1,256]{1,0:T(1,128)S(1)} %get-tuple-element.76) | copy-start | bytes 3076
Sparse Core Ops, SparseCore 0:
  138.7 115.7 all-reduce.1
